TPU v7x, 256 devices: a whole 4x4x8 slice. The times are simulated.
256 devices in a mesh: facet: 16 (over y, x_lo, core), team: 8 (over z), sub: 2 (over x_hi).
Axes of the slice: x: 4 (x_hi: 2, x_lo: 2; x = x_hi * 2 + x_lo), y: 4, z: 8, core: 2. Of those that a mesh axis runs over, the one named last changes fastest.
Arguments:
- facet_rows: bfloat16 [16, 2, 64, 4096], P('facet', None, 'team'), may hold values from -6 to 6
- sub_offsets: int32 [32, 2], replicated, may hold values from 0 to 4095
- facet_offsets: int32 [16, 2], replicated, may hold values from 0 to 4095
- aterm: bfloat16 [16, 2, 256, 256], P('facet'), may hold values from 0.29882812 to 3
- cells: int32 [16, 2, 8, 2, 256], P('facet', None, 'team'), may hold values from 0 to 1023
- observed: bfloat16 [16, 2, 8, 2, 256], P('facet', None, 'team'), may hold values from -6 to 6
- weights: bfloat16 [16, 2, 8, 256], P('facet', None, 'team'), may hold values from 0.29882812 to 3
- counts: int32 [16, 2, 8], replicated, may hold values from 1 to 256, as said below
Outputs:
- facet_update: float32 [16, 2, 64, 4096], P('facet', None, 'team', 'sub')
Inputs may be any that keep to these rules, and one draw needn't show every extreme that they name: Slots 0 to counts[a, b, t] - 1 are live. For every a and t one of the two subgrids with indices [a, 0] and [a, 1] has at most 64 live slots, and which of the two it is does not change with t.
All inputs are finite; a program needn't handle non-finite values.
Results may differ from a plain program's by a relative error of at most 0.019.
Values may be sent and summed in bfloat16 or wider, within the bound.
No kernel may reach another device: no remote copies, remote signals or barrier semaphores. Data moves between devices by JAX's collectives and lax.ppermute only.
A program may use at most 64 MiB of HBM per device.

v0:
```python
import math

import jax
import jax.numpy as jnp
from jax import lax
from jax.sharding import PartitionSpec as P

L = 4096
M = 128
SG = 256
VB = 256


TWO_PI = 2.0 * math.pi
HIGHEST = lax.Precision.HIGHEST


def cut_along(shard, dim, peers):
    before, after = (shard.shape[:dim], shard.shape[dim + 1 :])
    return jnp.moveaxis(shard.reshape(*before, peers, -1, *after), dim, 0)


def sum_at_owner(shard, axis, dim):
    peers = lax.axis_size(axis)
    parts = lax.all_to_all(cut_along(shard, dim, peers), axis, 0, 0, tiled=True)
    return jnp.sum(parts, axis=0)


def in_order(parts, dim):
    parts = jnp.moveaxis(parts, 0, dim)
    lengths = parts.shape
    return parts.reshape(*lengths[:dim], lengths[dim] * lengths[dim + 1], *lengths[dim + 2 :])


def from_everyone(shard, axis):
    copies = jnp.broadcast_to(shard, (lax.axis_size(axis), *shard.shape))
    return lax.all_to_all(copies, axis, split_axis=0, concat_axis=0, tiled=True)


def collect(shard, axis, dim):
    return in_order(from_everyone(shard, axis), dim)


def over_copies(shard, axis):
    return from_everyone(shard, axis).astype(jnp.float32).sum(axis=0)


def partner(value, axis, stride):
    mask = 2**stride
    pairs = [(source, source ^ mask) for source in range(lax.axis_size(axis))]
    return lax.ppermute(value, axis, pairs)


def angles(left_ints, right_ints, period):
    return (left_ints * right_ints % period).astype(jnp.float32) * (TWO_PI / period)


def transform_tables():
    columns = jnp.arange(L, dtype=jnp.int32)
    frequency = jnp.arange(M, dtype=jnp.int32)
    angle_grid = angles(columns[:, None], frequency[None, :], L)
    cos_part = jnp.cos(angle_grid)
    sin_part = jnp.sin(angle_grid)
    spec_re = (cos_part / math.sqrt(L)).astype(jnp.bfloat16)
    spec_im = (-sin_part / math.sqrt(L)).astype(jnp.bfloat16)
    forward = jnp.concatenate(
        [jnp.concatenate([spec_re, spec_im], 1), jnp.concatenate([-spec_im, spec_re], 1)], 0
    )
    back_re = (cos_part.T / math.sqrt(M)).astype(jnp.bfloat16)
    back_im = (sin_part.T / math.sqrt(M)).astype(jnp.bfloat16)
    backward = jnp.concatenate(
        [jnp.concatenate([back_re, back_im], 1), jnp.concatenate([-back_im, back_re], 1)], 0
    )
    return (forward, backward)


def subgrid_table(size_sub):
    freq_ids = jnp.arange(M, dtype=jnp.int32)
    cell_ids = jnp.arange(size_sub, dtype=jnp.int32)
    angle_grid = angles(freq_ids[:, None], cell_ids[None, :], size_sub)
    factor = 1.0 / math.sqrt(M)
    return (jnp.cos(angle_grid) * factor, jnp.sin(angle_grid) * factor)


def facet_phase(row_ids, facet_offsets):
    col_ids = jnp.arange(M, dtype=jnp.int32)
    along_rows = row_ids[:, None] * facet_offsets[None, :, 0] % L
    along_cols = col_ids[None, :] * facet_offsets[:, 1:2] % L
    angle_grid = ((along_rows[:, :, None] + along_cols[None, :, :]) % L).astype(jnp.float32) * (
        TWO_PI / L
    )
    return (jnp.cos(angle_grid), jnp.sin(angle_grid))


def hdot(left, right):
    return jnp.dot(left, right, precision=HIGHEST, preferred_element_type=jnp.float32)


def hsum(form, left, right):
    return jnp.einsum(form, left, right, precision=HIGHEST, preferred_element_type=jnp.float32)


def to_image(assembled, k_re, k_im):
    grid_re = assembled[:, 0]
    grid_im = assembled[:, 1]
    temp_re = hdot(k_re.T, grid_re) - hdot(k_im.T, grid_im)
    temp_im = hdot(k_re.T, grid_im) + hdot(k_im.T, grid_re)
    image_re = hdot(temp_re, k_re) - hdot(temp_im, k_im)
    image_im = hdot(temp_re, k_im) + hdot(temp_im, k_re)
    return (image_re, image_im)


def to_return(grid, weight_map, k_re, k_im):
    size_sub = weight_map.shape[0]
    grid_re = grid[:, :size_sub] * weight_map / size_sub
    grid_im = grid[:, size_sub:] * weight_map / size_sub
    temp_re = hdot(k_re, grid_re) + hdot(k_im, grid_im)
    temp_im = hdot(k_re, grid_im) - hdot(k_im, grid_re)
    out_re = hdot(temp_re, k_re.T) + hdot(temp_im, k_im.T)
    out_im = hdot(temp_im, k_re.T) - hdot(temp_re, k_im.T)
    return jnp.stack([out_re, out_im], 1)


def degrid_block(weighted, cell_pair, observed_pair, weight, live):
    size_sub = weighted.shape[1]
    block_len = cell_pair.shape[1]
    index = jnp.arange(size_sub, dtype=jnp.int32)
    row_angle = angles(cell_pair[0][:, None], index[None, :], 4 * size_sub)
    col_angle = angles(cell_pair[1][:, None], index[None, :], 4 * size_sub)
    row_cos = jnp.cos(row_angle).astype(jnp.bfloat16)
    row_sin = jnp.sin(row_angle).astype(jnp.bfloat16)
    col_cos = jnp.cos(col_angle).astype(jnp.bfloat16)
    col_sin = jnp.sin(col_angle).astype(jnp.bfloat16)
    col_stack = jnp.concatenate([col_cos, col_sin], 0)
    products = jnp.einsum("jk,ik->ji", col_stack, weighted, preferred_element_type=jnp.float32)
    part_re = products[:block_len, :size_sub] + products[block_len:, size_sub:]
    part_im = products[:block_len, size_sub:] - products[block_len:, :size_sub]
    cos_rows = row_cos.astype(jnp.float32)
    sin_rows = row_sin.astype(jnp.float32)
    cos_cols = col_cos.astype(jnp.float32)
    sin_cols = col_sin.astype(jnp.float32)
    pred_re = jnp.sum(cos_rows * part_re + sin_rows * part_im, 1) / size_sub
    pred_im = jnp.sum(cos_rows * part_im - sin_rows * part_re, 1) / size_sub
    res_re = live * weight * (observed_pair[0] - pred_re)
    res_im = live * weight * (observed_pair[1] - pred_im)
    spread_re = (res_re[:, None] * cos_cols - res_im[:, None] * sin_cols).astype(jnp.bfloat16)
    spread_im = (res_re[:, None] * sin_cols + res_im[:, None] * cos_cols).astype(jnp.bfloat16)
    right = jnp.concatenate(
        [jnp.concatenate([spread_re, spread_im], 1), jnp.concatenate([-spread_im, spread_re], 1)], 0
    )
    left = jnp.concatenate([row_cos, row_sin], 0)
    return jnp.einsum("ji,jk->ik", left, right, preferred_element_type=jnp.float32)


def weigh_image(assembled, weight_map, k_re, k_im):
    image_re, image_im = to_image(assembled, k_re, k_im)
    return jnp.concatenate(
        [
            (weight_map * image_re).astype(jnp.bfloat16),
            (weight_map * image_im).astype(jnp.bfloat16),
        ],
        0,
    )


def local(facet_rows, sub_offsets, facet_offsets, aterm, cells, observed, weights, counts):
    n_facet = lax.axis_size("facet")
    n_team = lax.axis_size("team")
    n_sub = lax.axis_size("sub")
    my_facet = lax.axis_index("facet")
    my_team = lax.axis_index("team")
    my_side = lax.axis_index("sub")
    rows_dev = facet_rows.shape[2]
    rows_all = rows_dev * n_team
    norm = 1.0 / math.sqrt(n_facet)
    share = M // n_team
    forward, backward = transform_tables()
    k_re, k_im = subgrid_table(SG)
    sub_ids = jnp.arange(n_facet, dtype=jnp.int32) * n_sub + my_side
    shifts = sub_offsets[sub_ids, 0]
    tunings = sub_offsets[sub_ids, 1]
    columns = jnp.arange(L, dtype=jnp.int32)
    mod_angle = angles(tunings[:, None], columns[None, :], L)
    mod_cos = jnp.cos(mod_angle)[:, None, :]
    mod_sin = jnp.sin(mod_angle)[:, None, :]
    rows_re = facet_rows[0, 0].astype(jnp.float32)[None]
    rows_im = facet_rows[0, 1].astype(jnp.float32)[None]
    mod_re = (rows_re * mod_cos + rows_im * mod_sin).astype(jnp.bfloat16)
    mod_im = (rows_im * mod_cos - rows_re * mod_sin).astype(jnp.bfloat16)
    stacked = jnp.concatenate([mod_re, mod_im], 2).reshape(n_facet * rows_dev, 2 * L)
    spectrum = jnp.dot(stacked, forward, preferred_element_type=jnp.float32).reshape(
        n_facet, rows_dev, 2, M
    )
    row_ids = my_team * rows_dev + jnp.arange(rows_dev, dtype=jnp.int32)
    out_ids = jnp.arange(M, dtype=jnp.int32)
    w_angle = angles(
        out_ids[None, :, None] + shifts[:, None, None], row_ids[None, None, :], rows_all
    )
    w_re = jnp.cos(w_angle) / math.sqrt(rows_all)
    w_im = -jnp.sin(w_angle) / math.sqrt(rows_all)
    part_re = w_re
    part_im = w_im
    real_out = hsum("fpr,frm->pfm", part_re, spectrum[:, :, 0]) - hsum(
        "fpr,frm->pfm", part_im, spectrum[:, :, 1]
    )
    imag_out = hsum("fpr,frm->pfm", part_re, spectrum[:, :, 1]) + hsum(
        "fpr,frm->pfm", part_im, spectrum[:, :, 0]
    )
    mine = sum_at_owner(jnp.stack([real_out, imag_out], 2), "team", 0)
    received = lax.all_to_all(mine, "facet", split_axis=1, concat_axis=1, tiled=True)
    block_rows = received.shape[0]
    phase_cos, phase_sin = facet_phase(
        my_team * share + jnp.arange(block_rows, dtype=jnp.int32), facet_offsets
    )
    grid_re = jnp.sum(phase_cos * received[:, :, 0] - phase_sin * received[:, :, 1], 1) * norm
    grid_im = jnp.sum(phase_cos * received[:, :, 1] + phase_sin * received[:, :, 0], 1) * norm
    assembled = collect(jnp.stack([grid_re, grid_im], 1), "team", 0)
    maps = aterm[0].astype(jnp.float32)
    own_map = lax.dynamic_index_in_dim(maps, my_side, 0, keepdims=False)
    weighted = weigh_image(assembled, own_map, k_re, k_im)
    own_cells = cells[0, :, 0]
    own_obs = observed[0, :, 0]
    own_weights = weights[0, :, 0]
    zero_int = jnp.zeros((), jnp.int32)
    lane_ids = jnp.arange(VB, dtype=jnp.int32)
    empty_grid = jnp.zeros((SG, 2 * SG), jnp.float32)

    def block_term(side, block, image_stack):
        start = block * VB
        cell_pair = lax.dynamic_slice(own_cells, (side, zero_int, start), (1, 2, VB))[0]
        obs_pair = lax.dynamic_slice(own_obs, (side, zero_int, start), (1, 2, VB))[0].astype(
            jnp.float32
        )
        weight = lax.dynamic_slice(own_weights, (side, start), (1, VB))[0].astype(jnp.float32)
        live = (start + lane_ids < counts[my_facet, side, my_team]).astype(jnp.float32)
        return degrid_block(image_stack, cell_pair, obs_pair, weight, live)

    own_blocks = (counts[my_facet, my_side, my_team] + VB - 1) // VB

    def own_step(block, total):
        return total + block_term(my_side, block, weighted)

    grid = lax.fori_loop(0, own_blocks, own_step, empty_grid)
    returned = to_return(grid, own_map, k_re, k_im)
    total_back = over_copies(returned.astype(jnp.bfloat16), "team").astype(jnp.float32)
    block_rows = total_back.shape[0]
    phase_cos, phase_sin = facet_phase(jnp.arange(block_rows, dtype=jnp.int32), facet_offsets)
    back_re = (phase_cos * total_back[:, None, 0] + phase_sin * total_back[:, None, 1]) * norm
    back_im = (phase_cos * total_back[:, None, 1] - phase_sin * total_back[:, None, 0]) * norm
    arrived = lax.all_to_all(
        jnp.stack([back_re, back_im], 2).astype(jnp.bfloat16),
        "facet",
        split_axis=1,
        concat_axis=1,
        tiled=True,
    ).astype(jnp.float32)
    part_re = w_re
    part_im = w_im
    fold_re = hsum("fpr,pfm->frm", part_re, arrived[:, :, 0]) + hsum(
        "fpr,pfm->frm", part_im, arrived[:, :, 1]
    )
    fold_im = hsum("fpr,pfm->frm", part_re, arrived[:, :, 1]) - hsum(
        "fpr,pfm->frm", part_im, arrived[:, :, 0]
    )
    folded = jnp.stack([fold_re, fold_im], 2)
    folded_stack = folded.astype(jnp.bfloat16).reshape(n_facet * rows_dev, 2 * M)
    half = L // n_sub
    col_start = my_side * half
    other_stack = partner(folded_stack, "sub", 0)
    both_stacks = jnp.concatenate([folded_stack, other_stack], 0)
    back_half = jnp.concatenate(
        [
            lax.dynamic_slice_in_dim(backward, col_start, half, 1),
            lax.dynamic_slice_in_dim(backward, L + col_start, half, 1),
        ],
        1,
    )
    spectra_half = jnp.dot(both_stacks, back_half, preferred_element_type=jnp.float32).reshape(
        2 * n_facet, rows_dev, 2, half
    )
    other_ids = jnp.arange(n_facet, dtype=jnp.int32) * n_sub + (1 - my_side)
    all_tunings = jnp.concatenate([tunings, sub_offsets[other_ids, 1]], 0)
    half_cols = col_start + jnp.arange(half, dtype=jnp.int32)
    half_angle = angles(all_tunings[:, None], half_cols[None, :], L)
    half_cos = jnp.cos(half_angle)[:, None, :]
    half_sin = jnp.sin(half_angle)[:, None, :]
    update_re = jnp.sum(spectra_half[:, :, 0] * half_cos - spectra_half[:, :, 1] * half_sin, 0)
    update_im = jnp.sum(spectra_half[:, :, 1] * half_cos + spectra_half[:, :, 0] * half_sin, 0)
    return jnp.stack([update_re, update_im], 0)[None]


def solution(mesh):
    placed = (
        P("facet", None, "team", None),
        P(),
        P(),
        P("facet", None, None, None),
        P("facet", None, "team", None, None),
        P("facet", None, "team", None, None),
        P("facet", None, "team", None),
        P(),
    )
    return jax.shard_map(
        local,
        mesh=mesh,
        in_specs=placed,
        out_specs=P("facet", None, "team", "sub"),
        check_vma=False,
    )
```

profile of v0, /device:TPU:1, one launch (start us, length us, event | category | flops | bytes accessed | tf_op | source)
XLA Modules:
  0.0 229.4 jit_solution(1294391637697271506)
XLA Ops:
  0.0 8.5 %multiply_convert_fusion.2 = (bf16[4096,128]{0,1:T(8,128)(2,1)S(1)}, bf16[4096,128]{0,1:T(8,128)(2,1)S(1)}) fusion(), kind=kLoop, calls=%fused_computation.82 | loop fusion | flops 9961472 | bytes 2097152 | tf_op jit(solution)/shard_map/convert_element_type | solution.py:65
  8.5 7.9 %fusion.68 = bf16[4096,128]{0,1:T(8,128)(2,1)S(1)} fusion(), kind=kLoop, calls=%fused_computation.135 | loop fusion | flops 10485760 | bytes 1048576 | tf_op jit(solution)/shard_map/neg | solution.py:67
  17.7 1.9 fusion.126
  19.5 1.5 bitcast_convert_fusion.1
  21.1 1.2 gather_fusion
  23.0 18.0 %maximum_maximum_fusion = bf16[8192,256]{0,1:T(8,128)(2,1)S(1)} fusion(bf16[4096,128]{0,1:T(8,128)(2,1)S(1)} %get-tuple-element.313, bf16[4096,128]{0,1:T(8,128)(2,1)S(1)} %fusion.68, bf16[4096,128]{0,1:T(8,128)(2,1)S(1)} %get-tuple-element.312), kind=kLoop, calls=%fused_computation.51 | loop fusion | flops 16777216 | bytes 7340032 | tf_op jit(solution)/shard_map/concatenate | solution.py:66
  41.6 1.5 fusion.36
  43.1 1.9 fusion.141
  45.0 1.9 fusion.142
  46.9 1.9 convolution_subtract_fusion
  48.9 1.9 convolution_add_fusion.1
  51.0 1.5 copy.42
  52.6 9.1 %all-to-all-start = ((f32[8,16,16,2,128]{4,1,2,3,0:T(8,128)}), f32[8,16,16,2,128]{4,1,2,3,0:T(8,128)S(1)}, u32[]{:S(2)}, u32[]{:S(2)}) async-start(f32[8,16,16,2,128]{4,1,2,3,0:T(8,128)} %copy.42), calls=%async_computation | async-start | bytes 4194304 | tf_op jit(solution)/shard_map/all_to_all | solution.py:25
  62.7 7.9 %fusion.69 = bf16[128,4096]{1,0:T(8,128)(2,1)S(1)} fusion(), kind=kLoop, calls=%fused_computation.136 | loop fusion | flops 9961472 | bytes 1048576 | tf_op jit(solution)/shard_map/neg | solution.py:72
  70.6 39.6 %all-to-all-done = f32[8,16,16,2,128]{4,1,2,3,0:T(8,128)S(1)} async-done(((f32[8,16,16,2,128]{4,1,2,3,0:T(8,128)}), f32[8,16,16,2,128]{4,1,2,3,0:T(8,128)S(1)}, u32[]{:S(2)}, u32[]{:S(2)}) %all-to-all-start) | async-done | bytes 2097184 | tf_op jit(solution)/shard_map/all_to_all | solution.py:25
  111.0 9.4 %all-to-all-start.1 = ((f32[16,16,2,128]{3,0,2,1:T(8,128)}), f32[16,16,2,128]{3,0,2,1:T(8,128)S(1)}, u32[]{:S(2)}, u32[]{:S(2)}) async-start(f32[16,16,2,128]{3,0,2,1:T(8,128)} %copy.34), calls=%async_computation.1 | async-start | bytes 524288 | tf_op jit(solution)/shard_map/all_to_all | solution.py:210
  120.6 1.3 dynamic_slice.40
  122.6 5.0 %all-to-all-done.1 = f32[16,16,2,128]{3,0,2,1:T(8,128)S(1)} async-done(((f32[16,16,2,128]{3,0,2,1:T(8,128)}), f32[16,16,2,128]{3,0,2,1:T(8,128)S(1)}, u32[]{:S(2)}, u32[]{:S(2)}) %all-to-all-start.1) | async-done | bytes 262176 | tf_op jit(solution)/shard_map/all_to_all | solution.py:210
  128.9 3.5 %all-to-all-start.2 = ((f32[8,16,2,128]{3,2,1,0:T(2,128)}), f32[8,16,2,128]{3,2,1,0:T(2,128)S(1)}, u32[]{:S(2)}, u32[]{:S(2)}) async-start(f32[8,16,2,128]{3,2,1,0:T(2,128)} %broadcast_in_dim.9), calls=%async_computation.2 | async-start | bytes 262144 | tf_op jit(solution)/shard_map/all_to_all | solution.py:37
  132.4 1.1 cosine_convert_fusion.2
  133.5 6.5 %all-to-all-done.2 = f32[8,16,2,128]{3,2,1,0:T(2,128)S(1)} async-done(((f32[8,16,2,128]{3,2,1,0:T(2,128)}), f32[8,16,2,128]{3,2,1,0:T(2,128)S(1)}, u32[]{:S(2)}, u32[]{:S(2)}) %all-to-all-start.2) | async-done | bytes 131104 | tf_op jit(solution)/shard_map/all_to_all | solution.py:37
  142.8 0.9 fusion.138
  143.6 0.9 fusion.140
  144.5 0.8 convolution_add_fusion.4
  145.4 0.9 fusion.51
  146.3 0.9 fusion.52
  147.4 1.2 fusion.73
  148.7 5.3 %while.15 = (s32[]{:T(128)}, f32[256,512]{1,0:T(8,128)S(1)}, s32[]{:T(128)}, s32[1,2,256]{2,1,0:T(2,128)S(1)}, s32[1,1,1]{2,1,0:T(1,128)}, /*index=5*/bf16[1,256...) while((s32[]{:T(128)}, f32[256,512]{1,0:T(8,128)S(1)}, ...), condition=%wide.region_6.7_spmd.clone, body=%wide.region_5.6_spmd.clone.sunk | while | flops 141363712 | bytes 2383489 | solution.py:243
  149.4 1.3 fusion.327
  150.7 1.3 fusion.328
  152.0 1.3 cosine_convert_fusion.5
  160.4 0.9 broadcast_in_dim.10
  161.3 4.1 %all-to-all-start.3 = ((bf16[8,128,2,128]{3,1,2,0:T(8,128)(2,1)}), bf16[8,128,2,128]{3,1,2,0:T(8,128)(2,1)}, u32[]{:S(2)}, u32[]{:S(2)}) async-start(bf16[8,128,2,128]{3,1,2,0:T(8,128)(2,1)} %broadcast_in_dim.10), calls=%async_computation.3 | async-start | bytes 1048576 | tf_op jit(solution)/shard_map/all_to_all | solution.py:37
  165.5 1.9 fusion.120
  167.3 8.5 %multiply_convert_fusion = (bf16[128,4096]{1,0:T(8,128)(2,1)S(1)}, bf16[128,4096]{1,0:T(8,128)(2,1)S(1)}) fusion(), kind=kLoop, calls=%fused_computation.78 | loop fusion | flops 9437184 | bytes 2097152 | tf_op jit(solution)/shard_map/convert_element_type | solution.py:70
  175.9 4.8 %all-to-all-done.3 = bf16[8,128,2,128]{3,1,2,0:T(8,128)(2,1)} async-done(((bf16[8,128,2,128]{3,1,2,0:T(8,128)(2,1)}), bf16[8,128,2,128]{3,1,2,0:T(8,128)(2,1)}, u32[]{:S(2)}, u32[]{:S(2)}) %all-to-all-start.3) | async-done | bytes 524320 | tf_op jit(solution)/shard_map/all_to_all | solution.py:37
  180.6 1.1 convert_reduce_fusion
  181.8 4.8 %multiply_convert_fusion.5 = (bf16[128,16,1,128]{3,0,2,1:T(8,128)(2,1)S(1)}, bf16[128,16,1,128]{3,0,2,1:T(8,128)(2,1)S(1)}) fusion(f32[128,128]{1,0:T(8,128)S(1)} %get-tuple-element.295, f32[128,128]{1,0:T(8,128)S(1)} %get-tuple-element.294, s32[16,128]{1,0:T(8,128)S(1)} %add_select_fusion.15, s32[128,16]{0,1:T(8,128)S(1)} %add_select_fusion.16), kind=kLoop, calls=%fused_computation.124 | loop fusion | flops 6291456 | bytes 1196032 | tf_op jit(solution)/shard_map/convert.7
  186.6 1.1 pad_maximum_fusion.1
  187.7 8.2 %all-to-all-start.4 = ((bf16[128,16,2,128]{3,0,2,1:T(8,128)(2,1)}), bf16[128,16,2,128]{3,0,2,1:T(8,128)(2,1)}, u32[]{:S(2)}, u32[]{:S(2)}) async-start(bf16[128,16,2,128]{3,0,2,1:T(8,128)(2,1)} %pad_maximum_fusion.1), calls=%async_computation.4 | async-start | bytes 2097152 | tf_op jit(solution)/shard_map/all_to_all | solution.py:250
  195.9 18.6 %maximum_maximum_fusion.1 = bf16[256,8192]{1,0:T(8,128)(2,1)} fusion(bf16[128,4096]{1,0:T(8,128)(2,1)S(1)} %get-tuple-element.315, bf16[128,4096]{1,0:T(8,128)(2,1)S(1)} %fusion.69, bf16[128,4096]{1,0:T(8,128)(2,1)S(1)} %get-tuple-element.314), kind=kLoop, calls=%fused_computation.52 | loop fusion | flops 16777216 | bytes 7340032 | tf_op jit(solution)/shard_map/concatenate | solution.py:71
  214.5 1.8 fusion.66
  216.2 1.8 fusion.67
  218.0 1.8 fusion.60
  219.8 1.8 fusion.59
  221.6 2.5 %collective-permute-start = (bf16[128,256]{1,0:T(8,128)(2,1)S(1)}, bf16[128,256]{1,0:T(8,128)(2,1)S(1)}, u32[]{:S(2)}, u32[]{:S(2)}) collective-permute-start(bf16[128,256]{1,0:T(8,128)(2,1)S(1)} %copy_bitcast_fusion), channel_id=1, source_target_pairs={{0,1},{1,0},{2,3},{3,2},{4,5},{5,4},{6,7},{7,6},{8,9},{9,8},{10,11... | collective-permute-start | bytes 196616 | tf_op jit(solution)/shard_map/ppermute | solution.py:51
  224.1 1.7 constant_dynamic-slice_fusion.1
  225.8 1.1 collective-permute-done
  (79 shorter events, 18.6 us)
Async XLA Ops:
  0.0 62.5 %copy-start = (s32[1,2,1,2,256]{4,3,2,1,0:T(2,128)S(1)}, s32[1,2,1,2,256]{4,3,2,1,0:T(2,128)}, u32[]{:S(2)}) copy-start(s32[1,2,1,2,256]{4,3,2,1,0:T(2,128)} %param.14) | copy-start | bytes 12292
  0.0 16.4 %copy-start.1 = (s32[32,2]{0,1:T(2,128)S(1)}, s32[32,2]{0,1:T(2,128)}, u32[]{:S(2)}) copy-start(s32[32,2]{0,1:T(2,128)} %param.11) | copy-start | bytes 772
  17.1 0.6 copy-start.7
  23.0 25.9 %copy-start.5 = (s32[8]{0:T(128)}, s32[8]{0:T(128)S(1)}, u32[]{:S(2)}) copy-start(s32[8]{0:T(128)S(1)} %iota_add_fusion.4) | copy-start | bytes 100
  23.0 18.1 %copy-start.3 = (f32[16,4096]{1,0:T(8,128)S(1)}, f32[16,4096]{1,0:T(8,128)}, u32[]{:S(2)}) copy-start(f32[16,4096]{1,0:T(8,128)} %get-tuple-element.309) | copy-start | bytes 786436
  23.0 18.1 %copy-start.4 = (f32[8,4096]{1,0:T(8,128)S(1)}, f32[8,4096]{1,0:T(8,128)}, u32[]{:S(2)}) copy-start(f32[8,4096]{1,0:T(8,128)} %get-tuple-element.299) | copy-start | bytes 393220
  52.6 9.8 %copy-start.9 = (bf16[1,2,1,256]{3,1,2,0:T(2,128)(2,1)S(1)}, bf16[1,2,1,256]{3,1,2,0:T(2,128)(2,1)}, u32[]{:S(2)}) copy-start(bf16[1,2,1,256]{3,1,2,0:T(2,128)(2,1)} %param.16) | copy-start | bytes 3076
  52.6 9.9 %copy-start.11 = (bf16[1,2,1,2,256]{4,3,2,1,0:T(2,128)(2,1)S(1)}, bf16[1,2,1,2,256]{4,3,2,1,0:T(2,128)(2,1)}, u32[]{:S(2)}) copy-start(bf16[1,2,1,2,256]{4,3,2,1,0:T(2,128)(2,1)} %param.15) | copy-start | bytes 6148
  52.6 9.9 %copy-start.10 = (s32[16,2]{0,1:T(2,128)S(1)}, s32[16,2]{0,1:T(2,128)}, u32[]{:S(2)}) copy-start(s32[16,2]{0,1:T(2,128)} %param.12) | copy-start | bytes 388
  52.6 57.6 %all-to-all-start = ((f32[8,16,16,2,128]{4,1,2,3,0:T(8,128)}), f32[8,16,16,2,128]{4,1,2,3,0:T(8,128)S(1)}, u32[]{:S(2)}, u32[]{:S(2)}) async-start(f32[8,16,16,2,128]{4,1,2,3,0:T(8,128)} %copy.42), calls=%async_computation | async-start | bytes 4194304 | tf_op jit(solution)/shard_map/all_to_all | solution.py:25
  62.7 57.8 %copy-start.8 = (s32[16]{0:T(128)S(1)}, s32[16]{0:T(128)}, u32[]{:S(2)}) copy-start(s32[16]{0:T(128)} %copy-done.7) | copy-start | bytes 196
  111.0 16.5 %all-to-all-start.1 = ((f32[16,16,2,128]{3,0,2,1:T(8,128)}), f32[16,16,2,128]{3,0,2,1:T(8,128)S(1)}, u32[]{:S(2)}, u32[]{:S(2)}) async-start(f32[16,16,2,128]{3,0,2,1:T(8,128)} %copy.34), calls=%async_computation.1 | async-start | bytes 524288 | tf_op jit(solution)/shard_map/all_to_all | solution.py:210
  128.9 16.5 %copy-start.12 = (bf16[1,2,256,256]{3,2,1,0:T(8,128)(2,1)S(1)}, bf16[1,2,256,256]{3,2,1,0:T(8,128)(2,1)}, u32[]{:S(2)}) copy-start(bf16[1,2,256,256]{3,2,1,0:T(8,128)(2,1)} %param.13) | copy-start | bytes 786436
  128.9 11.2 %all-to-all-start.2 = ((f32[8,16,2,128]{3,2,1,0:T(2,128)}), f32[8,16,2,128]{3,2,1,0:T(2,128)S(1)}, u32[]{:S(2)}, u32[]{:S(2)}) async-start(f32[8,16,2,128]{3,2,1,0:T(2,128)} %broadcast_in_dim.9), calls=%async_computation.2 | async-start | bytes 262144 | tf_op jit(solution)/shard_map/all_to_all | solution.py:37
  161.3 19.3 %all-to-all-start.3 = ((bf16[8,128,2,128]{3,1,2,0:T(8,128)(2,1)}), bf16[8,128,2,128]{3,1,2,0:T(8,128)(2,1)}, u32[]{:S(2)}, u32[]{:S(2)}) async-start(bf16[8,128,2,128]{3,1,2,0:T(8,128)(2,1)} %broadcast_in_dim.10), calls=%async_computation.3 | async-start | bytes 1048576 | tf_op jit(solution)/shard_map/all_to_all | solution.py:37
  187.7 26.8 %all-to-all-start.4 = ((bf16[128,16,2,128]{3,0,2,1:T(8,128)(2,1)}), bf16[128,16,2,128]{3,0,2,1:T(8,128)(2,1)}, u32[]{:S(2)}, u32[]{:S(2)}) async-start(bf16[128,16,2,128]{3,0,2,1:T(8,128)(2,1)} %pad_maximum_fusion.1), calls=%async_computation.4 | async-start | bytes 2097152 | tf_op jit(solution)/shard_map/all_to_all | solution.py:250
  195.9 18.6 %copy-start.6 = (s32[8]{0:T(128)S(1)}, s32[8]{0:T(128)}, u32[]{:S(2)}) copy-start(s32[8]{0:T(128)} %copy-done.5) | copy-start | bytes 100
  221.6 5.3 %collective-permute-start = (bf16[128,256]{1,0:T(8,128)(2,1)S(1)}, bf16[128,256]{1,0:T(8,128)(2,1)S(1)}, u32[]{:S(2)}, u32[]{:S(2)}) collective-permute-start(bf16[128,256]{1,0:T(8,128)(2,1)S(1)} %copy_bitcast_fusion), channel_id=1, source_target_pairs={{0,1},{1,0},{2,3},{3,2},{4,5},{5,4},{6,7},{7,6},{8,9},{9,8},{10,11... | collective-permute-start | bytes 196616 | tf_op jit(solution)/shard_map/ppermute | solution.py:51
  226.9 1.0 copy-start.2
where the time goes:
time: 233 us; the launch traced here: 229 us
  other arithmetic  92.3 us (40%)
  waiting for transfers between devices  57 us (24%)
  starting transfers between devices  37 us (16%)
  matrix products  30.9 us (13%)
  local copies, waits for them, and re-layouts  10.5 us (5%)
    all_to_all x1, waiting for transfers between devices, sum_at_owner(): parts = lax.all_to_all(cut_along(shard, dim, peers), axis, 0, 0, tiled=True)  39.6 us
    concatenate x1, other arithmetic, transform_tables(): jnp.concatenate([jnp.concatenate([back_re, back_im], 1), jnp.concatenate(...  18.6 us
    concatenate x1, other arithmetic, transform_tables(): jnp.concatenate([jnp.concatenate([spec_re, spec_im], 1), jnp.concatenate(...  18 us
    dot_general x8, matrix products, hsum(): jnp.einsum(form, left, right, precision=HIGHEST, preferred_element_type=j...  14.8 us
    dot_general x16, matrix products, hdot(): jnp.dot(left, right, precision=HIGHEST, preferred_element_type=jnp.float32)  13.2 us
    all_to_all x2, waiting for transfers between devices, from_everyone(): return lax.all_to_all(copies, axis, split_axis=0, concat_axis=0, tiled=True)  11.3 us
    all_to_all x1, starting transfers between devices, local(): lax.all_to_all(mine, 'facet', split_axis=1, concat_axis=1, tiled=True)  9.44 us
    all_to_all x1, starting transfers between devices, sum_at_owner(): parts = lax.all_to_all(cut_along(shard, dim, peers), axis, 0, 0, tiled=True)  9.14 us
  transfers between devices with their start and end apart: 6, of which 5 were waited for; matrix products, arithmetic and copies ran while one was open for 18% of the time, Pallas kernels for 0%

commit v1 on v0

v1 whole, which is shorter than its diff:
```python
import math

import jax
import jax.numpy as jnp
import numpy as np
from jax import lax
from jax.experimental import pallas as pl
from jax.experimental.pallas import tpu as pltpu
from jax.sharding import PartitionSpec as P

L = 4096
M = 128
SG = 256
VB = 256
R = 64
NF = 16
NT = 8
NB = 2
RD = R // NT
NH = L // M
NV = NT * VB
TWO_PI = 2.0 * math.pi
BF = jnp.bfloat16
F32 = jnp.float32

ROOT = np.exp(2j * np.pi * np.arange(L) / L)


def wave(left, right, period, sign):
    steps = (np.outer(left, right) % period) * (L // period)
    table = ROOT[steps]
    return table if sign > 0 else table.conj()


def as_real(matrix):
    return np.block([[matrix.real, -matrix.imag], [matrix.imag, matrix.real]])


def half(matrix):
    return jnp.asarray(np.asarray(matrix, np.float32), BF)


def tables():
    lanes = np.arange(M)
    highs = np.arange(NH)
    fwd_rows = as_real(wave(lanes, highs, NH, -1))
    fwd_turn = wave(lanes, lanes, L, -1)
    fwd_high = as_real(wave(highs, lanes, NH, -1) / math.sqrt(L))
    bwd_rows = as_real(wave(lanes, highs, NH, 1))
    bwd_turn = wave(lanes, lanes, L, 1) / math.sqrt(M)
    bwd_full = wave(highs, lanes, NH, 1)
    bwd_high = np.stack([as_real(part) for part in np.split(bwd_full, NB)])
    k_table = wave(lanes, np.arange(SG), SG, 1) / math.sqrt(M)
    k_left = as_real(k_table.T)
    k_right = as_real(k_table).reshape(2, M, 2, SG)
    k_right = np.block([[k_table.real, k_table.imag], [-k_table.imag, k_table.real]])
    k_back = np.concatenate([k_table.real.T, -k_table.imag.T], 1)
    return {
        "fwd_rows": half(fwd_rows),
        "fwd_turn": jnp.asarray(np.stack([fwd_turn.real, fwd_turn.imag]), F32),
        "fwd_high": half(fwd_high),
        "bwd_rows": half(bwd_rows),
        "bwd_turn": jnp.asarray(np.stack([bwd_turn.real, bwd_turn.imag]), F32),
        "bwd_high": half(bwd_high),
        "k_left": half(k_left),
        "k_left_t": half(k_left.T),
        "k_right": half(k_right),
        "k_back": half(k_back),
    }


COS_TERMS = [(-1.0) ** n / math.factorial(2 * n) for n in range(10)]
SIN_TERMS = [(-1.0) ** n / math.factorial(2 * n + 1) for n in range(10)]


def turn_angle(steps, period):
    steps = steps & (period - 1)
    steps = jnp.where(steps >= period // 2, steps - period, steps)
    return steps.astype(F32) * (TWO_PI / period)


def series(square, terms):
    total = jnp.full_like(square, terms[-1])
    for term in terms[-2::-1]:
        total = total * square + term
    return total


def cos_of(angle):
    return series(angle * angle, COS_TERMS)


def sin_of(angle):
    return angle * series(angle * angle, SIN_TERMS)


def dot(left, right):
    return jnp.dot(left, right, preferred_element_type=F32)


def dot_nt(left, right):
    return lax.dot_general(left, right, (((1,), (1,)), ((), ())), preferred_element_type=F32)


def column_phase(offset):
    lane = lax.broadcasted_iota(jnp.int32, (RD, M), 1)
    angle = turn_angle(lane * offset, L)
    return cos_of(angle), sin_of(angle)


def forward_kernel(offs, foffs, rows, w_rows, turn, w_high, out, xs, xo):
    side = lax.axis_index("sub")
    facet = lax.axis_index("facet")
    for part in range(2):
        whole = rows[part].astype(F32)
        for high in range(NH):
            xs[pl.ds((part * NH + high) * RD, RD), :] = whole[:, high * M : (high + 1) * M]
    stacked = jnp.concatenate(
        [xs[pl.ds(r, 2 * NH, stride=RD), :].astype(BF) for r in range(RD)], 1
    )
    mixed = dot(w_rows[...], stacked)
    t_re = turn[0]
    t_im = turn[1]
    for r in range(RD):
        y_re = mixed[:M, r * M : (r + 1) * M]
        y_im = mixed[M:, r * M : (r + 1) * M]
        z_re = (y_re * t_re - y_im * t_im).astype(BF)
        z_im = (y_re * t_im + y_im * t_re).astype(BF)
        xo[pl.ds(r, 2 * NH, stride=RD), :] = dot_nt(
            w_high[...], jnp.concatenate([z_re, z_im], 1)
        )
    p_cos, p_sin = column_phase(foffs[facet, 1])
    lane = lax.broadcasted_iota(jnp.int32, (RD, M), 1)
    for a in range(NF):
        tuning = offs[a * NB + side, 1]
        low = tuning & (M - 1)
        first = tuning // M
        second = (first + 1) & (NH - 1)
        shift = (M - low) & (M - 1)
        parts = []
        for part in range(2):
            here = xo[pl.ds(pl.multiple_of((part * NH + first) * RD, RD), RD), :]
            after = xo[pl.ds(pl.multiple_of((part * NH + second) * RD, RD), RD), :]
            parts.append(pltpu.roll(jnp.where(lane >= low, here, after), shift, axis=1))
        re = parts[0] * p_cos - parts[1] * p_sin
        im = parts[0] * p_sin + parts[1] * p_cos
        out[a] = jnp.concatenate([re, im], 0).astype(BF)


def setup_kernel(offs, foffs, slots, k_left, k_left_t, col_t, row_t, lift, lift_t):
    facet = lax.axis_index("facet")
    team = lax.axis_index("team")
    side = lax.axis_index("sub")
    height = 16
    count = lax.broadcasted_iota(jnp.int32, (height, M), 0)
    for place, target in ((0, row_t), (2, col_t)):
        for tile in range(NV // M):
            spot = slots[tile // 2, place + tile % 2 : place + tile % 2 + 1, :]
            spot = jnp.broadcast_to(spot.astype(jnp.int32), (height, M))
            angle = turn_angle(spot * count, 4 * SG)
            cos, sin = cos_of(angle), sin_of(angle)
            step = turn_angle(spot * height, 4 * SG)
            step_cos, step_sin = cos_of(step), sin_of(step)
            for block in range(SG // height):
                target[block * height : (block + 1) * height, tile * M : (tile + 1) * M] = (
                    cos.astype(BF)
                )
                target[
                    SG + block * height : SG + (block + 1) * height, tile * M : (tile + 1) * M
                ] = sin.astype(BF)
                if block + 1 < SG // height:
                    cos, sin = cos * step_cos - sin * step_sin, cos * step_sin + sin * step_cos
    shift_u = offs[facet * NB + side, 0]
    row = lax.broadcasted_iota(jnp.int32, (2 * RD, 2 * M), 0)
    lane = lax.broadcasted_iota(jnp.int32, (2 * RD, 2 * M), 1)
    p = lane & (M - 1)
    quarter = (row // RD - lane // M) * (L // 4)
    row_turn = (L // R) * (p + shift_u) * (team * RD + (row & (RD - 1)))
    base = quarter - row_turn
    blocks = []
    for f in range(NF):
        steps = base + p * foffs[f, 0]
        blocks.append((cos_of(turn_angle(steps, L)) * (1.0 / 32.0)).astype(BF))
    joined = jnp.concatenate(blocks, 0)
    lift[...] = dot_nt(k_left[...], joined).astype(BF)
    lift_t[...] = dot(joined, k_left_t[...]).astype(BF)


def predict_kernel(spec, lift, k_right, aterm, col_t, row_t, out, rows_out):
    side = lax.axis_index("sub")
    turned = dot(lift[...], spec[...]).astype(BF)
    image = dot(jnp.concatenate([turned[:SG], turned[SG:]], 1), k_right[...])
    weight = aterm[side].astype(F32)
    w_re = image[:, :SG] * weight
    w_im = image[:, SG:] * weight
    left = jnp.concatenate(
        [
            jnp.concatenate([w_re, w_im], 1).astype(BF),
            jnp.concatenate([w_im, -w_re], 1).astype(BF),
        ],
        0,
    )
    width = 256
    for chunk in range(NV // width):
        span = slice(chunk * width, (chunk + 1) * width)
        z = dot(left, col_t[:, span])
        cos = row_t[:SG, span].astype(F32)
        sin = row_t[SG:, span].astype(F32)
        re = jnp.sum(cos * z[:SG] + sin * z[SG:], 0, keepdims=True) * (1.0 / SG)
        im = jnp.sum(cos * z[SG:] - sin * z[:SG], 0, keepdims=True) * (1.0 / SG)
        for tile in range(width // M):
            at = chunk * (width // M) + tile
            rows_out[at : at + 1, :] = re[:, tile * M : (tile + 1) * M]
            rows_out[NV // M + at : NV // M + at + 1, :] = im[:, tile * M : (tile + 1) * M]
    packed = rows_out[...].astype(BF)
    for peer in range(NT):
        out[peer] = packed


def grid_kernel(counts, parts, slots, col_t, row_t, aterm, lift_t, k_back, out, spread, res):
    facet = lax.axis_index("facet")
    side = lax.axis_index("sub")
    total = parts[0].astype(F32)
    for peer in range(1, NT):
        total = total + parts[peer].astype(F32)
    res[...] = total
    lane = lax.broadcasted_iota(jnp.int32, (1, M), 1)
    for tile in range(NV // M):
        t = tile // 2
        h = tile % 2
        live = lane + h * M < counts[facet, side, t]
        weight = jnp.where(live, slots[t, 8 + h : 9 + h, :], 0.0)
        r_re = weight * (slots[t, 4 + h : 5 + h, :] - res[tile : tile + 1, :])
        r_im = weight * (slots[t, 6 + h : 7 + h, :] - res[NV // M + tile : NV // M + tile + 1, :])
        span = slice(tile * M, (tile + 1) * M)
        cos = col_t[:SG, span].astype(F32)
        sin = col_t[SG:, span].astype(F32)
        spread[:SG, span] = (r_re * cos - r_im * sin).astype(BF)
        spread[SG:, span] = (r_re * sin + r_im * cos).astype(BF)
    both = dot_nt(row_t[...], spread[...])
    weight = aterm[side].astype(F32) * (1.0 / SG)
    g_re = (both[:SG, :SG] - both[SG:, SG:]) * weight
    g_im = (both[:SG, SG:] + both[SG:, :SG]) * weight
    grid = jnp.concatenate([g_re, g_im], 0).astype(BF)
    low = dot(lift_t[...], grid).astype(BF)
    back = dot(low, k_back[...])
    for f in range(NF):
        top = back[f * 16 : f * 16 + 8]
        bot = back[f * 16 + 8 : f * 16 + 16]
        re = top[:, :M] - bot[:, M:]
        im = bot[:, :M] + top[:, M:]
        both_parts = jnp.concatenate([re, im], 0).astype(BF)
        for b in range(NB):
            out[f * NB + b] = both_parts


def update_kernel(offs, foffs, folded, w_rows, turn, w_high, out, us, os):
    facet = lax.axis_index("facet")
    side = lax.axis_index("sub")
    us[...] = jnp.zeros_like(us)
    p_cos, p_sin = column_phase(foffs[facet, 1])
    lane = lax.broadcasted_iota(jnp.int32, (RD, M), 1)
    for s in range(NF * NB):
        tuning = offs[s, 1]
        low = tuning & (M - 1)
        first = tuning // M
        second = (first + 1) & (NH - 1)
        both = folded[s].astype(F32)
        re = both[:RD] * p_cos + both[RD:] * p_sin
        im = both[RD:] * p_cos - both[:RD] * p_sin
        for part, value in ((0, re), (1, im)):
            turned = pltpu.roll(value, low, axis=1)
            here = pl.ds(pl.multiple_of((part * NH + first) * RD, RD), RD)
            after = pl.ds(pl.multiple_of((part * NH + second) * RD, RD), RD)
            us[here, :] += jnp.where(lane >= low, turned, 0.0)
            us[after, :] += jnp.where(lane >= low, 0.0, turned)
    stacked = jnp.concatenate(
        [us[pl.ds(r, 2 * NH, stride=RD), :].astype(BF) for r in range(RD)], 1
    )
    mixed = dot(w_rows[...], stacked)
    t_re = turn[0]
    t_im = turn[1]
    high = w_high[side]
    n_out = NH // NB
    for r in range(RD):
        y_re = mixed[:M, r * M : (r + 1) * M]
        y_im = mixed[M:, r * M : (r + 1) * M]
        z_re = (y_re * t_re - y_im * t_im).astype(BF)
        z_im = (y_re * t_im + y_im * t_re).astype(BF)
        os[pl.ds(r, 2 * n_out, stride=RD), :] = dot_nt(high, jnp.concatenate([z_re, z_im], 1))
    for part in range(2):
        for h in range(n_out):
            at = (part * n_out + h) * RD
            out[part, :, h * M : (h + 1) * M] = os[at : at + RD, :]


def shape(*dims, dtype=BF):
    return jax.ShapeDtypeStruct(dims, dtype)


SMEM = pl.BlockSpec(memory_space=pltpu.SMEM)
VMEM = pl.BlockSpec(memory_space=pltpu.VMEM)
PARAMS = pltpu.CompilerParams(vmem_limit_bytes=48 * 2**20)


def call(kernel, specs, outs, scratch, name):
    single = not isinstance(outs, (list, tuple))
    return pl.pallas_call(
        kernel,
        out_shape=outs,
        in_specs=specs,
        out_specs=VMEM if single else [VMEM] * len(outs),
        scratch_shapes=scratch,
        compiler_params=PARAMS,
        name=name,
    )


def local(facet_rows, sub_offsets, facet_offsets, aterm, cells, observed, weights, counts):
    side = lax.axis_index("sub")
    t = tables()
    mine = lambda array: lax.dynamic_index_in_dim(array[0, :, 0], side, 0, keepdims=False)
    slot_rows = jnp.concatenate(
        [
            mine(cells).astype(F32).reshape(4, M),
            mine(observed).astype(F32).reshape(4, M),
            mine(weights).astype(F32).reshape(2, M),
            jnp.zeros((6, M), F32),
        ],
        0,
    )
    slots = lax.all_to_all(
        jnp.broadcast_to(slot_rows, (NT, 16, M)), "team", 0, 0, tiled=True
    )
    windows = call(
        forward_kernel,
        [SMEM, SMEM, VMEM, VMEM, VMEM, VMEM],
        shape(NF, 2 * RD, M),
        [pltpu.VMEM((2 * L // M * RD, M), F32)] * 2,
        "windows",
    )(sub_offsets, facet_offsets, facet_rows[0], t["fwd_rows"], t["fwd_turn"], t["fwd_high"])
    arrived = lax.all_to_all(windows, "facet", 0, 0, tiled=True)
    col_t, row_t, lift, lift_t = call(
        setup_kernel,
        [SMEM, SMEM, VMEM, VMEM, VMEM],
        [shape(2 * SG, NV), shape(2 * SG, NV), shape(2 * SG, 2 * M), shape(2 * M, 2 * SG)],
        [],
        "setup",
    )(sub_offsets, facet_offsets, slots, t["k_left"], t["k_left_t"])
    parts = call(
        predict_kernel,
        [VMEM] * 6,
        shape(NT, 2 * NV // M, M),
        [pltpu.VMEM((2 * NV // M, M), F32)],
        "predict",
    )(arrived.reshape(2 * M, M), lift, t["k_right"], aterm[0], col_t, row_t)
    gathered = lax.all_to_all(parts, "team", 0, 0, tiled=True)
    folded = call(
        grid_kernel,
        [SMEM] + [VMEM] * 7,
        shape(NF * NB, 2 * RD, M),
        [pltpu.VMEM((2 * SG, NV), BF), pltpu.VMEM((2 * NV // M, M), F32)],
        "grid",
    )(counts, gathered, slots, col_t, row_t, aterm[0], lift_t, t["k_back"])
    returned = lax.all_to_all(folded, ("facet", "sub"), 0, 0, tiled=True)
    update = call(
        update_kernel,
        [SMEM, SMEM, VMEM, VMEM, VMEM, VMEM],
        shape(2, RD, L // NB, dtype=F32),
        [pltpu.VMEM((2 * NH * RD, M), F32), pltpu.VMEM((NH * RD, M), F32)],
        "update",
    )(sub_offsets, facet_offsets, returned, t["bwd_rows"], t["bwd_turn"], t["bwd_high"])
    return update[None]


def solution(mesh):
    placed = (
        P("facet", None, "team", None),
        P(),
        P(),
        P("facet", None, None, None),
        P("facet", None, "team", None, None),
        P("facet", None, "team", None, None),
        P("facet", None, "team", None),
        P(),
    )
    return jax.shard_map(
        local,
        mesh=mesh,
        in_specs=placed,
        out_specs=P("facet", None, "team", "sub"),
        check_vma=False,
    )
```

time: 233 us -> 76.2 us (0.33); the launches traced: 229 us -> 75.4 us
  other arithmetic: 92.3 us -> 2.12 us
  waiting for transfers between devices: 57 us -> 7.14 us
  matrix products: 30.9 us -> 0 us
  blocking collectives: 0 us -> 15.9 us
  starting transfers between devices: 37 us -> 22.3 us
  Pallas kernels: 0 us -> 13.9 us
  local copies, waits for them, and re-layouts: 10.5 us -> 14 us
    all_to_all x5 -> x3, waiting for transfers between devices: 55.9 us -> 7.14 us  [the longest x1 7.06 us: local(): gathered = lax.all_to_all(parts, 'team', 0, 0, tiled=True)]
    concatenate x5 -> x1, other arithmetic: 36.7 us -> 0.08 us  [local(): jnp.concatenate([mine(cells).astype(F32).reshape(4, M), mine(observed).as...]
    dot_general x28 -> x0, matrix products: 30.9 us -> none  [the longest x8 14.8 us: hsum(): jnp.einsum(form, left, right, precision=HIGHEST, preferred_element_type=j...]
    convert_element_type x9 -> x3, other arithmetic: 22.8 us -> 2.05 us  [the longest x1 0.68 us: local(): mine(cells).astype(F32).reshape(4, M)]
    neg x3 -> x0, other arithmetic: 17 us -> none  [the longest x1 7.87 us: transform_tables(): -spec_im]
    all_to_all x0 -> x1, blocking collectives: none -> 15.9 us  [local(): returned = lax.all_to_all(folded, ('facet', 'sub'), 0, 0, tiled=True)]
    pallas_call x0 -> x5, Pallas kernels: none -> 13.9 us  [the longest x1 3.13 us: local(): call(setup_kernel, [SMEM, SMEM, VMEM, VMEM, VMEM], [shape(2 * SG, NV), sh...]
    unnamed x26 -> x37, local copies, waits for them, and re-layouts: 0.85 us -> 13.3 us
  transfers between devices with their start and end apart: 6 -> 3, of which waited for: 5 -> 2; matrix products, arithmetic and copies ran while one was open for 18% -> 2% of each run, Pallas kernels for 0% -> 7%
where the time goes in v1:
time: 76.2 us; the launch traced here: 75.4 us
  starting transfers between devices  22.3 us (29%)
  blocking collectives  15.9 us (21%)
  local copies, waits for them, and re-layouts  14 us (18%)
  Pallas kernels  13.9 us (18%)
  waiting for transfers between devices  7.14 us (9%)
  other arithmetic  2.12 us (3%)
    all_to_all x1, blocking collectives, local(): returned = lax.all_to_all(folded, ('facet', 'sub'), 0, 0, tiled=True)  15.9 us
    unnamed x37, local copies, waits for them, and re-layouts  13.3 us
    all_to_all x1, starting transfers between devices, local(): lax.all_to_all(jnp.broadcast_to(slot_rows, (NT, 16, M)), 'team', 0, 0, ti...  9.01 us
    all_to_all x1, starting transfers between devices, local(): arrived = lax.all_to_all(windows, 'facet', 0, 0, tiled=True)  7.5 us
    all_to_all x1, waiting for transfers between devices, local(): gathered = lax.all_to_all(parts, 'team', 0, 0, tiled=True)  7.06 us
    all_to_all x1, starting transfers between devices, local(): gathered = lax.all_to_all(parts, 'team', 0, 0, tiled=True)  5.74 us
    pallas_call x1, Pallas kernels, local(): call(setup_kernel, [SMEM, SMEM, VMEM, VMEM, VMEM], [shape(2 * SG, NV), sh...  3.13 us
    pallas_call x1, Pallas kernels, local(): call(grid_kernel, [SMEM] + [VMEM] * 7, shape(NF * NB, 2 * RD, M), [pltpu....  2.96 us
  transfers between devices with their start and end apart: 3, of which 2 were waited for; matrix products, arithmetic and copies ran while one was open for 2% of the time, Pallas kernels for 7%

profile of v1, /device:TPU:1, one launch (start us, length us, event | category | flops | bytes accessed | tf_op | source)
XLA Modules:
  0.0 75.4 jit_solution(11119836533705159915)
XLA Ops:
  0.0 0.7 dynamic-slice_convert_fusion
  0.7 0.7 dynamic-slice_convert_fusion.2
  1.4 0.7 dynamic-slice_convert_fusion.1
  2.1 0.1 pad.3.clone
  2.2 0.1 maximum_maximum_fusion
  2.2 0.6 broadcast_in_dim.10
  2.9 9.0 %all-to-all-start.1 = ((f32[8,16,128]{2,1,0:T(8,128)}), f32[8,16,128]{2,1,0:T(8,128)S(1)}, u32[]{:S(2)}, u32[]{:S(2)}) async-start(f32[8,16,128]{2,1,0:T(8,128)} %broadcast_in_dim.10), calls=%async_computation.1 | async-start | bytes 131072 | tf_op jit(solution)/shard_map/all_to_all | solution.py:332
  11.9 0.8 %copy.24.offs = s32[32,2]{1,0:T(8,128)S(1)} copy(s32[32,2]{0,1:T(2,128)} %param.19) | data formatting | bytes 512 | tf_op args[1]
  12.6 0.8 %copy.25.foffs = s32[16,2]{1,0:T(8,128)S(1)} copy(s32[16,2]{0,1:T(2,128)} %param.20) | data formatting | bytes 256 | tf_op args[2]
  13.4 0.0 copy-start.8
  13.4 0.9 %copy-done.8 = bf16[1,2,8,4096]{3,2,1,0:T(8,128)(2,1)S(1)} copy-done((bf16[1,2,8,4096]{3,2,1,0:T(8,128)(2,1)S(1)}, bf16[1,2,8,4096]{3,2,1,0:T(8,128)(2,1)}, u32[]{:S(2)}) %copy-start.8) | copy-done | bytes 131096
  14.3 0.9 %copy-done.10 = f32[2,128,128]{2,1,0:T(8,128)S(1)} copy-done((f32[2,128,128]{2,1,0:T(8,128)S(1)}, f32[2,128,128]{2,1,0:T(8,128)}, u32[]{:S(2)}) %copy-start.10) | copy-done | bytes 131096
  15.2 0.0 copy-start.12
  15.2 0.8 %copy-done.12 = bf16[256,64]{1,0:T(8,128)(2,1)S(1)} copy-done((bf16[256,64]{1,0:T(8,128)(2,1)S(1)}, bf16[256,64]{1,0:T(8,128)(2,1)}, u32[]{:S(2)}) %copy-start.12) | copy-done | bytes 32792
  16.0 0.0 copy-start.15
  16.0 0.8 %copy-done.15 = bf16[64,256]{1,0:T(8,128)(2,1)S(1)} copy-done((bf16[64,256]{1,0:T(8,128)(2,1)S(1)}, bf16[64,256]{1,0:T(8,128)(2,1)}, u32[]{:S(2)}) %copy-start.15) | copy-done | bytes 32792
  16.8 2.2 %windows.1 = bf16[16,16,128]{2,1,0:T(8,128)(2,1)} custom-call(s32[32,2]{1,0:T(8,128)S(1)} %copy.24.offs, s32[16,2]{1,0:T(8,128)S(1)} %copy.25.foffs, bf16[2,8,4096]{2,1,0:T(8,128)(2,1)S(1)} %bitcast.8, bf16[256,64]{1,0:T(8,128)(2,1)S(1)} %copy-done.12, f32[2,128,128]{2,1,0:T(8,128)S(1)} %copy-done.10, bf16[64,256]{1,0:T(8,128)(2,1)S(1)} %copy-done.15), custom_call_target="tpu_custom_call" | custom-call | tf_op jit(solution)/shard_map/windows/pallas_call | solution.py:335
  19.0 0.1 all-to-all-done.1.slots
  19.1 7.5 %all-to-all-start = ((bf16[16,16,128]{2,1,0:T(8,128)(2,1)}), bf16[16,16,128]{2,1,0:T(8,128)(2,1)S(1)}, u32[]{:S(2)}, u32[]{:S(2)}) async-start(bf16[16,16,128]{2,1,0:T(8,128)(2,1)} %windows.1), calls=%async_computation | async-start | bytes 131072 | tf_op jit(solution)/shard_map/all_to_all | solution.py:342
  26.6 0.0 copy-start.5
  26.6 0.9 %copy-done.5 = bf16[256,512]{1,0:T(8,128)(2,1)S(1)} copy-done((bf16[256,512]{1,0:T(8,128)(2,1)S(1)}, bf16[256,512]{1,0:T(8,128)(2,1)}, u32[]{:S(2)}) %copy-start.5) | copy-done | bytes 262168
  27.6 0.0 copy-start.7
  27.6 0.9 %copy-done.7 = bf16[512,256]{1,0:T(8,128)(2,1)S(1)} copy-done((bf16[512,256]{1,0:T(8,128)(2,1)S(1)}, bf16[512,256]{1,0:T(8,128)(2,1)}, u32[]{:S(2)}) %copy-start.7) | copy-done | bytes 262168
  28.5 3.1 %setup.1 = (bf16[512,2048]{1,0:T(8,128)(2,1)S(1)}, bf16[512,2048]{1,0:T(8,128)(2,1)S(1)}, bf16[512,256]{1,0:T(8,128)(2,1)S(1)}, bf16[256,512]{1,0:T(8,128)(2,1)S(1)}) custom-call(s32[32,2]{1,0:T(8,128)S(1)} %copy.24.offs, s32[16,2]{1,0:T(8,128)S(1)} %copy.25.foffs, f32[8,16,128]{2,1,0:T(8,128)S(1)} %all-to-all-done.1.slots, bf16[512,256]{1,0:T(8,128)(2,1)S(1)} %copy-done.7, ...), custom_call_target="tpu_custom_call" | custom-call | tf_op jit(solution)/shard_map/setup/pallas_call | solution.py:343
  31.7 0.0 copy-start
  31.7 1.3 %copy-done = bf16[512,2048]{1,0:T(8,128)(2,1)} copy-done((bf16[512,2048]{1,0:T(8,128)(2,1)}, bf16[512,2048]{1,0:T(8,128)(2,1)S(1)}, u32[]{:S(2)}) %copy-start) | copy-done | bytes 2097176
  33.0 0.0 all-to-all-done
  33.0 0.0 copy-start.1
  33.0 1.6 %copy-done.1 = bf16[512,2048]{1,0:T(8,128)(2,1)S(1)} copy-done((bf16[512,2048]{1,0:T(8,128)(2,1)S(1)}, bf16[512,2048]{1,0:T(8,128)(2,1)}, u32[]{:S(2)}) %copy-start.1) | copy-done | bytes 2097176
  34.6 0.0 copy-start.3
  34.6 0.9 %copy-done.3 = bf16[1,2,256,256]{3,2,1,0:T(8,128)(2,1)S(1)} copy-done((bf16[1,2,256,256]{3,2,1,0:T(8,128)(2,1)S(1)}, bf16[1,2,256,256]{3,2,1,0:T(8,128)(2,1)}, u32[]{:S(2)}) %copy-start.3) | copy-done | bytes 262168
  35.5 0.0 copy-start.6
  35.5 0.9 %copy-done.6 = bf16[256,512]{1,0:T(8,128)(2,1)S(1)} copy-done((bf16[256,512]{1,0:T(8,128)(2,1)S(1)}, bf16[256,512]{1,0:T(8,128)(2,1)}, u32[]{:S(2)}) %copy-start.6) | copy-done | bytes 262168
  36.5 0.0 copy-start.16
  36.5 2.8 %predict.1 = bf16[8,32,128]{2,1,0:T(8,128)(2,1)} custom-call(bf16[256,128]{1,0:T(8,128)(2,1)S(1)} %bitcast.7, bf16[512,256]{1,0:T(8,128)(2,1)S(1)} %get-tuple-element.9.lift, bf16[256,512]{1,0:T(8,128)(2,1)S(1)} %copy-done.6, bf16[2,256,256]{2,1,0:T(8,128)(2,1)S(1)} %bitcast.5, bf16[512,2048]{1,0:T(8,128)(2,1)S(1)} %get-tuple-element.10.col_t, ...), custom_call_target="tpu_custom_call" | custom-call | tf_op jit(solution)/shard_map/predict/pallas_call | solution.py:350
  39.3 5.7 %all-to-all-start.2 = ((bf16[8,32,128]{2,1,0:T(8,128)(2,1)}), bf16[8,32,128]{2,1,0:T(8,128)(2,1)S(1)}, u32[]{:S(2)}, u32[]{:S(2)}) async-start(bf16[8,32,128]{2,1,0:T(8,128)(2,1)} %predict.1), calls=%async_computation.2 | async-start | bytes 131072 | tf_op jit(solution)/shard_map/all_to_all | solution.py:357
  45.0 0.0 copy-done.16
  45.0 0.1 copy.23.counts
  45.1 7.1 %all-to-all-done.2.parts = bf16[8,32,128]{2,1,0:T(8,128)(2,1)S(1)} async-done(((bf16[8,32,128]{2,1,0:T(8,128)(2,1)}), bf16[8,32,128]{2,1,0:T(8,128)(2,1)S(1)}, u32[]{:S(2)}, u32[]{:S(2)}) %all-to-all-start.2) | async-done | bytes 65568 | tf_op jit(solution)/shard_map/all_to_all | solution.py:357
  52.2 0.0 copy-done.4
  52.2 0.0 copy-done.9
  52.2 1.6 %copy-done.2 = bf16[512,2048]{1,0:T(8,128)(2,1)S(1)} copy-done((bf16[512,2048]{1,0:T(8,128)(2,1)S(1)}, bf16[512,2048]{1,0:T(8,128)(2,1)}, u32[]{:S(2)}) %copy-start.2) | copy-done | bytes 2097176
  53.8 3.0 %grid.1 = bf16[32,16,128]{2,1,0:T(8,128)(2,1)S(1)} custom-call(s32[16,2,8]{2,1,0:T(2,128)S(1)} %copy.23.counts, bf16[8,32,128]{2,1,0:T(8,128)(2,1)S(1)} %all-to-all-done.2.parts, f32[8,16,128]{2,1,0:T(8,128)S(1)} %all-to-all-done.1.slots, bf16[512,2048]{1,0:T(8,128)(2,1)S(1)} %get-tuple-element.10.col_t, bf16[512,2048]{1,0:T(8,128)(2,1)S(1)} %copy-done.2, ...), custom_call_target="tpu_custom_call" | custom-call | tf_op jit(solution)/shard_map/grid/pallas_call | solution.py:358
  56.7 15.9 %all_to_all.20.folded = bf16[32,16,128]{2,1,0:T(8,128)(2,1)S(1)} all-to-all(bf16[32,16,128]{2,1,0:T(8,128)(2,1)S(1)} %grid.1), channel_id=1, replica_groups=mesh['facet'=16,'team'=8,'sub'=2] {'facet','sub'}, dimensions={0} | all-to-all | bytes 262144 | tf_op jit(solution)/shard_map/all_to_all | solution.py:365
  72.6 0.0 copy-done.11
  72.6 0.0 copy-done.13
  72.6 0.0 copy-done.14
  72.7 2.7 %update.1 = f32[2,8,2048]{2,1,0:T(8,128)} custom-call(s32[32,2]{1,0:T(8,128)S(1)} %copy.24.offs, s32[16,2]{1,0:T(8,128)S(1)} %copy.25.foffs, bf16[32,16,128]{2,1,0:T(8,128)(2,1)S(1)} %all_to_all.20.folded, bf16[256,64]{1,0:T(8,128)(2,1)S(1)} %copy-done.13, f32[2,128,128]{2,1,0:T(8,128)S(1)} %copy-done.11, bf16[2,32,256]{2,1,0:T(8,128)(2,1)S(1)} %copy-done.14), custom_call_target="tpu_custom_call" | custom-call | tf_op jit(solution)/shard_map/update/pallas_call | solution.py:366
  (10 shorter events, 0.0 us)
Async XLA Ops:
  2.9 16.3 %all-to-all-start.1 = ((f32[8,16,128]{2,1,0:T(8,128)}), f32[8,16,128]{2,1,0:T(8,128)S(1)}, u32[]{:S(2)}, u32[]{:S(2)}) async-start(f32[8,16,128]{2,1,0:T(8,128)} %broadcast_in_dim.10), calls=%async_computation.1 | async-start | bytes 131072 | tf_op jit(solution)/shard_map/all_to_all | solution.py:332
  13.4 0.9 %copy-start.8 = (bf16[1,2,8,4096]{3,2,1,0:T(8,128)(2,1)S(1)}, bf16[1,2,8,4096]{3,2,1,0:T(8,128)(2,1)}, u32[]{:S(2)}) copy-start(bf16[1,2,8,4096]{3,2,1,0:T(8,128)(2,1)} %param.18) | copy-start | bytes 393220
  14.3 0.9 %copy-start.10 = (f32[2,128,128]{2,1,0:T(8,128)S(1)}, f32[2,128,128]{2,1,0:T(8,128)}, u32[]{:S(2)}) copy-start(f32[2,128,128]{2,1,0:T(8,128)} %constant.42.clone.turn) | copy-start | bytes 393220
  15.2 0.8 %copy-start.12 = (bf16[256,64]{1,0:T(8,128)(2,1)S(1)}, bf16[256,64]{1,0:T(8,128)(2,1)}, u32[]{:S(2)}) copy-start(bf16[256,64]{1,0:T(8,128)(2,1)} %constant.41.clone.w_rows) | copy-start | bytes 98308
  16.0 0.8 %copy-start.15 = (bf16[64,256]{1,0:T(8,128)(2,1)S(1)}, bf16[64,256]{1,0:T(8,128)(2,1)}, u32[]{:S(2)}) copy-start(bf16[64,256]{1,0:T(8,128)(2,1)} %constant.43.clone.w_high) | copy-start | bytes 98308
  19.1 13.9 %all-to-all-start = ((bf16[16,16,128]{2,1,0:T(8,128)(2,1)}), bf16[16,16,128]{2,1,0:T(8,128)(2,1)S(1)}, u32[]{:S(2)}, u32[]{:S(2)}) async-start(bf16[16,16,128]{2,1,0:T(8,128)(2,1)} %windows.1), calls=%async_computation | async-start | bytes 131072 | tf_op jit(solution)/shard_map/all_to_all | solution.py:342
  26.6 0.9 %copy-start.5 = (bf16[256,512]{1,0:T(8,128)(2,1)S(1)}, bf16[256,512]{1,0:T(8,128)(2,1)}, u32[]{:S(2)}) copy-start(bf16[256,512]{1,0:T(8,128)(2,1)} %constant.48.clone.k_left_t.k_right) | copy-start | bytes 786436
  27.6 0.9 %copy-start.7 = (bf16[512,256]{1,0:T(8,128)(2,1)S(1)}, bf16[512,256]{1,0:T(8,128)(2,1)}, u32[]{:S(2)}) copy-start(bf16[512,256]{1,0:T(8,128)(2,1)} %constant.47.clone.k_left) | copy-start | bytes 786436
  31.7 1.3 %copy-start = (bf16[512,2048]{1,0:T(8,128)(2,1)}, bf16[512,2048]{1,0:T(8,128)(2,1)S(1)}, u32[]{:S(2)}) copy-start(bf16[512,2048]{1,0:T(8,128)(2,1)S(1)} %get-tuple-element.11.row_t) | copy-start | bytes 6291460
  33.0 1.6 %copy-start.1 = (bf16[512,2048]{1,0:T(8,128)(2,1)S(1)}, bf16[512,2048]{1,0:T(8,128)(2,1)}, u32[]{:S(2)}) copy-start(bf16[512,2048]{1,0:T(8,128)(2,1)} %copy-done) | copy-start | bytes 6291460
  34.6 0.9 %copy-start.3 = (bf16[1,2,256,256]{3,2,1,0:T(8,128)(2,1)S(1)}, bf16[1,2,256,256]{3,2,1,0:T(8,128)(2,1)}, u32[]{:S(2)}) copy-start(bf16[1,2,256,256]{3,2,1,0:T(8,128)(2,1)} %param.21) | copy-start | bytes 786436
  35.5 0.9 %copy-start.6 = (bf16[256,512]{1,0:T(8,128)(2,1)S(1)}, bf16[256,512]{1,0:T(8,128)(2,1)}, u32[]{:S(2)}) copy-start(bf16[256,512]{1,0:T(8,128)(2,1)} %constant.48.clone.k_left_t.k_right) | copy-start | bytes 786436
  36.5 8.6 %copy-start.16 = (s32[16,2,8]{0,2,1:T(8,128)S(1)}, s32[16,2,8]{0,2,1:T(8,128)}, u32[]{:S(2)}) copy-start(s32[16,2,8]{0,2,1:T(8,128)} %param.25) | copy-start | bytes 3076
  36.5 15.7 %copy-start.4 = (bf16[1,2,256,256]{3,2,1,0:T(8,128)(2,1)S(1)}, bf16[1,2,256,256]{3,2,1,0:T(8,128)(2,1)}, u32[]{:S(2)}) copy-start(bf16[1,2,256,256]{3,2,1,0:T(8,128)(2,1)} %param.21) | copy-start | bytes 786436
  36.5 15.7 %copy-start.9 = (bf16[256,256]{1,0:T(8,128)(2,1)S(1)}, bf16[256,256]{1,0:T(8,128)(2,1)}, u32[]{:S(2)}) copy-start(bf16[256,256]{1,0:T(8,128)(2,1)} %constant.49.clone.k_back) | copy-start | bytes 393220
  39.3 12.9 %all-to-all-start.2 = ((bf16[8,32,128]{2,1,0:T(8,128)(2,1)}), bf16[8,32,128]{2,1,0:T(8,128)(2,1)S(1)}, u32[]{:S(2)}, u32[]{:S(2)}) async-start(bf16[8,32,128]{2,1,0:T(8,128)(2,1)} %predict.1), calls=%async_computation.2 | async-start | bytes 131072 | tf_op jit(solution)/shard_map/all_to_all | solution.py:357
  52.2 1.6 %copy-start.2 = (bf16[512,2048]{1,0:T(8,128)(2,1)S(1)}, bf16[512,2048]{1,0:T(8,128)(2,1)}, u32[]{:S(2)}) copy-start(bf16[512,2048]{1,0:T(8,128)(2,1)} %copy-done) | copy-start | bytes 6291460
  53.8 18.9 %copy-start.11 = (f32[2,128,128]{2,1,0:T(8,128)S(1)}, f32[2,128,128]{2,1,0:T(8,128)}, u32[]{:S(2)}) copy-start(f32[2,128,128]{2,1,0:T(8,128)} %constant.45.clone.turn) | copy-start | bytes 393220
  53.8 18.9 %copy-start.13 = (bf16[256,64]{1,0:T(8,128)(2,1)S(1)}, bf16[256,64]{1,0:T(8,128)(2,1)}, u32[]{:S(2)}) copy-start(bf16[256,64]{1,0:T(8,128)(2,1)} %constant.44.clone.w_rows) | copy-start | bytes 98308
  53.8 18.9 %copy-start.14 = (bf16[2,32,256]{2,1,0:T(8,128)(2,1)S(1)}, bf16[2,32,256]{2,1,0:T(8,128)(2,1)}, u32[]{:S(2)}) copy-start(bf16[2,32,256]{2,1,0:T(8,128)(2,1)} %constant.46.clone.w_high) | copy-start | bytes 98308

commit v2 on v1

v2 whole, which is shorter than its diff:
```python
import math

import jax
import jax.numpy as jnp
import numpy as np
from jax import lax
from jax.experimental import pallas as pl
from jax.experimental.pallas import tpu as pltpu
from jax.sharding import PartitionSpec as P

L = 4096
M = 128
SG = 256
VB = 256
R = 64
NF = 16
NT = 8
NB = 2
RD = R // NT
NH = L // M
NV = NT * VB
TWO_PI = 2.0 * math.pi
BF = jnp.bfloat16
F32 = jnp.float32

ROOT = np.exp(2j * np.pi * np.arange(L) / L)


def wave(left, right, period, sign):
    steps = (np.outer(left, right) % period) * (L // period)
    table = ROOT[steps]
    return table if sign > 0 else table.conj()


def as_real(matrix):
    return np.block([[matrix.real, -matrix.imag], [matrix.imag, matrix.real]])


def half(matrix):
    return jnp.asarray(np.asarray(matrix, np.float32), BF)


def tables():
    lanes = np.arange(M)
    highs = np.arange(NH)
    fwd_rows = as_real(wave(lanes, highs, NH, -1))
    fwd_turn = wave(lanes, lanes, L, -1)
    fwd_high = as_real(wave(highs, lanes, NH, -1) / math.sqrt(L))
    bwd_rows = as_real(wave(lanes, highs, NH, 1))
    bwd_turn = wave(lanes, lanes, L, 1) / math.sqrt(M)
    bwd_full = wave(highs, lanes, NH, 1)
    bwd_high = np.stack([as_real(part) for part in np.split(bwd_full, NB)])
    k_table = wave(lanes, np.arange(SG), SG, 1) / math.sqrt(M)
    k_left = as_real(k_table.T)
    k_right = np.block([[k_table.real, k_table.imag], [-k_table.imag, k_table.real]])
    k_back = np.concatenate([k_table.real.T, -k_table.imag.T], 1)
    return {
        "fwd_rows": half(fwd_rows),
        "fwd_turn": jnp.asarray(np.stack([fwd_turn.real, fwd_turn.imag]), F32),
        "fwd_high": half(fwd_high),
        "bwd_rows": half(bwd_rows),
        "bwd_turn": jnp.asarray(np.stack([bwd_turn.real, bwd_turn.imag]), F32),
        "bwd_high": half(bwd_high),
        "k_left": half(k_left),
        "k_left_t": half(k_left.T),
        "k_right": half(k_right),
        "k_back": half(k_back),
    }


COS_TERMS = [(-1.0) ** n / math.factorial(2 * n) for n in range(9)]
SIN_TERMS = [(-1.0) ** n / math.factorial(2 * n + 1) for n in range(8)]


def turn_angle(steps, period):
    steps = steps & (period - 1)
    steps = jnp.where(steps >= period // 2, steps - period, steps)
    return steps.astype(F32) * (TWO_PI / period)


def series(square, terms):
    total = jnp.full_like(square, terms[-1])
    for term in terms[-2::-1]:
        total = total * square + term
    return total


def cos_of(angle):
    return series(angle * angle, COS_TERMS)


def sin_of(angle):
    return angle * series(angle * angle, SIN_TERMS)


def dot(left, right):
    return jnp.dot(left, right, preferred_element_type=F32)


def dot_nt(left, right):
    return lax.dot_general(left, right, (((1,), (1,)), ((), ())), preferred_element_type=F32)


def column_phase(offset):
    lane = lax.broadcasted_iota(jnp.int32, (RD, M), 1)
    angle = turn_angle(lane * offset, L)
    return cos_of(angle), sin_of(angle)


def fetch(pairs, sems):
    copies = []
    for at, (source, target) in enumerate(pairs):
        copy = pltpu.make_async_copy(source, target, sems.at[at])
        copy.start()
        copies.append(copy)
    return copies


def slot_kernel(
    cells_h, seen_h, weights_h, rows_h, w_rows_h, turn_h, w_high_h,
    slots, stacked, w_rows, turn, w_high, cells, seen, weights, rows, xs, packed, sems,
):
    side = lax.axis_index("sub")
    copies = fetch(
        [
            (cells_h.at[0, side, 0], cells),
            (seen_h.at[0, side, 0], seen),
            (weights_h.at[0, 0], weights),
            (rows_h.at[0], rows),
            (w_rows_h, w_rows),
            (turn_h, turn),
            (w_high_h, w_high),
        ],
        sems,
    )
    packed[...] = jnp.zeros_like(packed)
    for copy in copies:
        copy.wait()
    pair = weights[...].astype(F32)
    weight = jnp.where(side == 0, pair[0:1], pair[1:2])
    for at in range(2):
        span = slice(at * M, (at + 1) * M)
        packed[at : at + 1, :] = cells[0:1, span].astype(F32)
        packed[2 + at : 3 + at, :] = cells[1:2, span].astype(F32)
        both = seen[:, span].astype(F32)
        packed[4 + at : 5 + at, :] = both[0:1]
        packed[6 + at : 7 + at, :] = both[1:2]
        packed[8 + at : 9 + at, :] = weight[:, span]
    for peer in range(NT):
        slots[peer] = packed[...]
    for part in range(2):
        whole = rows[part].astype(F32)
        for high in range(NH):
            xs[pl.ds((part * NH + high) * RD, RD), :] = whole[:, high * M : (high + 1) * M]
    for r in range(RD):
        stacked[:, r * M : (r + 1) * M] = xs[pl.ds(r, 2 * NH, stride=RD), :].astype(BF)


def forward_kernel(offs_h, foffs_h, stacked, w_rows, turn, w_high, out, offs, foffs, xo, sems):
    side = lax.axis_index("sub")
    facet = lax.axis_index("facet")
    copies = fetch([(offs_h, offs), (foffs_h, foffs)], sems)
    mixed = dot(w_rows[...], stacked[...])
    t_re = turn[0]
    t_im = turn[1]
    for r in range(RD):
        y_re = mixed[:M, r * M : (r + 1) * M]
        y_im = mixed[M:, r * M : (r + 1) * M]
        z_re = (y_re * t_re - y_im * t_im).astype(BF)
        z_im = (y_re * t_im + y_im * t_re).astype(BF)
        xo[pl.ds(r, 2 * NH, stride=RD), :] = dot_nt(
            w_high[...], jnp.concatenate([z_re, z_im], 1)
        )
    for copy in copies:
        copy.wait()
    p_cos, p_sin = column_phase(foffs[1, facet])
    lane = lax.broadcasted_iota(jnp.int32, (RD, M), 1)
    for a in range(NF):
        tuning = offs[1, a * NB + side]
        low = tuning & (M - 1)
        first = tuning // M
        second = (first + 1) & (NH - 1)
        shift = (M - low) & (M - 1)
        parts = []
        for part in range(2):
            here = xo[pl.ds(pl.multiple_of((part * NH + first) * RD, RD), RD), :]
            after = xo[pl.ds(pl.multiple_of((part * NH + second) * RD, RD), RD), :]
            parts.append(pltpu.roll(jnp.where(lane >= low, here, after), shift, axis=1))
        re = parts[0] * p_cos - parts[1] * p_sin
        im = parts[0] * p_sin + parts[1] * p_cos
        out[a] = jnp.concatenate([re, im], 0).astype(BF)


HEIGHT = 16
STEPS = SG // HEIGHT


def setup_kernel(
    offs_h, foffs_h, slots, k_left_h, k_left_t_h, k_right_h, aterm_h, k_back_h,
    col_t, row_base, row_step, lift, lift_t, k_right, aterm, k_back,
    offs, foffs, k_left, k_left_t, sems,
):
    facet = lax.axis_index("facet")
    team = lax.axis_index("team")
    side = lax.axis_index("sub")
    copies = fetch(
        [
            (offs_h, offs),
            (foffs_h, foffs),
            (k_left_h, k_left),
            (k_left_t_h, k_left_t),
            (k_right_h, k_right),
            (aterm_h.at[0, side], aterm),
            (k_back_h, k_back),
        ],
        sems,
    )
    count = lax.broadcasted_iota(jnp.int32, (HEIGHT, M), 0)

    def turns(place, tile):
        at = place + tile % 2
        spot = jnp.broadcast_to(slots[tile // 2, at : at + 1, :].astype(jnp.int32), (HEIGHT, M))
        angle = turn_angle(spot * count, 4 * SG)
        step = turn_angle(spot[:8] * HEIGHT, 4 * SG)
        return cos_of(angle), sin_of(angle), cos_of(step), sin_of(step)

    for tile in range(NV // M):
        lanes = slice(tile * M, (tile + 1) * M)
        cos, sin, step_cos, step_sin = turns(0, tile)
        row_base[0, :, lanes] = cos
        row_base[1, :, lanes] = sin
        row_step[0, :, lanes] = step_cos
        row_step[1, :, lanes] = step_sin
        cos, sin, step_cos, step_sin = turns(2, tile)
        step_cos = jnp.concatenate([step_cos, step_cos], 0)
        step_sin = jnp.concatenate([step_sin, step_sin], 0)
        for block in range(STEPS):
            at = block * HEIGHT
            col_t[at : at + HEIGHT, lanes] = cos.astype(BF)
            col_t[SG + at : SG + at + HEIGHT, lanes] = sin.astype(BF)
            if block + 1 < STEPS:
                cos, sin = cos * step_cos - sin * step_sin, cos * step_sin + sin * step_cos
    for copy in copies:
        copy.wait()
    shift_u = offs[0, facet * NB + side]
    row = lax.broadcasted_iota(jnp.int32, (2 * RD, 2 * M), 0)
    lane = lax.broadcasted_iota(jnp.int32, (2 * RD, 2 * M), 1)
    p = lane & (M - 1)
    quarter = (row // RD - lane // M) * (L // 4)
    row_turn = (L // R) * (p + shift_u) * (team * RD + (row & (RD - 1)))
    base = quarter - row_turn
    blocks = []
    for f in range(NF):
        steps = base + p * foffs[0, f]
        blocks.append((cos_of(turn_angle(steps, L)) * (1.0 / 32.0)).astype(BF))
    joined = jnp.concatenate(blocks, 0)
    lift[...] = dot_nt(k_left[...], joined).astype(BF)
    lift_t[...] = dot(joined, k_left_t[...]).astype(BF)


def twice(value):
    return jnp.concatenate([value, value], 0)


def predict_kernel(spec, lift, k_right, aterm, col_t, row_base, row_step, out, rows_out):
    turned = dot(lift[...], spec[...]).astype(BF)
    image = dot(jnp.concatenate([turned[:SG], turned[SG:]], 1), k_right[...])
    weight = aterm[...].astype(F32)
    w_re = image[:, :SG] * weight
    w_im = image[:, SG:] * weight
    left = jnp.concatenate(
        [
            jnp.concatenate([w_re, w_im], 1).astype(BF),
            jnp.concatenate([w_im, -w_re], 1).astype(BF),
        ],
        0,
    )
    for chunk in range(NT):
        span = slice(chunk * VB, (chunk + 1) * VB)
        z = dot(left, col_t[:, span])
        step_cos = twice(row_step[0, :, span])
        step_sin = twice(row_step[1, :, span])
        re = z[SG - HEIGHT : SG]
        im = z[2 * SG - HEIGHT :]
        for block in range(STEPS - 2, -1, -1):
            at = block * HEIGHT
            re, im = (
                re * step_cos + im * step_sin + z[at : at + HEIGHT],
                im * step_cos - re * step_sin + z[SG + at : SG + at + HEIGHT],
            )
        cos = row_base[0, :, span]
        sin = row_base[1, :, span]
        re, im = re * cos + im * sin, im * cos - re * sin
        re = jnp.sum(re, 0, keepdims=True) * (1.0 / SG)
        im = jnp.sum(im, 0, keepdims=True) * (1.0 / SG)
        for tile in range(VB // M):
            at = chunk * (VB // M) + tile
            rows_out[at : at + 1, :] = re[:, tile * M : (tile + 1) * M]
            rows_out[NV // M + at : NV // M + at + 1, :] = im[:, tile * M : (tile + 1) * M]
    packed = rows_out[...].astype(BF)
    for peer in range(NT):
        out[peer] = packed


def grid_kernel(
    counts, parts, slots, col_t, row_base, row_step, aterm, lift_t, k_back, out, spread, res
):
    facet = lax.axis_index("facet")
    side = lax.axis_index("sub")
    total = parts[0].astype(F32)
    for peer in range(1, NT):
        total = total + parts[peer].astype(F32)
    res[...] = total
    lane = lax.broadcasted_iota(jnp.int32, (1, M), 1)
    for tile in range(NV // M):
        t = tile // 2
        h = tile % 2
        live = lane + h * M < counts[side, t, facet]
        weight = jnp.where(live, slots[t, 8 + h : 9 + h, :], 0.0)
        r_re = weight * (slots[t, 4 + h : 5 + h, :] - res[tile : tile + 1, :])
        r_im = weight * (slots[t, 6 + h : 7 + h, :] - res[NV // M + tile : NV // M + tile + 1, :])
        span = slice(tile * M, (tile + 1) * M)
        step_cos = twice(row_step[0, :, span])
        step_sin = twice(row_step[1, :, span])
        cos = row_base[0, :, span]
        sin = row_base[1, :, span]
        re, im = r_re * cos - r_im * sin, r_re * sin + r_im * cos
        for block in range(STEPS):
            at = block * HEIGHT
            spread[at : at + HEIGHT, span] = re.astype(BF)
            spread[SG + at : SG + at + HEIGHT, span] = im.astype(BF)
            if block + 1 < STEPS:
                re, im = re * step_cos - im * step_sin, re * step_sin + im * step_cos
    both = dot_nt(spread[...], col_t[...])
    weight = aterm[...].astype(F32) * (1.0 / SG)
    g_re = (both[:SG, :SG] - both[SG:, SG:]) * weight
    g_im = (both[:SG, SG:] + both[SG:, :SG]) * weight
    grid = jnp.concatenate([g_re, g_im], 0).astype(BF)
    low = dot(lift_t[...], grid).astype(BF)
    back = dot(low, k_back[...])
    for f in range(NF):
        top = back[f * 16 : f * 16 + 8]
        bot = back[f * 16 + 8 : f * 16 + 16]
        re = top[:, :M] - bot[:, M:]
        im = bot[:, :M] + top[:, M:]
        both_parts = jnp.concatenate([re, im], 0).astype(BF)
        for b in range(NB):
            out[f * NB + b] = both_parts


def update_kernel(
    offs_h, foffs_h, folded, w_rows_h, turn_h, w_high_h,
    out, offs, foffs, us, os, w_rows, turn, w_high, sems,
):
    facet = lax.axis_index("facet")
    side = lax.axis_index("sub")
    copies = fetch(
        [
            (offs_h, offs),
            (foffs_h, foffs),
            (w_rows_h, w_rows),
            (turn_h, turn),
            (w_high_h.at[side], w_high),
        ],
        sems,
    )
    us[...] = jnp.zeros_like(us)
    for copy in copies[:2]:
        copy.wait()
    p_cos, p_sin = column_phase(foffs[1, facet])
    lane = lax.broadcasted_iota(jnp.int32, (RD, M), 1)
    for s in range(NF * NB):
        tuning = offs[1, s]
        low = tuning & (M - 1)
        first = tuning // M
        second = (first + 1) & (NH - 1)
        both = folded[s].astype(F32)
        re = both[:RD] * p_cos + both[RD:] * p_sin
        im = both[RD:] * p_cos - both[:RD] * p_sin
        for part, value in ((0, re), (1, im)):
            turned = pltpu.roll(value, low, axis=1)
            here = pl.ds(pl.multiple_of((part * NH + first) * RD, RD), RD)
            after = pl.ds(pl.multiple_of((part * NH + second) * RD, RD), RD)
            us[here, :] += jnp.where(lane >= low, turned, 0.0)
            us[after, :] += jnp.where(lane >= low, 0.0, turned)
    stacked = jnp.concatenate(
        [us[pl.ds(r, 2 * NH, stride=RD), :].astype(BF) for r in range(RD)], 1
    )
    for copy in copies[2:]:
        copy.wait()
    mixed = dot(w_rows[...], stacked)
    t_re = turn[0]
    t_im = turn[1]
    high = w_high[...]
    n_out = NH // NB
    for r in range(RD):
        y_re = mixed[:M, r * M : (r + 1) * M]
        y_im = mixed[M:, r * M : (r + 1) * M]
        z_re = (y_re * t_re - y_im * t_im).astype(BF)
        z_im = (y_re * t_im + y_im * t_re).astype(BF)
        os[pl.ds(r, 2 * n_out, stride=RD), :] = dot_nt(high, jnp.concatenate([z_re, z_im], 1))
    for part in range(2):
        for h in range(n_out):
            at = (part * n_out + h) * RD
            out[part, :, h * M : (h + 1) * M] = os[at : at + RD, :]


def shape(*dims, dtype=BF):
    return jax.ShapeDtypeStruct(dims, dtype)


SMEM = pl.BlockSpec(memory_space=pltpu.SMEM)
VMEM = pl.BlockSpec(memory_space=pltpu.VMEM)
HBM = pl.BlockSpec(memory_space=pltpu.HBM)
PARAMS = pltpu.CompilerParams(vmem_limit_bytes=24 * 2**20)


def buf(*dims, dtype=BF):
    return pltpu.VMEM(dims, dtype)


def smem(*dims):
    return pltpu.SMEM(dims, jnp.int32)


def sems(count):
    return pltpu.SemaphoreType.DMA((count,))


def call(kernel, specs, outs, scratch, name, places=None):
    single = not isinstance(outs, (list, tuple))
    return pl.pallas_call(
        kernel,
        out_shape=outs,
        in_specs=specs,
        out_specs=places or (VMEM if single else [VMEM] * len(outs)),
        scratch_shapes=scratch,
        compiler_params=PARAMS,
        name=name,
    )


def local(facet_rows, sub_offsets, facet_offsets, aterm, cells, observed, weights, counts):
    t = tables()
    offs = sub_offsets.T
    foffs = facet_offsets.T
    live = counts.transpose(1, 2, 0)
    keep = lambda array: pltpu.with_memory_space_constraint(array, pltpu.HBM)
    offs = keep(offs)
    foffs = keep(foffs)
    ids = [smem(2, NF * NB), smem(2, NF)]
    slot_rows, stacked, w_rows, turn, w_high = call(
        slot_kernel,
        [HBM] * 7,
        [
            shape(NT, 16, M, dtype=F32),
            shape(2 * NH, RD * M),
            shape(2 * M, 2 * NH),
            shape(2, M, M, dtype=F32),
            shape(2 * NH, 2 * M),
        ],
        [
            buf(2, VB, dtype=jnp.int32),
            buf(2, VB),
            buf(2, VB),
            buf(2, RD, L),
            buf(2 * NH * RD, M, dtype=F32),
            buf(16, M, dtype=F32),
            sems(7),
        ],
        "slots",
    )(
        keep(cells), keep(observed), keep(weights.transpose(0, 2, 1, 3)), keep(facet_rows),
        keep(t["fwd_rows"]), keep(t["fwd_turn"]), keep(t["fwd_high"]),
    )
    slots = lax.all_to_all(slot_rows, "team", 0, 0, tiled=True)
    windows = call(
        forward_kernel,
        [HBM] * 2 + [VMEM] * 4,
        shape(NF, 2 * RD, M),
        ids + [buf(2 * NH * RD, M, dtype=F32), sems(2)],
        "windows",
    )(offs, foffs, stacked, w_rows, turn, w_high)
    arrived = lax.all_to_all(windows, "facet", 0, 0, tiled=True)
    col_t, row_base, row_step, lift, lift_t, k_right, own_map, k_back = call(
        setup_kernel,
        [HBM, HBM, VMEM] + [HBM] * 5,
        [
            shape(2 * SG, NV),
            shape(2, HEIGHT, NV, dtype=F32),
            shape(2, 8, NV, dtype=F32),
            shape(2 * SG, 2 * M),
            shape(2 * M, 2 * SG),
            shape(2 * M, 2 * SG),
            shape(SG, SG),
            shape(SG, 2 * M),
        ],
        ids + [buf(2 * SG, 2 * M), buf(2 * M, 2 * SG), sems(7)],
        "setup",
    )(
        offs, foffs, slots, keep(t["k_left"]), keep(t["k_left_t"]), keep(t["k_right"]),
        keep(aterm), keep(t["k_back"]),
    )
    parts = call(
        predict_kernel,
        [VMEM] * 7,
        shape(NT, 2 * NV // M, M),
        [buf(2 * NV // M, M, dtype=F32)],
        "predict",
    )(arrived.reshape(2 * M, M), lift, k_right, own_map, col_t, row_base, row_step)
    gathered = lax.all_to_all(parts, "team", 0, 0, tiled=True)
    folded = call(
        grid_kernel,
        [SMEM] + [VMEM] * 8,
        shape(NF * NB, 2 * RD, M),
        [buf(2 * SG, NV), buf(2 * NV // M, M, dtype=F32)],
        "grid",
    )(live, gathered, slots, col_t, row_base, row_step, own_map, lift_t, k_back)
    returned = lax.all_to_all(folded, ("facet", "sub"), 0, 0, tiled=True)
    update = call(
        update_kernel,
        [HBM, HBM, VMEM, HBM, HBM, HBM],
        shape(2, RD, L // NB, dtype=F32),
        ids
        + [
            buf(2 * NH * RD, M, dtype=F32),
            buf(NH * RD, M, dtype=F32),
            buf(2 * M, 2 * NH),
            buf(2, M, M, dtype=F32),
            buf(NH, 2 * M),
            sems(5),
        ],
        "update",
    )(
        offs, foffs, returned,
        keep(t["bwd_rows"]), keep(t["bwd_turn"]), keep(t["bwd_high"]),
    )
    return update[None]


def solution(mesh):
    placed = (
        P("facet", None, "team", None),
        P(),
        P(),
        P("facet", None, None, None),
        P("facet", None, "team", None, None),
        P("facet", None, "team", None, None),
        P("facet", None, "team", None),
        P(),
    )
    return jax.shard_map(
        local,
        mesh=mesh,
        in_specs=placed,
        out_specs=P("facet", None, "team", "sub"),
        check_vma=False,
    )
```

time: 76.2 us -> 62.2 us (0.82)
  local copies, waits for them, and re-layouts: 14 us -> 0.66 us
  blocking collectives: 15.9 us -> 23.2 us
  starting transfers between devices: 22.3 us -> 16.5 us
  other arithmetic: 2.12 us -> 0 us
  waiting for transfers between devices: 7.14 us -> 9.05 us
  Pallas kernels: 13.9 us -> 12.3 us
    unnamed x37 -> x6, local copies, waits for them, and re-layouts: 13.3 us -> 0.66 us
    all_to_all x0 -> x1, blocking collectives: none -> 9.54 us  [local(): gathered = lax.all_to_all(parts, 'team', 0, 0, tiled=True)]
    all_to_all x2 -> x1, starting transfers between devices: 14.8 us -> 9.03 us  [local(): slots = lax.all_to_all(slot_rows, 'team', 0, 0, tiled=True)]
    all_to_all x1, waiting for transfers between devices: 0.01 us -> 3.4 us  [local(): arrived = lax.all_to_all(windows, 'facet', 0, 0, tiled=True)]
    all_to_all x1, blocking collectives: 15.9 us -> 13.7 us  [local(): returned = lax.all_to_all(folded, ('facet', 'sub'), 0, 0, tiled=True)]
    convert_element_type x3 -> x0, other arithmetic: 2.05 us -> none  [the longest x1 0.68 us: local(): mine(cells).astype(F32).reshape(4, M)]
    pallas_call x5 -> x6, Pallas kernels: 13.9 us -> 12.3 us  [the longest x1 2.57 us: local(): call(update_kernel, [HBM, HBM, VMEM, HBM, HBM, HBM], shape(2, RD, L // NB...]
    all_to_all x2 -> x1, waiting for transfers between devices: 7.13 us -> 5.65 us  [local(): slots = lax.all_to_all(slot_rows, 'team', 0, 0, tiled=True)]
  transfers between devices with their start and end apart: 3 -> 2, of which waited for: 2 -> 2; matrix products, arithmetic and copies ran while one was open for 2% -> 0% of each run, Pallas kernels for 7% -> 5%
where the time goes in v2:
time: 62.2 us; the launch traced here: 61.8 us
  blocking collectives  23.2 us (37%)
  starting transfers between devices  16.5 us (27%)
  Pallas kernels  12.3 us (20%)
  waiting for transfers between devices  9.05 us (15%)
  local copies, waits for them, and re-layouts  0.66 us (1%)
    all_to_all x1, blocking collectives, local(): returned = lax.all_to_all(folded, ('facet', 'sub'), 0, 0, tiled=True)  13.7 us
    all_to_all x1, blocking collectives, local(): gathered = lax.all_to_all(parts, 'team', 0, 0, tiled=True)  9.54 us
    all_to_all x1, starting transfers between devices, local(): slots = lax.all_to_all(slot_rows, 'team', 0, 0, tiled=True)  9.03 us
    all_to_all x1, starting transfers between devices, local(): arrived = lax.all_to_all(windows, 'facet', 0, 0, tiled=True)  7.5 us
    all_to_all x1, waiting for transfers between devices, local(): slots = lax.all_to_all(slot_rows, 'team', 0, 0, tiled=True)  5.65 us
    all_to_all x1, waiting for transfers between devices, local(): arrived = lax.all_to_all(windows, 'facet', 0, 0, tiled=True)  3.4 us
    pallas_call x1, Pallas kernels, local(): call(update_kernel, [HBM, HBM, VMEM, HBM, HBM, HBM], shape(2, RD, L // NB...  2.57 us
    pallas_call x1, Pallas kernels, local(): call(grid_kernel, [SMEM] + [VMEM] * 8, shape(NF * NB, 2 * RD, M), [buf(2...  2.56 us
  transfers between devices with their start and end apart: 2, of which 2 were waited for; matrix products, arithmetic and copies ran while one was open for 0% of the time, Pallas kernels for 5%

profile of v2, /device:TPU:1, one launch (start us, length us, event | category | flops | bytes accessed | tf_op | source)
XLA Modules:
  0.0 61.8 jit_solution(11502178907629054326)
XLA Ops:
  0.0 1.8 %slots.1 = (f32[8,16,128]{2,1,0:T(8,128)}, bf16[64,1024]{1,0:T(8,128)(2,1)S(1)}, bf16[256,64]{1,0:T(8,128)(2,1)S(1)}, f32[2,128,128]{2,1,0:T(8,128)S(1)}, bf16[64,256]{1,0:T(8,128)(2,1)S(1)}) custom-call(s32[1,2,1,2,256]{4,3,2,1,0:T(2,128)} %cells_h.1, bf16[1,2,1,2,256]{4,3,2,1,0:T(2,128)(2,1)} %seen_h.1, bf16[1,1,2,256]{3,2,1,0:T(2,128)(2,1)} %bitcast.14, ...), custom_call_target="tpu_custom_call" | custom-call | tf_op jit(solution)/shard_map/slots/pallas_call | solution.py:452
  1.8 9.0 %all-to-all-start.1 = ((f32[8,16,128]{2,1,0:T(8,128)}), f32[8,16,128]{2,1,0:T(8,128)S(1)}, u32[]{:S(2)}, u32[]{:S(2)}) async-start(f32[8,16,128]{2,1,0:T(8,128)} %get-tuple-element.22), calls=%async_computation.1 | async-start | bytes 131072 | tf_op jit(solution)/shard_map/all_to_all | solution.py:476
  10.8 1.6 %windows.1 = bf16[16,16,128]{2,1,0:T(8,128)(2,1)} custom-call(s32[2,32]{1,0:T(2,128)} %bitcast.8, s32[2,16]{1,0:T(2,128)} %bitcast.11, bf16[64,1024]{1,0:T(8,128)(2,1)S(1)} %get-tuple-element.18.stacked, bf16[256,64]{1,0:T(8,128)(2,1)S(1)} %get-tuple-element.19.w_rows, f32[2,128,128]{2,1,0:T(8,128)S(1)} %get-tuple-element.20.turn, ...), custom_call_target="tpu_custom_call" | custom-call | tf_op jit(solution)/shard_map/windows/pallas_call | solution.py:477
  12.4 5.7 %all-to-all-done.1.slots = f32[8,16,128]{2,1,0:T(8,128)S(1)} async-done(((f32[8,16,128]{2,1,0:T(8,128)}), f32[8,16,128]{2,1,0:T(8,128)S(1)}, u32[]{:S(2)}, u32[]{:S(2)}) %all-to-all-start.1) | async-done | bytes 65568 | tf_op jit(solution)/shard_map/all_to_all | solution.py:476
  18.1 7.5 %all-to-all-start = ((bf16[16,16,128]{2,1,0:T(8,128)(2,1)}), bf16[16,16,128]{2,1,0:T(8,128)(2,1)S(1)}, u32[]{:S(2)}, u32[]{:S(2)}) async-start(bf16[16,16,128]{2,1,0:T(8,128)(2,1)} %windows.1), calls=%async_computation | async-start | bytes 131072 | tf_op jit(solution)/shard_map/all_to_all | solution.py:484
  25.6 0.0 copy-start.2
  25.6 1.8 %setup.1 = (bf16[512,2048]{1,0:T(8,128)(2,1)S(1)}, f32[2,16,2048]{2,1,0:T(8,128)S(1)}, f32[2,8,2048]{2,1,0:T(8,128)S(1)}, bf16[512,256]{1,0:T(8,128)(2,1)S(1)}, ...) custom-call(s32[2,32]{1,0:T(2,128)} %bitcast.9, ...), custom_call_target="tpu_custom_call" | custom-call | tf_op jit(solution)/shard_map/setup/pallas_call | solution.py:485
  27.4 0.0 copy-start
  27.4 0.6 %copy-done = bf16[256,256]{1,0:T(8,128)(2,1)} copy-done((bf16[256,256]{1,0:T(8,128)(2,1)}, bf16[256,256]{1,0:T(8,128)(2,1)S(1)}, u32[]{:S(2)}) %copy-start) | copy-done | bytes 131096
  28.0 3.4 %all-to-all-done = bf16[16,16,128]{2,1,0:T(8,128)(2,1)S(1)} async-done(((bf16[16,16,128]{2,1,0:T(8,128)(2,1)}), bf16[16,16,128]{2,1,0:T(8,128)(2,1)S(1)}, u32[]{:S(2)}, u32[]{:S(2)}) %all-to-all-start) | async-done | bytes 65568 | tf_op jit(solution)/shard_map/all_to_all | solution.py:484
  31.4 0.0 copy-start.1
  31.4 2.0 %predict.1 = bf16[8,32,128]{2,1,0:T(8,128)(2,1)S(1)} custom-call(bf16[256,128]{1,0:T(8,128)(2,1)S(1)} %bitcast.6, bf16[512,256]{1,0:T(8,128)(2,1)S(1)} %get-tuple-element.23.lift, bf16[256,512]{1,0:T(8,128)(2,1)S(1)} %get-tuple-element.24.k_right, bf16[256,256]{1,0:T(8,128)(2,1)S(1)} %get-tuple-element.25.aterm, ...), custom_call_target="tpu_custom_call" | custom-call | tf_op jit(solution)/shard_map/predict/pallas_call | solution.py:504
  33.5 9.5 %all_to_all.20.parts = bf16[8,32,128]{2,1,0:T(8,128)(2,1)S(1)} all-to-all(bf16[8,32,128]{2,1,0:T(8,128)(2,1)S(1)} %predict.1), channel_id=1, replica_groups=mesh['facet'=16,'team'=8,'sub'=2] {'team'}, dimensions={0} | all-to-all | bytes 131072 | tf_op jit(solution)/shard_map/all_to_all | solution.py:511
  43.0 0.0 copy-done.2
  43.0 0.0 copy-done.1
  43.0 2.6 %grid.1 = bf16[32,16,128]{2,1,0:T(8,128)(2,1)S(1)} custom-call(s32[2,8,16]{2,1,0:T(8,128)S(1)} %bitcast.7, bf16[8,32,128]{2,1,0:T(8,128)(2,1)S(1)} %all_to_all.20.parts, f32[8,16,128]{2,1,0:T(8,128)S(1)} %all-to-all-done.1.slots, bf16[512,2048]{1,0:T(8,128)(2,1)S(1)} %get-tuple-element.26.col_t, f32[2,16,2048]{2,1,0:T(8,128)S(1)} %get-tuple-element.27.row_base, ...), custom_call_target="tpu_custom_call" | custom-call | tf_op jit(solution)/shard_map/grid/pallas_call | solution.py:512
  45.6 13.7 %all_to_all.21.folded = bf16[32,16,128]{2,1,0:T(8,128)(2,1)S(1)} all-to-all(bf16[32,16,128]{2,1,0:T(8,128)(2,1)S(1)} %grid.1), channel_id=1, replica_groups=mesh['facet'=16,'team'=8,'sub'=2] {'facet','sub'}, dimensions={0} | all-to-all | bytes 262144 | tf_op jit(solution)/shard_map/all_to_all | solution.py:519
  59.3 2.6 %update.1 = f32[2,8,2048]{2,1,0:T(8,128)} custom-call(s32[2,32]{1,0:T(2,128)} %bitcast.10, s32[2,16]{1,0:T(2,128)} %bitcast.13, bf16[32,16,128]{2,1,0:T(8,128)(2,1)S(1)} %all_to_all.21.folded, bf16[256,64]{1,0:T(8,128)(2,1)} %constant.21.clone.w_rows_h, f32[2,128,128]{2,1,0:T(8,128)} %constant.22.clone.turn_h, bf16[2,32,256]{2,1,0:T(8,128)(2,1)} %constant.23.clone.w_high_h), custom_call_target="tpu_custom_call" | custom-call | tf_op jit(solution)/shard_map/update/pallas_call | solution.py:520
Async XLA Ops:
  1.8 16.3 %all-to-all-start.1 = ((f32[8,16,128]{2,1,0:T(8,128)}), f32[8,16,128]{2,1,0:T(8,128)S(1)}, u32[]{:S(2)}, u32[]{:S(2)}) async-start(f32[8,16,128]{2,1,0:T(8,128)} %get-tuple-element.22), calls=%async_computation.1 | async-start | bytes 131072 | tf_op jit(solution)/shard_map/all_to_all | solution.py:476
  18.1 13.3 %all-to-all-start = ((bf16[16,16,128]{2,1,0:T(8,128)(2,1)}), bf16[16,16,128]{2,1,0:T(8,128)(2,1)S(1)}, u32[]{:S(2)}, u32[]{:S(2)}) async-start(bf16[16,16,128]{2,1,0:T(8,128)(2,1)} %windows.1), calls=%async_computation | async-start | bytes 131072 | tf_op jit(solution)/shard_map/all_to_all | solution.py:484
  25.6 17.4 %copy-start.2 = (s32[16,2,8]{0,2,1:T(8,128)S(1)}, s32[16,2,8]{0,2,1:T(8,128)}, u32[]{:S(2)}) copy-start(s32[16,2,8]{0,2,1:T(8,128)} %param.25) | copy-start | bytes 3076
  27.4 0.7 %copy-start = (bf16[256,256]{1,0:T(8,128)(2,1)}, bf16[256,256]{1,0:T(8,128)(2,1)S(1)}, u32[]{:S(2)}) copy-start(bf16[256,256]{1,0:T(8,128)(2,1)S(1)} %get-tuple-element.30.k_back) | copy-start | bytes 393220
  31.4 11.6 %copy-start.1 = (bf16[256,256]{1,0:T(8,128)(2,1)S(1)}, bf16[256,256]{1,0:T(8,128)(2,1)}, u32[]{:S(2)}) copy-start(bf16[256,256]{1,0:T(8,128)(2,1)} %copy-done) | copy-start | bytes 393220

commit v3 on v2

--- a/solution.py
+++ b/solution.py
@@ -116,51 +116,36 @@
     return copies
 
 
-def slot_kernel(
-    cells_h, seen_h, weights_h, rows_h, w_rows_h, turn_h, w_high_h,
-    slots, stacked, w_rows, turn, w_high, cells, seen, weights, rows, xs, packed, sems,
+def forward_kernel(
+    offs_h, foffs_h, cells_h, rows_h, w_rows_h, turn_h, w_high_h,
+    out, offs_v, foffs_v, cells_v, offs, foffs, rows, w_rows, turn, w_high, xs, xo, sems,
 ):
     side = lax.axis_index("sub")
+    facet = lax.axis_index("facet")
     copies = fetch(
         [
-            (cells_h.at[0, side, 0], cells),
-            (seen_h.at[0, side, 0], seen),
-            (weights_h.at[0, 0], weights),
             (rows_h.at[0], rows),
             (w_rows_h, w_rows),
             (turn_h, turn),
             (w_high_h, w_high),
+            (offs_h, offs),
+            (foffs_h, foffs),
+            (offs_h, offs_v),
+            (foffs_h, foffs_v),
+            (cells_h.at[0, :, 0], cells_v),
         ],
         sems,
     )
-    packed[...] = jnp.zeros_like(packed)
     for copy in copies:
         copy.wait()
-    pair = weights[...].astype(F32)
-    weight = jnp.where(side == 0, pair[0:1], pair[1:2])
-    for at in range(2):
-        span = slice(at * M, (at + 1) * M)
-        packed[at : at + 1, :] = cells[0:1, span].astype(F32)
-        packed[2 + at : 3 + at, :] = cells[1:2, span].astype(F32)
-        both = seen[:, span].astype(F32)
-        packed[4 + at : 5 + at, :] = both[0:1]
-        packed[6 + at : 7 + at, :] = both[1:2]
-        packed[8 + at : 9 + at, :] = weight[:, span]
-    for peer in range(NT):
-        slots[peer] = packed[...]
     for part in range(2):
         whole = rows[part].astype(F32)
         for high in range(NH):
             xs[pl.ds((part * NH + high) * RD, RD), :] = whole[:, high * M : (high + 1) * M]
-    for r in range(RD):
-        stacked[:, r * M : (r + 1) * M] = xs[pl.ds(r, 2 * NH, stride=RD), :].astype(BF)
-
-
-def forward_kernel(offs_h, foffs_h, stacked, w_rows, turn, w_high, out, offs, foffs, xo, sems):
-    side = lax.axis_index("sub")
-    facet = lax.axis_index("facet")
-    copies = fetch([(offs_h, offs), (foffs_h, foffs)], sems)
-    mixed = dot(w_rows[...], stacked[...])
+    stacked = jnp.concatenate(
+        [xs[pl.ds(r, 2 * NH, stride=RD), :].astype(BF) for r in range(RD)], 1
+    )
+    mixed = dot(w_rows[...], stacked)
     t_re = turn[0]
     t_im = turn[1]
     for r in range(RD):
@@ -171,14 +156,12 @@
         xo[pl.ds(r, 2 * NH, stride=RD), :] = dot_nt(
             w_high[...], jnp.concatenate([z_re, z_im], 1)
         )
-    for copy in copies:
-        copy.wait()
     p_cos, p_sin = column_phase(foffs[1, facet])
     lane = lax.broadcasted_iota(jnp.int32, (RD, M), 1)
     for a in range(NF):
         tuning = offs[1, a * NB + side]
         low = tuning & (M - 1)
-        first = tuning // M
+        first = tuning >> 7
         second = (first + 1) & (NH - 1)
         shift = (M - low) & (M - 1)
         parts = []
@@ -191,35 +174,70 @@
         out[a] = jnp.concatenate([re, im], 0).astype(BF)
 
 
+SENT = 40
+OBS = 2 * NV // M
 HEIGHT = 16
 STEPS = SG // HEIGHT
 
 
 def setup_kernel(
-    offs_h, foffs_h, slots, k_left_h, k_left_t_h, k_right_h, aterm_h, k_back_h,
-    col_t, row_base, row_step, lift, lift_t, k_right, aterm, k_back,
-    offs, foffs, k_left, k_left_t, sems,
+    offs_v, foffs_v, near_h, far_h, k_left_h, k_left_t_h, k_right_h, aterm_h, seen_h, weights_h,
+    col_t, row_base, row_step, lift, lift_t, k_right, aterm, tail,
+    offs, foffs, near, far, k_left, k_left_t, spots, seen, weights, sems,
 ):
     facet = lax.axis_index("facet")
     team = lax.axis_index("team")
     side = lax.axis_index("sub")
     copies = fetch(
         [
-            (offs_h, offs),
-            (foffs_h, foffs),
+            (offs_v, offs),
+            (foffs_v, foffs),
             (k_left_h, k_left),
             (k_left_t_h, k_left_t),
+            (near_h.at[:, side], near),
+            (far_h.at[:, side], far),
             (k_right_h, k_right),
             (aterm_h.at[0, side], aterm),
-            (k_back_h, k_back),
+            (seen_h.at[0, side, 0], seen),
+            (weights_h.at[0, 0], weights),
         ],
         sems,
     )
+    for copy in copies[:2]:
+        copy.wait()
+    shift_u = offs[0, facet * NB + side]
+    row = lax.broadcasted_iota(jnp.int32, (2 * RD, 2 * M), 0)
+    lane = lax.broadcasted_iota(jnp.int32, (2 * RD, 2 * M), 1)
+    p = lane & (M - 1)
+    quarter = ((row >> 3) - (lane >> 7)) * (L // 4)
+    row_turn = (L // R) * (p + shift_u) * (team * RD + (row & (RD - 1)))
+    base = quarter - row_turn
+    blocks = []
+    for f in range(NF):
+        steps = base + p * foffs[0, f]
+        blocks.append((cos_of(turn_angle(steps, L)) * (1.0 / 32.0)).astype(BF))
+    joined = jnp.concatenate(blocks, 0)
+    for copy in copies[2:]:
+        copy.wait()
+    lift[...] = dot_nt(k_left[...], joined).astype(BF)
+    lift_t[...] = dot(joined, k_left_t[...]).astype(BF)
+    pair = weights[...].astype(F32)
+    weight = jnp.where(side == 0, pair[0:1], pair[1:2])
+    both = seen[...].astype(F32)
+    tail[...] = jnp.zeros_like(tail)
+    for at in range(2):
+        half = slice(at * M, (at + 1) * M)
+        tail[at : at + 1, :] = both[0:1, half]
+        tail[2 + at : 3 + at, :] = both[1:2, half]
+        tail[4 + at : 5 + at, :] = weight[:, half]
+    for step in range(NT // 2):
+        spots[team ^ step] = near[step]
+        spots[team ^ (step + NT // 2)] = far[step]
     count = lax.broadcasted_iota(jnp.int32, (HEIGHT, M), 0)
 
     def turns(place, tile):
-        at = place + tile % 2
-        spot = jnp.broadcast_to(slots[tile // 2, at : at + 1, :].astype(jnp.int32), (HEIGHT, M))
+        half = slice(tile % 2 * M, (tile % 2 + 1) * M)
+        spot = jnp.broadcast_to(spots[tile // 2, place : place + 1, half], (HEIGHT, M))
         angle = turn_angle(spot * count, 4 * SG)
         step = turn_angle(spot[:8] * HEIGHT, 4 * SG)
         return cos_of(angle), sin_of(angle), cos_of(step), sin_of(step)
@@ -231,38 +249,24 @@
         row_base[1, :, lanes] = sin
         row_step[0, :, lanes] = step_cos
         row_step[1, :, lanes] = step_sin
-        cos, sin, step_cos, step_sin = turns(2, tile)
-        step_cos = jnp.concatenate([step_cos, step_cos], 0)
-        step_sin = jnp.concatenate([step_sin, step_sin], 0)
+        cos, sin, step_cos, step_sin = turns(1, tile)
+        step_cos = twice(step_cos)
+        step_sin = twice(step_sin)
         for block in range(STEPS):
             at = block * HEIGHT
             col_t[at : at + HEIGHT, lanes] = cos.astype(BF)
             col_t[SG + at : SG + at + HEIGHT, lanes] = sin.astype(BF)
             if block + 1 < STEPS:
                 cos, sin = cos * step_cos - sin * step_sin, cos * step_sin + sin * step_cos
-    for copy in copies:
-        copy.wait()
-    shift_u = offs[0, facet * NB + side]
-    row = lax.broadcasted_iota(jnp.int32, (2 * RD, 2 * M), 0)
-    lane = lax.broadcasted_iota(jnp.int32, (2 * RD, 2 * M), 1)
-    p = lane & (M - 1)
-    quarter = (row // RD - lane // M) * (L // 4)
-    row_turn = (L // R) * (p + shift_u) * (team * RD + (row & (RD - 1)))
-    base = quarter - row_turn
-    blocks = []
-    for f in range(NF):
-        steps = base + p * foffs[0, f]
-        blocks.append((cos_of(turn_angle(steps, L)) * (1.0 / 32.0)).astype(BF))
-    joined = jnp.concatenate(blocks, 0)
-    lift[...] = dot_nt(k_left[...], joined).astype(BF)
-    lift_t[...] = dot(joined, k_left_t[...]).astype(BF)
 
 
 def twice(value):
     return jnp.concatenate([value, value], 0)
 
 
-def predict_kernel(spec, lift, k_right, aterm, col_t, row_base, row_step, out, rows_out):
+def predict_kernel(
+    spec, lift, k_right, aterm, col_t, row_base, row_step, tail, out, rows_out
+):
     turned = dot(lift[...], spec[...]).astype(BF)
     image = dot(jnp.concatenate([turned[:SG], turned[SG:]], 1), k_right[...])
     weight = aterm[...].astype(F32)
@@ -297,28 +301,35 @@
             at = chunk * (VB // M) + tile
             rows_out[at : at + 1, :] = re[:, tile * M : (tile + 1) * M]
             rows_out[NV // M + at : NV // M + at + 1, :] = im[:, tile * M : (tile + 1) * M]
+    rows_out[OBS:, :] = tail[...]
     packed = rows_out[...].astype(BF)
     for peer in range(NT):
         out[peer] = packed
 
 
 def grid_kernel(
-    counts, parts, slots, col_t, row_base, row_step, aterm, lift_t, k_back, out, spread, res
+    counts, parts, col_t, row_base, row_step, aterm, lift_t, k_back_h,
+    out, spread, res, slots, k_back, sems,
 ):
     facet = lax.axis_index("facet")
     side = lax.axis_index("sub")
-    total = parts[0].astype(F32)
+    copies = fetch([(k_back_h, k_back)], sems)
+    part = parts[0].astype(F32)
+    total = part[:OBS]
+    slots[0] = part[OBS:]
     for peer in range(1, NT):
-        total = total + parts[peer].astype(F32)
+        part = parts[peer].astype(F32)
+        total = total + part[:OBS]
+        slots[peer] = part[OBS:]
     res[...] = total
     lane = lax.broadcasted_iota(jnp.int32, (1, M), 1)
     for tile in range(NV // M):
         t = tile // 2
         h = tile % 2
         live = lane + h * M < counts[side, t, facet]
-        weight = jnp.where(live, slots[t, 8 + h : 9 + h, :], 0.0)
-        r_re = weight * (slots[t, 4 + h : 5 + h, :] - res[tile : tile + 1, :])
-        r_im = weight * (slots[t, 6 + h : 7 + h, :] - res[NV // M + tile : NV // M + tile + 1, :])
+        weight = jnp.where(live, slots[t, 4 + h : 5 + h, :], 0.0)
+        r_re = weight * (slots[t, h : 1 + h, :] - res[tile : tile + 1, :])
+        r_im = weight * (slots[t, 2 + h : 3 + h, :] - res[NV // M + tile : NV // M + tile + 1, :])
         span = slice(tile * M, (tile + 1) * M)
         step_cos = twice(row_step[0, :, span])
         step_sin = twice(row_step[1, :, span])
@@ -337,6 +348,7 @@
     g_im = (both[:SG, SG:] + both[SG:, :SG]) * weight
     grid = jnp.concatenate([g_re, g_im], 0).astype(BF)
     low = dot(lift_t[...], grid).astype(BF)
+    copies[0].wait()
     back = dot(low, k_back[...])
     for f in range(NF):
         top = back[f * 16 : f * 16 + 8]
@@ -372,7 +384,7 @@
     for s in range(NF * NB):
         tuning = offs[1, s]
         low = tuning & (M - 1)
-        first = tuning // M
+        first = tuning >> 7
         second = (first + 1) & (NH - 1)
         both = folded[s].astype(F32)
         re = both[:RD] * p_cos + both[RD:] * p_sin
@@ -412,6 +424,7 @@
 SMEM = pl.BlockSpec(memory_space=pltpu.SMEM)
 VMEM = pl.BlockSpec(memory_space=pltpu.VMEM)
 HBM = pl.BlockSpec(memory_space=pltpu.HBM)
+ANY = pl.BlockSpec(memory_space=pl.ANY)
 PARAMS = pltpu.CompilerParams(vmem_limit_bytes=24 * 2**20)
 
 
@@ -427,7 +440,7 @@
     return pltpu.SemaphoreType.DMA((count,))
 
 
-def call(kernel, specs, outs, scratch, name, places=None):
+def call(kernel, specs, outs, scratch, name, places=None, cost=None):
     single = not isinstance(outs, (list, tuple))
     return pl.pallas_call(
         kernel,
@@ -436,8 +449,14 @@
         out_specs=places or (VMEM if single else [VMEM] * len(outs)),
         scratch_shapes=scratch,
         compiler_params=PARAMS,
+        cost_estimate=cost,
         name=name,
     )
+
+
+def partner(value, mask):
+    pairs = [(source, source ^ mask) for source in range(NT)]
+    return lax.ppermute(value, "team", pairs)
 
 
 def local(facet_rows, sub_offsets, facet_offsets, aterm, cells, observed, weights, counts):
@@ -449,42 +468,38 @@
     offs = keep(offs)
     foffs = keep(foffs)
     ids = [smem(2, NF * NB), smem(2, NF)]
-    slot_rows, stacked, w_rows, turn, w_high = call(
-        slot_kernel,
+    others = [partner(cells, mask) for mask in (1, 2, 3)]
+    windows, offs_v, foffs_v, cells_v = call(
+        forward_kernel,
         [HBM] * 7,
         [
-            shape(NT, 16, M, dtype=F32),
-            shape(2 * NH, RD * M),
-            shape(2 * M, 2 * NH),
-            shape(2, M, M, dtype=F32),
-            shape(2 * NH, 2 * M),
-        ],
-        [
-            buf(2, VB, dtype=jnp.int32),
-            buf(2, VB),
-            buf(2, VB),
+            shape(NF, 2 * RD, M),
+            shape(2, NF * NB, dtype=jnp.int32),
+            shape(2, NF, dtype=jnp.int32),
+            shape(NB, 2, VB, dtype=jnp.int32),
+        ],
+        ids
+        + [
             buf(2, RD, L),
+            buf(2 * M, 2 * NH),
+            buf(2, M, M, dtype=F32),
+            buf(2 * NH, 2 * M),
             buf(2 * NH * RD, M, dtype=F32),
-            buf(16, M, dtype=F32),
-            sems(7),
-        ],
-        "slots",
+            buf(2 * NH * RD, M, dtype=F32),
+            sems(9),
+        ],
+        "windows",
     )(
-        keep(cells), keep(observed), keep(weights.transpose(0, 2, 1, 3)), keep(facet_rows),
+        offs, foffs, keep(cells), keep(facet_rows),
         keep(t["fwd_rows"]), keep(t["fwd_turn"]), keep(t["fwd_high"]),
     )
-    slots = lax.all_to_all(slot_rows, "team", 0, 0, tiled=True)
-    windows = call(
-        forward_kernel,
-        [HBM] * 2 + [VMEM] * 4,
-        shape(NF, 2 * RD, M),
-        ids + [buf(2 * NH * RD, M, dtype=F32), sems(2)],
-        "windows",
-    )(offs, foffs, stacked, w_rows, turn, w_high)
+    *others, windows = lax.optimization_barrier((*others, windows))
+    near = jnp.stack([part.reshape(NB, 2, VB) for part in [cells_v] + others])
+    far = partner(near, NT // 2)
     arrived = lax.all_to_all(windows, "facet", 0, 0, tiled=True)
-    col_t, row_base, row_step, lift, lift_t, k_right, own_map, k_back = call(
+    col_t, row_base, row_step, lift, lift_t, k_right, own_map, tail = call(
         setup_kernel,
-        [HBM, HBM, VMEM] + [HBM] * 5,
+        [VMEM] * 2 + [ANY] * 2 + [HBM] * 6,
         [
             shape(2 * SG, NV),
             shape(2, HEIGHT, NV, dtype=F32),
@@ -493,33 +508,49 @@
             shape(2 * M, 2 * SG),
             shape(2 * M, 2 * SG),
             shape(SG, SG),
-            shape(SG, 2 * M),
-        ],
-        ids + [buf(2 * SG, 2 * M), buf(2 * M, 2 * SG), sems(7)],
+            shape(SENT - OBS, M, dtype=F32),
+        ],
+        ids
+        + [buf(NT // 2, 2, VB, dtype=jnp.int32)] * 2
+        + [
+            buf(2 * SG, 2 * M),
+            buf(2 * M, 2 * SG),
+            buf(NT, 2, VB, dtype=jnp.int32),
+            buf(2, VB),
+            buf(2, VB),
+            sems(10),
+        ],
         "setup",
+        cost=pl.CostEstimate(flops=20 * 10**9, transcendentals=0, bytes_accessed=2**22),
     )(
-        offs, foffs, slots, keep(t["k_left"]), keep(t["k_left_t"]), keep(t["k_right"]),
-        keep(aterm), keep(t["k_back"]),
+        offs_v, foffs_v, near, far, keep(t["k_left"]), keep(t["k_left_t"]),
+        keep(t["k_right"]), keep(aterm), keep(observed), keep(weights.transpose(0, 2, 1, 3)),
     )
     parts = call(
         predict_kernel,
-        [VMEM] * 7,
-        shape(NT, 2 * NV // M, M),
-        [buf(2 * NV // M, M, dtype=F32)],
+        [VMEM] * 8,
+        shape(NT, SENT, M),
+        [buf(SENT, M, dtype=F32)],
         "predict",
-    )(arrived.reshape(2 * M, M), lift, k_right, own_map, col_t, row_base, row_step)
+    )(arrived.reshape(2 * M, M), lift, k_right, own_map, col_t, row_base, row_step, tail)
     gathered = lax.all_to_all(parts, "team", 0, 0, tiled=True)
     folded = call(
         grid_kernel,
-        [SMEM] + [VMEM] * 8,
+        [SMEM] + [VMEM] * 6 + [HBM],
         shape(NF * NB, 2 * RD, M),
-        [buf(2 * SG, NV), buf(2 * NV // M, M, dtype=F32)],
+        [
+            buf(2 * SG, NV),
+            buf(OBS, M, dtype=F32),
+            buf(NT, SENT - OBS, M, dtype=F32),
+            buf(SG, 2 * M),
+            sems(1),
+        ],
         "grid",
-    )(live, gathered, slots, col_t, row_base, row_step, own_map, lift_t, k_back)
+    )(live, gathered, col_t, row_base, row_step, own_map, lift_t, keep(t["k_back"]))
     returned = lax.all_to_all(folded, ("facet", "sub"), 0, 0, tiled=True)
     update = call(
         update_kernel,
-        [HBM, HBM, VMEM, HBM, HBM, HBM],
+        [VMEM, VMEM, VMEM, HBM, HBM, HBM],
         shape(2, RD, L // NB, dtype=F32),
         ids
         + [
@@ -532,7 +563,7 @@
         ],
         "update",
     )(
-        offs, foffs, returned,
+        offs_v, foffs_v, returned,
         keep(t["bwd_rows"]), keep(t["bwd_turn"]), keep(t["bwd_high"]),
     )
     return update[None]

time: 62.2 us -> 58.3 us (0.937)
  waiting for transfers between devices: 9.05 us -> 4.3 us
  starting transfers between devices: 16.5 us -> 17.7 us
  blocking collectives: 23.2 us -> 24 us
  local copies, waits for them, and re-layouts: 0.66 us -> 0.01 us
    ppermute x0 -> x4, starting transfers between devices: none -> 10.5 us  [partner(): return lax.ppermute(value, 'team', pairs)]
    all_to_all x1 -> x0, starting transfers between devices: 9.03 us -> none  [local(): slots = lax.all_to_all(slot_rows, 'team', 0, 0, tiled=True)]
    all_to_all x1 -> x0, waiting for transfers between devices: 5.65 us -> none  [local(): slots = lax.all_to_all(slot_rows, 'team', 0, 0, tiled=True)]
    ppermute x0 -> x4, waiting for transfers between devices: none -> 0.9 us  [partner(): return lax.ppermute(value, 'team', pairs)]
    unnamed x6 -> x2, local copies, waits for them, and re-layouts: 0.66 us -> 0.01 us
    pallas_call x6 -> x5, Pallas kernels: 12.3 us -> 12 us  [the longest x1 2.75 us: local(): call(grid_kernel, [SMEM] + [VMEM] * 6 + [HBM], shape(NF * NB, 2 * RD, M),...]
  transfers between devices with their start and end apart: 2 -> 5, of which waited for: 2 -> 2; matrix products, arithmetic and copies ran while one was open for 0% -> 0% of each run, Pallas kernels for 5% -> 8%
where the time goes in v3:
time: 58.3 us; the launch traced here: 58.1 us
  blocking collectives  24 us (41%)
  starting transfers between devices  17.7 us (30%)
  Pallas kernels  12 us (21%)
  waiting for transfers between devices  4.3 us (7%)
    all_to_all x1, blocking collectives, local(): returned = lax.all_to_all(folded, ('facet', 'sub'), 0, 0, tiled=True)  14 us
    ppermute x4, starting transfers between devices, partner(): return lax.ppermute(value, 'team', pairs)  10.5 us
    all_to_all x1, blocking collectives, local(): gathered = lax.all_to_all(parts, 'team', 0, 0, tiled=True)  10 us
    all_to_all x1, starting transfers between devices, local(): arrived = lax.all_to_all(windows, 'facet', 0, 0, tiled=True)  7.2 us
    all_to_all x1, waiting for transfers between devices, local(): arrived = lax.all_to_all(windows, 'facet', 0, 0, tiled=True)  3.41 us
    pallas_call x1, Pallas kernels, local(): call(grid_kernel, [SMEM] + [VMEM] * 6 + [HBM], shape(NF * NB, 2 * RD, M),...  2.75 us
    pallas_call x1, Pallas kernels, local(): call(update_kernel, [VMEM, VMEM, VMEM, HBM, HBM, HBM], shape(2, RD, L //...  2.4 us
    pallas_call x1, Pallas kernels, local(): call(setup_kernel, [VMEM] * 2 + [ANY] * 2 + [HBM] * 6, [shape(2 * SG, NV)...  2.39 us
  transfers between devices with their start and end apart: 5, of which 2 were waited for; matrix products, arithmetic and copies ran while one was open for 0% of the time, Pallas kernels for 8%

profile of v3, /device:TPU:1, one launch (start us, length us, event | category | flops | bytes accessed | tf_op | source)
XLA Modules:
  0.0 58.1 jit_solution(15153068794932557079)
XLA Ops:
  0.0 5.2 %collective-permute-start.2 = (s32[1,2,1,2,256]{4,3,1,2,0:T(2,128)}, s32[1,2,1,2,256]{4,3,1,2,0:T(2,128)S(1)}, u32[]{:S(2)}, u32[]{:S(2)}) collective-permute-start(s32[1,2,1,2,256]{4,3,1,2,0:T(2,128)} %bitcast.14), channel_id=1, source_target_pairs={{0,6},{2,4},{4,2},{6,0},{8,14},{10,12},{12,10},{14,8},{1,7},{3,5},... | collective-permute-start | bytes 12296 | tf_op jit(solution)/shard_map/ppermute | solution.py:459
  5.2 0.0 collective-permute-start.1
  5.2 0.3 collective-permute-start
  5.5 2.4 %windows.1 = (bf16[16,16,128]{2,1,0:T(8,128)(2,1)}, s32[2,32]{1,0:T(2,128)S(1)}, s32[2,16]{1,0:T(2,128)S(1)}, s32[2,2,256]{2,1,0:T(2,128)S(1)}) custom-call(s32[2,32]{1,0:T(2,128)} %bitcast.20, s32[2,16]{1,0:T(2,128)} %bitcast.21, s32[1,2,1,2,256]{4,3,2,1,0:T(2,128)} %cells_h.1, bf16[1,2,8,4096]{3,2,1,0:T(8,128)(2,1)} %rows_h.1, ...), custom_call_target="tpu_custom_call" | custom-call | tf_op jit(solution)/shard_map/windows/pallas_call | solution.py:472
  7.8 0.0 collective-permute-done.2
  7.9 0.9 %collective-permute-done.1 = s32[1,2,1,2,256]{4,3,1,2,0:T(2,128)S(1)} collective-permute-done((s32[1,2,1,2,256]{4,3,1,2,0:T(2,128)}, s32[1,2,1,2,256]{4,3,1,2,0:T(2,128)S(1)}, u32[]{:S(2)}, u32[]{:S(2)}) %collective-permute-start.1) | collective-permute-done | bytes 4128 | tf_op jit(solution)/shard_map/ppermute | solution.py:459
  8.7 0.0 collective-permute-done
  8.8 5.0 %collective-permute-start.3 = (s32[4,2,2,256]{3,2,1,0:T(2,128)S(1)}, s32[4,2,2,256]{3,2,1,0:T(2,128)S(1)}, u32[]{:S(2)}, u32[]{:S(2)}) collective-permute-start(s32[4,2,2,256]{3,2,1,0:T(2,128)S(1)} %pad_add_fusion.near_h), channel_id=1, source_target_pairs={{0,8},{2,10},{4,12},{6,14},{8,0},{10,2},{12,4},{14,6},{1,9},{3,11}... | collective-permute-start | bytes 49160 | tf_op jit(solution)/shard_map/ppermute | solution.py:459
  13.8 7.2 %all-to-all-start = ((bf16[16,16,128]{2,1,0:T(8,128)(2,1)}), bf16[16,16,128]{2,1,0:T(8,128)(2,1)S(1)}, u32[]{:S(2)}, u32[]{:S(2)}) async-start(bf16[16,16,128]{2,1,0:T(8,128)(2,1)} %get-tuple-element.24), calls=%async_computation | async-start | bytes 131072 | tf_op jit(solution)/shard_map/all_to_all | solution.py:499
  21.0 0.0 collective-permute-done.3.far_h
  21.0 2.4 %setup.1 = (bf16[512,2048]{1,0:T(8,128)(2,1)S(1)}, f32[2,16,2048]{2,1,0:T(8,128)S(1)}, f32[2,8,2048]{2,1,0:T(8,128)S(1)}, bf16[512,256]{1,0:T(8,128)(2,1)S(1)}, ...) custom-call(s32[2,32]{1,0:T(2,128)S(1)} %get-tuple-element.21.offs_v, ...), custom_call_target="tpu_custom_call" | custom-call | flops 20000000000 | bytes 4194304 | tf_op jit(solution)/shard_map/setup/pallas_call | solution.py:500
  23.4 0.0 copy-start
  23.4 3.4 %all-to-all-done = bf16[16,16,128]{2,1,0:T(8,128)(2,1)S(1)} async-done(((bf16[16,16,128]{2,1,0:T(8,128)(2,1)}), bf16[16,16,128]{2,1,0:T(8,128)(2,1)S(1)}, u32[]{:S(2)}, u32[]{:S(2)}) %all-to-all-start) | async-done | bytes 65568 | tf_op jit(solution)/shard_map/all_to_all | solution.py:499
  26.8 2.1 %predict.1 = bf16[8,40,128]{2,1,0:T(8,128)(2,1)S(1)} custom-call(bf16[256,128]{1,0:T(8,128)(2,1)S(1)} %bitcast.11, bf16[512,256]{1,0:T(8,128)(2,1)S(1)} %get-tuple-element.29.lift, bf16[256,512]{1,0:T(8,128)(2,1)S(1)} %get-tuple-element.30.k_right, bf16[256,256]{1,0:T(8,128)(2,1)S(1)} %get-tuple-element.31.aterm, ...), custom_call_target="tpu_custom_call" | custom-call | tf_op jit(solution)/shard_map/predict/pallas_call | solution.py:529
  28.9 10.0 %all_to_all.15.parts = bf16[8,40,128]{2,1,0:T(8,128)(2,1)S(1)} all-to-all(bf16[8,40,128]{2,1,0:T(8,128)(2,1)S(1)} %predict.1), channel_id=1, replica_groups=mesh['facet'=16,'team'=8,'sub'=2] {'team'}, dimensions={0} | all-to-all | bytes 163840 | tf_op jit(solution)/shard_map/all_to_all | solution.py:536
  38.9 0.0 copy-done
  38.9 2.7 %grid.1 = bf16[32,16,128]{2,1,0:T(8,128)(2,1)S(1)} custom-call(s32[2,8,16]{2,1,0:T(8,128)S(1)} %bitcast.12, bf16[8,40,128]{2,1,0:T(8,128)(2,1)S(1)} %all_to_all.15.parts, bf16[512,2048]{1,0:T(8,128)(2,1)S(1)} %get-tuple-element.32.col_t, f32[2,16,2048]{2,1,0:T(8,128)S(1)} %get-tuple-element.33.row_base, f32[2,8,2048]{2,1,0:T(8,128)S(1)} %get-tuple-element.34.row_step, ...), custom_call_target="tpu_custom_call" | custom-call | tf_op jit(solution)/shard_map/grid/pallas_call | solution.py:537
  41.7 14.0 %all_to_all.16.folded = bf16[32,16,128]{2,1,0:T(8,128)(2,1)S(1)} all-to-all(bf16[32,16,128]{2,1,0:T(8,128)(2,1)S(1)} %grid.1), channel_id=1, replica_groups=mesh['facet'=16,'team'=8,'sub'=2] {'facet','sub'}, dimensions={0} | all-to-all | bytes 262144 | tf_op jit(solution)/shard_map/all_to_all | solution.py:550
  55.7 2.4 %update.1 = f32[2,8,2048]{2,1,0:T(8,128)} custom-call(s32[2,32]{1,0:T(2,128)S(1)} %get-tuple-element.21.offs_v.offs_h, s32[2,16]{1,0:T(2,128)S(1)} %get-tuple-element.22.foffs_v.foffs_h, bf16[32,16,128]{2,1,0:T(8,128)(2,1)S(1)} %all_to_all.16.folded, bf16[256,64]{1,0:T(8,128)(2,1)} %constant.21.clone.w_rows_h, f32[2,128,128]{2,1,0:T(8,128)} %constant.22.clone.turn_h, ...), custom_call_target="tpu_custom_call" | custom-call | tf_op jit(solution)/shard_map/update/pallas_call | solution.py:551
  (1 shorter events, 0.0 us)
Async XLA Ops:
  0.0 7.8 %collective-permute-start.2 = (s32[1,2,1,2,256]{4,3,1,2,0:T(2,128)}, s32[1,2,1,2,256]{4,3,1,2,0:T(2,128)S(1)}, u32[]{:S(2)}, u32[]{:S(2)}) collective-permute-start(s32[1,2,1,2,256]{4,3,1,2,0:T(2,128)} %bitcast.14), channel_id=1, source_target_pairs={{0,6},{2,4},{4,2},{6,0},{8,14},{10,12},{12,10},{14,8},{1,7},{3,5},... | collective-permute-start | bytes 12296 | tf_op jit(solution)/shard_map/ppermute | solution.py:459
  5.2 3.6 %collective-permute-start.1 = (s32[1,2,1,2,256]{4,3,1,2,0:T(2,128)}, s32[1,2,1,2,256]{4,3,1,2,0:T(2,128)S(1)}, u32[]{:S(2)}, u32[]{:S(2)}) collective-permute-start(s32[1,2,1,2,256]{4,3,1,2,0:T(2,128)} %bitcast.15), channel_id=1, source_target_pairs={{0,4},{2,6},{4,0},{6,2},{8,12},{10,14},{12,8},{14,10},{1,5},{3,7},... | collective-permute-start | bytes 12296 | tf_op jit(solution)/shard_map/ppermute | solution.py:459
  5.2 3.6 %collective-permute-start = (s32[1,2,1,2,256]{4,3,1,2,0:T(2,128)}, s32[1,2,1,2,256]{4,3,1,2,0:T(2,128)S(1)}, u32[]{:S(2)}, u32[]{:S(2)}) collective-permute-start(s32[1,2,1,2,256]{4,3,1,2,0:T(2,128)} %bitcast.16), channel_id=1, source_target_pairs={{0,2},{2,0},{4,6},{6,4},{8,10},{10,8},{12,14},{14,12},{1,3},{3,1},... | collective-permute-start | bytes 12296 | tf_op jit(solution)/shard_map/ppermute | solution.py:459
  8.8 12.2 %collective-permute-start.3 = (s32[4,2,2,256]{3,2,1,0:T(2,128)S(1)}, s32[4,2,2,256]{3,2,1,0:T(2,128)S(1)}, u32[]{:S(2)}, u32[]{:S(2)}) collective-permute-start(s32[4,2,2,256]{3,2,1,0:T(2,128)S(1)} %pad_add_fusion.near_h), channel_id=1, source_target_pairs={{0,8},{2,10},{4,12},{6,14},{8,0},{10,2},{12,4},{14,6},{1,9},{3,11}... | collective-permute-start | bytes 49160 | tf_op jit(solution)/shard_map/ppermute | solution.py:459
  13.8 13.0 %all-to-all-start = ((bf16[16,16,128]{2,1,0:T(8,128)(2,1)}), bf16[16,16,128]{2,1,0:T(8,128)(2,1)S(1)}, u32[]{:S(2)}, u32[]{:S(2)}) async-start(bf16[16,16,128]{2,1,0:T(8,128)(2,1)} %get-tuple-element.24), calls=%async_computation | async-start | bytes 131072 | tf_op jit(solution)/shard_map/all_to_all | solution.py:499
  23.4 15.5 %copy-start = (s32[16,2,8]{0,2,1:T(8,128)S(1)}, s32[16,2,8]{0,2,1:T(8,128)}, u32[]{:S(2)}) copy-start(s32[16,2,8]{0,2,1:T(8,128)} %param.25) | copy-start | bytes 3076

commit v4 on v3

v4 whole, which is shorter than its diff:
```python
import math

import jax
import jax.numpy as jnp
import numpy as np
from jax import lax
from jax.experimental import pallas as pl
from jax.experimental.pallas import tpu as pltpu
from jax.sharding import PartitionSpec as P

L = 4096
M = 128
SG = 256
VB = 256
R = 64
NF = 16
NT = 8
NB = 2
RD = R // NT
NH = L // M
NV = NT * VB
TWO_PI = 2.0 * math.pi
BF = jnp.bfloat16
F32 = jnp.float32

ROOT = np.exp(2j * np.pi * np.arange(L) / L)


def wave(left, right, period, sign):
    steps = (np.outer(left, right) % period) * (L // period)
    table = ROOT[steps]
    return table if sign > 0 else table.conj()


def as_real(matrix):
    return np.block([[matrix.real, -matrix.imag], [matrix.imag, matrix.real]])


def half(matrix):
    return jnp.asarray(np.asarray(matrix, np.float32), BF)


def tables():
    lanes = np.arange(M)
    highs = np.arange(NH)
    fwd_rows = as_real(wave(lanes, highs, NH, -1))
    fwd_turn = wave(lanes, lanes, L, -1)
    bwd_turn = wave(lanes, lanes, L, 1) / math.sqrt(M)
    bwd_full = wave(highs, lanes, NH, 1)
    bwd_high = np.stack([as_real(part) for part in np.split(bwd_full, NB)])
    k_table = wave(lanes, np.arange(SG), SG, 1) / math.sqrt(M)
    k_left = as_real(k_table.T)
    return {
        "fwd_rows": half(fwd_rows),
        "fwd_turn": jnp.asarray(np.stack([fwd_turn.real, fwd_turn.imag]), F32),
        "bwd_turn": jnp.asarray(np.stack([bwd_turn.real, bwd_turn.imag]), F32),
        "bwd_high": half(bwd_high),
        "k_left": half(k_left),
    }


COS_TERMS = [(-1.0) ** n / math.factorial(2 * n) for n in range(9)]
SIN_TERMS = [(-1.0) ** n / math.factorial(2 * n + 1) for n in range(8)]


def turn_angle(steps, period):
    steps = steps & (period - 1)
    steps = jnp.where(steps >= period // 2, steps - period, steps)
    return steps.astype(F32) * (TWO_PI / period)


def series(square, terms):
    total = jnp.full_like(square, terms[-1])
    for term in terms[-2::-1]:
        total = total * square + term
    return total


def cos_of(angle):
    return series(angle * angle, COS_TERMS)


def sin_of(angle):
    return angle * series(angle * angle, SIN_TERMS)


def dot(left, right):
    return jnp.dot(left, right, preferred_element_type=F32)


def dot_tn(left, right):
    return lax.dot_general(left, right, (((0,), (0,)), ((), ())), preferred_element_type=F32)


def dot_nt(left, right):
    return lax.dot_general(left, right, (((1,), (1,)), ((), ())), preferred_element_type=F32)


def fetch(pairs, sems):
    copies = []
    for at, (source, target) in enumerate(pairs):
        copy = pltpu.make_async_copy(source, target, sems.at[at])
        copy.start()
        copies.append(copy)
    return copies


def forward_kernel(
    offs_h, foffs_h, cells_h, rows_h, w_rows_h, turn_h,
    out, offs_v, foffs_v, cells_v, offs, rows, w_rows, turn, xs, xo, sems,
):
    side = lax.axis_index("sub")
    copies = fetch(
        [
            (offs_h, offs),
            (rows_h.at[0], rows),
            (w_rows_h, w_rows),
            (turn_h, turn),
            (offs_h, offs_v),
            (foffs_h, foffs_v),
            (cells_h.at[0, :, 0], cells_v),
        ],
        sems,
    )
    for copy in copies:
        copy.wait()
    row = lax.broadcasted_iota(jnp.int32, (NF, 2 * M), 0)
    lane = lax.broadcasted_iota(jnp.int32, (NF, 2 * M), 1)
    tuning = jnp.zeros((NF, 2 * M), jnp.int32)
    for a in range(NF):
        tuning = jnp.where(row == a, offs[1, a * NB + side], tuning)
    pick = lane[:, :M] >= (tuning[:, :M] & (M - 1))
    first = (tuning >> 7) * (lane & (M - 1))
    later = lane & (M - 1)
    blocks = []
    for part in range(2):
        for late in range(2):
            steps = (L // NH) * (first + late * later) + (L // 4) * (part - (lane >> 7))
            blocks.append((cos_of(turn_angle(steps, L)) * (1.0 / 64.0)).astype(BF))
    w_high = jnp.concatenate(blocks, 0)
    for part in range(2):
        whole = rows[part].astype(F32)
        for high in range(NH):
            xs[pl.ds((part * NH + high) * RD, RD), :] = whole[:, high * M : (high + 1) * M]
    stacked = jnp.concatenate(
        [xs[pl.ds(r, 2 * NH, stride=RD), :].astype(BF) for r in range(RD)], 1
    )
    mixed = dot(w_rows[...], stacked)
    t_re = turn[0]
    t_im = turn[1]
    for r in range(RD):
        y_re = mixed[:M, r * M : (r + 1) * M]
        y_im = mixed[M:, r * M : (r + 1) * M]
        z_re = (y_re * t_re - y_im * t_im).astype(BF)
        z_im = (y_re * t_im + y_im * t_re).astype(BF)
        found = dot_nt(w_high, jnp.concatenate([z_re, z_im], 1))
        for part in range(2):
            at = part * 2 * NF
            value = jnp.where(pick, found[at : at + NF], found[at + NF : at + 2 * NF])
            xo[pl.ds(part * RD + r, NF, stride=2 * RD), :] = value
    for a in range(NF):
        out[a] = xo[a * 2 * RD : (a + 1) * 2 * RD, :].astype(BF)


SENT = 40
OBS = 2 * NV // M
HEIGHT = 16
STEPS = SG // HEIGHT


def setup_kernel(
    offs_v, foffs_v, near_h, far_h, k_left_h, aterm_h, seen_h, weights_h, counts_h, turn_h, w_high_h,
    col_t, row_fac, lift, k_right, aterm, tail, phase, w_rows, picks, turn, w_high,
    offs, foffs, counts, near, far, k_left, spots, seen, weights, sems,
):
    facet = lax.axis_index("facet")
    team = lax.axis_index("team")
    side = lax.axis_index("sub")
    copies = fetch(
        [
            (offs_v, offs),
            (foffs_v, foffs),
            (k_left_h, k_left),
            (near_h.at[:, side], near),
            (far_h.at[:, side], far),
            (aterm_h.at[0, side], aterm),
            (seen_h.at[0, side, 0], seen),
            (weights_h.at[0, 0], weights),
            (counts_h, counts),
            (turn_h, turn),
            (w_high_h.at[side], w_high),
        ],
        sems,
    )
    for copy in copies[:2]:
        copy.wait()
    shift_u = offs[0, facet * NB + side]
    row = lax.broadcasted_iota(jnp.int32, (2 * RD, 2 * M), 0)
    lane = lax.broadcasted_iota(jnp.int32, (2 * RD, 2 * M), 1)
    p = lane & (M - 1)
    quarter = ((row >> 3) - (lane >> 7)) * (L // 4)
    row_turn = (L // R) * (p + shift_u) * (team * RD + (row & (RD - 1)))
    base = quarter - row_turn
    blocks = []
    for f in range(NF):
        steps = base + p * foffs[0, f]
        blocks.append((cos_of(turn_angle(steps, L)) * (1.0 / 32.0)).astype(BF))
    joined = jnp.concatenate(blocks, 0)
    own = offs[1, facet * NB + side]
    row = lax.broadcasted_iota(jnp.int32, (NF, M), 0)
    lane = lax.broadcasted_iota(jnp.int32, (NF, M), 1)
    column = jnp.zeros((NF, M), jnp.int32)
    for f in range(NF):
        column = jnp.where(row == f, foffs[1, f], column)
    angle = turn_angle(column * ((lane - own) & (M - 1)), L)
    phase[0] = cos_of(angle)
    phase[1] = sin_of(angle)
    row = lax.broadcasted_iota(jnp.int32, (M, SG), 0)
    lane = lax.broadcasted_iota(jnp.int32, (M, SG), 1)
    angle = turn_angle(((row - own) & (M - 1)) * lane, SG)
    k_re = (cos_of(angle) * (1.0 / math.sqrt(M))).astype(BF)
    k_im = (sin_of(angle) * (1.0 / math.sqrt(M))).astype(BF)
    k_right[:M, :SG] = k_re
    k_right[:M, SG:] = k_im
    k_right[M:, :SG] = -k_im
    k_right[M:, SG:] = k_re
    lane = lax.broadcasted_iota(jnp.int32, (8, M), 1)
    row = lax.broadcasted_iota(jnp.int32, (NF * NB, M), 0)
    high = jnp.zeros((8, M), jnp.int32)
    low = jnp.zeros((NF * NB, M), jnp.int32)
    for s in range(NF * NB):
        high = jnp.where((lane & (NF * NB - 1)) == s, offs[1, s] >> 7, high)
        low = jnp.where(row == s, offs[1, s] & (M - 1), low)
    lane_rows = lax.broadcasted_iota(jnp.int32, (NF * NB, M), 1)
    picks[...] = jnp.where(lane_rows >= low, 1.0, 0.0)
    high = high + ((lane >> 5) & 1)
    quarter = (lane >> 6) * (L // 4)
    high = jnp.concatenate([high] * 4, 0)
    quarter = jnp.concatenate([quarter] * 4, 0)
    for block in range(2 * M // 32):
        spot = lax.broadcasted_iota(jnp.int32, (32, M), 0) + block * 32
        steps = (L // NH) * (spot & (M - 1)) * high + quarter - (spot >> 7) * (L // 4)
        w_rows[block * 32 : (block + 1) * 32, :] = cos_of(turn_angle(steps, L)).astype(BF)
    for copy in copies[2:]:
        copy.wait()
    lift[...] = dot_nt(k_left[...], joined).astype(BF)
    pair = weights[...].astype(F32)
    weight = jnp.where(side == 0, pair[0:1], pair[1:2])
    slot = lax.broadcasted_iota(jnp.int32, (1, VB), 1)
    weight = jnp.where(slot < counts[side, team, facet], weight, 0.0)
    both = seen[...].astype(F32)
    tail[...] = jnp.zeros_like(tail)
    for at in range(2):
        half = slice(at * M, (at + 1) * M)
        tail[at : at + 1, :] = both[0:1, half]
        tail[2 + at : 3 + at, :] = both[1:2, half]
        tail[4 + at : 5 + at, :] = weight[:, half]
    for step in range(NT // 2):
        spots[team ^ step] = near[step]
        spots[team ^ (step + NT // 2)] = far[step]
    count = lax.broadcasted_iota(jnp.int32, (8, M), 0)

    def turns(place, tile):
        half = slice(tile % 2 * M, (tile % 2 + 1) * M)
        spot = jnp.broadcast_to(spots[tile // 2, place : place + 1, half], (8, M))
        angle = turn_angle(spot * count, 4 * SG)
        step = turn_angle(spot * 8, 4 * SG)
        return cos_of(angle), sin_of(angle), cos_of(step), sin_of(step)

    for tile in range(NV // M):
        lanes = slice(tile * M, (tile + 1) * M)
        cos, sin, step_cos, step_sin = turns(0, tile)
        row_fac[0:8, lanes] = cos
        row_fac[8:16, lanes] = sin
        row_fac[16:17, lanes] = step_cos[0:1]
        row_fac[17:18, lanes] = step_sin[0:1]
        cos, sin, step_cos, step_sin = widen(*turns(1, tile))
        for block in range(STEPS):
            at = block * HEIGHT
            col_t[at : at + HEIGHT, lanes] = cos.astype(BF)
            col_t[SG + at : SG + at + HEIGHT, lanes] = sin.astype(BF)
            if block + 1 < STEPS:
                cos, sin = cos * step_cos - sin * step_sin, cos * step_sin + sin * step_cos


def widen(cos, sin, step_cos, step_sin):
    far_cos = cos * step_cos - sin * step_sin
    far_sin = cos * step_sin + sin * step_cos
    twice_cos = step_cos * step_cos - step_sin * step_sin
    twice_sin = 2.0 * step_cos * step_sin
    return (
        jnp.concatenate([cos, far_cos], 0),
        jnp.concatenate([sin, far_sin], 0),
        twice(twice_cos),
        twice(twice_sin),
    )


def row_factors(row_fac, span):
    width = span.stop - span.start
    return widen(
        row_fac[0:8, span],
        row_fac[8:16, span],
        jnp.broadcast_to(row_fac[16:17, span], (8, width)),
        jnp.broadcast_to(row_fac[17:18, span], (8, width)),
    )


def twice(value):
    return jnp.concatenate([value, value], 0)


def predict_kernel(
    spec, lift, k_right, aterm, col_t, row_fac, tail, phase, out, rows_out
):
    parts = []
    for f in range(NF):
        both = spec[f].astype(F32)
        cos = phase[0, f : f + 1, :]
        sin = phase[1, f : f + 1, :]
        parts.append(both[:RD] * cos - both[RD:] * sin)
        parts.append(both[:RD] * sin + both[RD:] * cos)
    turned = dot(lift[...], jnp.concatenate(parts, 0).astype(BF)).astype(BF)
    image = dot(jnp.concatenate([turned[:SG], turned[SG:]], 1), k_right[...])
    weight = aterm[...].astype(F32)
    w_re = image[:, :SG] * weight
    w_im = image[:, SG:] * weight
    left = jnp.concatenate(
        [
            jnp.concatenate([w_re, w_im], 1).astype(BF),
            jnp.concatenate([w_im, -w_re], 1).astype(BF),
        ],
        0,
    )
    for chunk in range(NT):
        span = slice(chunk * VB, (chunk + 1) * VB)
        z = dot(left, col_t[:, span])
        cos, sin, step_cos, step_sin = row_factors(row_fac, span)
        re = z[SG - HEIGHT : SG]
        im = z[2 * SG - HEIGHT :]
        for block in range(STEPS - 2, -1, -1):
            at = block * HEIGHT
            re, im = (
                re * step_cos + im * step_sin + z[at : at + HEIGHT],
                im * step_cos - re * step_sin + z[SG + at : SG + at + HEIGHT],
            )
        re, im = re * cos + im * sin, im * cos - re * sin
        re = jnp.sum(re, 0, keepdims=True) * (1.0 / SG)
        im = jnp.sum(im, 0, keepdims=True) * (1.0 / SG)
        for tile in range(VB // M):
            at = chunk * (VB // M) + tile
            rows_out[at : at + 1, :] = re[:, tile * M : (tile + 1) * M]
            rows_out[NV // M + at : NV // M + at + 1, :] = im[:, tile * M : (tile + 1) * M]
    rows_out[OBS:, :] = tail[...]
    packed = rows_out[...].astype(BF)
    for peer in range(NT):
        out[peer] = packed


def grid_kernel(
    parts, col_t, row_fac, aterm, lift, k_right, phase, out, spread, res, slots
):
    part = parts[0].astype(F32)
    total = part[:OBS]
    slots[0] = part[OBS:]
    for peer in range(1, NT):
        part = parts[peer].astype(F32)
        total = total + part[:OBS]
        slots[peer] = part[OBS:]
    res[...] = total
    for tile in range(NV // M):
        t = tile // 2
        h = tile % 2
        weight = slots[t, 4 + h : 5 + h, :]
        r_re = weight * (slots[t, h : 1 + h, :] - res[tile : tile + 1, :])
        r_im = weight * (slots[t, 2 + h : 3 + h, :] - res[NV // M + tile : NV // M + tile + 1, :])
        span = slice(tile * M, (tile + 1) * M)
        cos, sin, step_cos, step_sin = row_factors(row_fac, span)
        re, im = r_re * cos - r_im * sin, r_re * sin + r_im * cos
        for block in range(STEPS):
            at = block * HEIGHT
            spread[at : at + HEIGHT, span] = re.astype(BF)
            spread[SG + at : SG + at + HEIGHT, span] = im.astype(BF)
            if block + 1 < STEPS:
                re, im = re * step_cos - im * step_sin, re * step_sin + im * step_cos
    both = dot_nt(spread[...], col_t[...])
    weight = aterm[...].astype(F32) * (1.0 / SG)
    g_re = (both[:SG, :SG] - both[SG:, SG:]) * weight
    g_im = (both[:SG, SG:] + both[SG:, :SG]) * weight
    grid = jnp.concatenate([g_re, g_im], 0).astype(BF)
    low = dot_tn(lift[...], grid).astype(BF)
    back = dot_nt(low, k_right[:, :SG])
    for f in range(NF):
        top = back[f * 16 : f * 16 + 8]
        bot = back[f * 16 + 8 : f * 16 + 16]
        re = top[:, :M] - bot[:, M:]
        im = bot[:, :M] + top[:, M:]
        cos = phase[0, f : f + 1, :]
        sin = phase[1, f : f + 1, :]
        both_parts = jnp.concatenate([re * cos + im * sin, im * cos - re * sin], 0).astype(BF)
        for b in range(NB):
            out[f * NB + b] = both_parts


def update_kernel(folded, w_rows, picks, turn, w_high, out, fs, os):
    count = NF * NB
    for s in range(count):
        fs[s * 2 * RD : (s + 1) * 2 * RD, :] = folded[s].astype(F32)
    mask = picks[...]
    columns = []
    for r in range(RD):
        pieces = []
        for part in range(2):
            value = fs[pl.ds(part * RD + r, count, stride=2 * RD), :]
            early = value * mask
            pieces.append(early)
            pieces.append(value - early)
        columns.append(jnp.concatenate(pieces, 0).astype(BF))
    stacked = jnp.concatenate(columns, 1)
    mixed = dot(w_rows[...], stacked)
    t_re = turn[0]
    t_im = turn[1]
    high = w_high[...]
    n_out = NH // NB
    for r in range(RD):
        y_re = mixed[:M, r * M : (r + 1) * M]
        y_im = mixed[M:, r * M : (r + 1) * M]
        z_re = (y_re * t_re - y_im * t_im).astype(BF)
        z_im = (y_re * t_im + y_im * t_re).astype(BF)
        os[pl.ds(r, 2 * n_out, stride=RD), :] = dot_nt(high, jnp.concatenate([z_re, z_im], 1))
    for part in range(2):
        for h in range(n_out):
            at = (part * n_out + h) * RD
            out[part, :, h * M : (h + 1) * M] = os[at : at + RD, :]


def shape(*dims, dtype=BF):
    return jax.ShapeDtypeStruct(dims, dtype)


SMEM = pl.BlockSpec(memory_space=pltpu.SMEM)
VMEM = pl.BlockSpec(memory_space=pltpu.VMEM)
HBM = pl.BlockSpec(memory_space=pltpu.HBM)
ANY = pl.BlockSpec(memory_space=pl.ANY)
PARAMS = pltpu.CompilerParams(vmem_limit_bytes=24 * 2**20)


def buf(*dims, dtype=BF):
    return pltpu.VMEM(dims, dtype)


def smem(*dims):
    return pltpu.SMEM(dims, jnp.int32)


def sems(count):
    return pltpu.SemaphoreType.DMA((count,))


def call(kernel, specs, outs, scratch, name, places=None, cost=None):
    single = not isinstance(outs, (list, tuple))
    return pl.pallas_call(
        kernel,
        out_shape=outs,
        in_specs=specs,
        out_specs=places or (VMEM if single else [VMEM] * len(outs)),
        scratch_shapes=scratch,
        compiler_params=PARAMS,
        cost_estimate=cost,
        name=name,
    )


def partner(value, mask):
    pairs = [(source, source ^ mask) for source in range(NT)]
    return lax.ppermute(value, "team", pairs)


def local(facet_rows, sub_offsets, facet_offsets, aterm, cells, observed, weights, counts):
    t = tables()
    offs = sub_offsets.T
    foffs = facet_offsets.T
    live = counts.transpose(1, 2, 0)
    keep = lambda array: pltpu.with_memory_space_constraint(array, pltpu.HBM)
    offs = keep(offs)
    foffs = keep(foffs)
    ids = [smem(2, NF * NB), smem(2, NF)]
    others = [partner(cells, mask) for mask in (1, 2, 3)]
    windows, offs_v, foffs_v, cells_v = call(
        forward_kernel,
        [HBM] * 6,
        [
            shape(NF, 2 * RD, M),
            shape(2, NF * NB, dtype=jnp.int32),
            shape(2, NF, dtype=jnp.int32),
            shape(NB, 2, VB, dtype=jnp.int32),
        ],
        [
            smem(2, NF * NB),
            buf(2, RD, L),
            buf(2 * M, 2 * NH),
            buf(2, M, M, dtype=F32),
            buf(2 * NH * RD, M, dtype=F32),
            buf(NF * 2 * RD, M, dtype=F32),
            sems(7),
        ],
        "windows",
    )(
        offs, foffs, keep(cells), keep(facet_rows),
        keep(t["fwd_rows"]), keep(t["fwd_turn"]),
    )
    *others, windows = lax.optimization_barrier((*others, windows))
    near = jnp.stack([part.reshape(NB, 2, VB) for part in [cells_v] + others])
    far = partner(near, NT // 2)
    arrived = lax.all_to_all(windows, "facet", 0, 0, tiled=True)
    col_t, row_fac, lift, k_right, own_map, tail, phase, w_rows, picks, turn, w_high = call(
        setup_kernel,
        [VMEM] * 2 + [ANY] * 2 + [HBM] * 7,
        [
            shape(2 * SG, NV),
            shape(24, NV, dtype=F32),
            shape(2 * SG, 2 * M),
            shape(2 * M, 2 * SG),
            shape(SG, SG),
            shape(SENT - OBS, M, dtype=F32),
            shape(2, NF, M, dtype=F32),
            shape(2 * M, 4 * NF * NB),
            shape(NF * NB, M, dtype=F32),
            shape(2, M, M, dtype=F32),
            shape(NH, 2 * M),
        ],
        ids
        + [smem(NB, NT, NF)]
        + [buf(NT // 2, 2, VB, dtype=jnp.int32)] * 2
        + [
            buf(2 * SG, 2 * M),
            buf(NT, 2, VB, dtype=jnp.int32),
            buf(2, VB),
            buf(2, VB),
            sems(11),
        ],
        "setup",
        cost=pl.CostEstimate(flops=20 * 10**9, transcendentals=0, bytes_accessed=2**22),
    )(
        offs_v, foffs_v, near, far, keep(t["k_left"]),
        keep(aterm), keep(observed), keep(weights.transpose(0, 2, 1, 3)),
        keep(live), keep(t["bwd_turn"]), keep(t["bwd_high"]),
    )
    parts = call(
        predict_kernel,
        [VMEM] * 8,
        shape(NT, SENT, M),
        [buf(SENT, M, dtype=F32)],
        "predict",
    )(arrived, lift, k_right, own_map, col_t, row_fac, tail, phase)
    gathered = lax.all_to_all(parts, "team", 0, 0, tiled=True)
    folded = call(
        grid_kernel,
        [VMEM] * 7,
        shape(NF * NB, 2 * RD, M),
        [
            buf(2 * SG, NV),
            buf(OBS, M, dtype=F32),
            buf(NT, SENT - OBS, M, dtype=F32),
        ],
        "grid",
    )(gathered, col_t, row_fac, own_map, lift, k_right, phase)
    returned = lax.all_to_all(folded, ("facet", "sub"), 0, 0, tiled=True)
    update = call(
        update_kernel,
        [VMEM] * 5,
        shape(2, RD, L // NB, dtype=F32),
        [buf(NF * NB * 2 * RD, M, dtype=F32), buf(NH * RD, M, dtype=F32)],
        "update",
    )(returned, w_rows, picks, turn, w_high)
    return update[None]


def solution(mesh):
    placed = (
        P("facet", None, "team", None),
        P(),
        P(),
        P("facet", None, None, None),
        P("facet", None, "team", None, None),
        P("facet", None, "team", None, None),
        P("facet", None, "team", None),
        P(),
    )
    return jax.shard_map(
        local,
        mesh=mesh,
        in_specs=placed,
        out_specs=P("facet", None, "team", "sub"),
        check_vma=False,
    )
```

time: 58.3 us -> 56.1 us (0.962)
  Pallas kernels: 12 us -> 9.68 us
    pallas_call x4, Pallas kernels: 9.92 us -> 7.64 us  [the longest x1 2.28 us: local(): call(setup_kernel, [VMEM] * 2 + [ANY] * 2 + [HBM] * 7, [shape(2 * SG, NV)...]
where the time goes in v4:
time: 56.1 us; the launch traced here: 55.9 us
  blocking collectives  24 us (43%)
  starting transfers between devices  17.6 us (31%)
  Pallas kernels  9.68 us (17%)
  waiting for transfers between devices  4.54 us (8%)
    all_to_all x1, blocking collectives, local(): returned = lax.all_to_all(folded, ('facet', 'sub'), 0, 0, tiled=True)  14 us
    ppermute x4, starting transfers between devices, partner(): return lax.ppermute(value, 'team', pairs)  10.4 us
    all_to_all x1, blocking collectives, local(): gathered = lax.all_to_all(parts, 'team', 0, 0, tiled=True)  10 us
    all_to_all x1, starting transfers between devices, local(): arrived = lax.all_to_all(windows, 'facet', 0, 0, tiled=True)  7.21 us
    all_to_all x1, waiting for transfers between devices, local(): arrived = lax.all_to_all(windows, 'facet', 0, 0, tiled=True)  3.53 us
    pallas_call x1, Pallas kernels, local(): call(setup_kernel, [VMEM] * 2 + [ANY] * 2 + [HBM] * 7, [shape(2 * SG, NV)...  2.28 us
    pallas_call x1, Pallas kernels, local(): call(forward_kernel, [HBM] * 6, [shape(NF, 2 * RD, M), shape(2, NF * NB,...  2.26 us
    pallas_call x1, Pallas kernels, local(): call(predict_kernel, [VMEM] * 8, shape(NT, SENT, M), [buf(SENT, M, dtype=...  2.05 us
  transfers between devices with their start and end apart: 5, of which 2 were waited for; matrix products, arithmetic and copies ran while one was open for 0% of the time, Pallas kernels for 8%

profile of v4, /device:TPU:1, one launch (start us, length us, event | category | flops | bytes accessed | tf_op | source)
XLA Modules:
  0.0 55.9 jit_solution(13575778681549727923)
XLA Ops:
  0.0 5.2 %collective-permute-start.2 = (s32[1,2,1,2,256]{4,3,1,2,0:T(2,128)}, s32[1,2,1,2,256]{4,3,1,2,0:T(2,128)S(1)}, u32[]{:S(2)}, u32[]{:S(2)}) collective-permute-start(s32[1,2,1,2,256]{4,3,1,2,0:T(2,128)} %bitcast.14), channel_id=1, source_target_pairs={{0,6},{2,4},{4,2},{6,0},{8,14},{10,12},{12,10},{14,8},{1,7},{3,5},... | collective-permute-start | bytes 12296 | tf_op jit(solution)/shard_map/ppermute | solution.py:476
  5.2 0.0 collective-permute-start.1
  5.2 0.3 collective-permute-start
  5.5 2.3 %windows.1 = (bf16[16,16,128]{2,1,0:T(8,128)(2,1)}, s32[2,32]{1,0:T(2,128)S(1)}, s32[2,16]{1,0:T(2,128)S(1)}, s32[2,2,256]{2,1,0:T(2,128)S(1)}) custom-call(s32[2,32]{1,0:T(2,128)} %bitcast.17, s32[2,16]{1,0:T(2,128)} %bitcast.18, s32[1,2,1,2,256]{4,3,2,1,0:T(2,128)} %cells_h.1, bf16[1,2,8,4096]{3,2,1,0:T(8,128)(2,1)} %rows_h.1, ...), custom_call_target="tpu_custom_call" | custom-call | tf_op jit(solution)/shard_map/windows/pallas_call | solution.py:489
  7.7 0.0 collective-permute-done.2
  7.7 1.0 %collective-permute-done.1 = s32[1,2,1,2,256]{4,3,1,2,0:T(2,128)S(1)} collective-permute-done((s32[1,2,1,2,256]{4,3,1,2,0:T(2,128)}, s32[1,2,1,2,256]{4,3,1,2,0:T(2,128)S(1)}, u32[]{:S(2)}, u32[]{:S(2)}) %collective-permute-start.1) | collective-permute-done | bytes 4128 | tf_op jit(solution)/shard_map/ppermute | solution.py:476
  8.7 0.0 collective-permute-done
  8.8 4.9 %collective-permute-start.3 = (s32[4,2,2,256]{3,2,1,0:T(2,128)S(1)}, s32[4,2,2,256]{3,2,1,0:T(2,128)S(1)}, u32[]{:S(2)}, u32[]{:S(2)}) collective-permute-start(s32[4,2,2,256]{3,2,1,0:T(2,128)S(1)} %pad_add_fusion.near_h), channel_id=1, source_target_pairs={{0,8},{2,10},{4,12},{6,14},{8,0},{10,2},{12,4},{14,6},{1,9},{3,11}... | collective-permute-start | bytes 49160 | tf_op jit(solution)/shard_map/ppermute | solution.py:476
  13.7 7.2 %all-to-all-start = ((bf16[16,16,128]{2,1,0:T(8,128)(2,1)}), bf16[16,16,128]{2,1,0:T(8,128)(2,1)S(1)}, u32[]{:S(2)}, u32[]{:S(2)}) async-start(bf16[16,16,128]{2,1,0:T(8,128)(2,1)} %get-tuple-element.25), calls=%async_computation | async-start | bytes 131072 | tf_op jit(solution)/shard_map/all_to_all | solution.py:515
  20.9 0.0 collective-permute-done.3.far_h
  20.9 2.3 %setup.1 = (bf16[512,2048]{1,0:T(8,128)(2,1)S(1)}, f32[24,2048]{1,0:T(8,128)S(1)}, bf16[512,256]{1,0:T(8,128)(2,1)S(1)}, bf16[256,512]{1,0:T(8,128)(2,1)S(1)}, b...) custom-call(s32[2,32]{1,0:T(2,128)S(1)} %get-tuple-element.26.offs_v, ...), custom_call_target="tpu_custom_call" | custom-call | flops 20000000000 | bytes 4194304 | tf_op jit(solution)/shard_map/setup/pallas_call | solution.py:516
  23.2 3.5 %all-to-all-done.spec = bf16[16,16,128]{2,1,0:T(8,128)(2,1)S(1)} async-done(((bf16[16,16,128]{2,1,0:T(8,128)(2,1)}), bf16[16,16,128]{2,1,0:T(8,128)(2,1)S(1)}, u32[]{:S(2)}, u32[]{:S(2)}) %all-to-all-start) | async-done | bytes 65568 | tf_op jit(solution)/shard_map/all_to_all | solution.py:515
  26.7 2.0 %predict.1 = bf16[8,40,128]{2,1,0:T(8,128)(2,1)S(1)} custom-call(bf16[16,16,128]{2,1,0:T(8,128)(2,1)S(1)} %all-to-all-done.spec, bf16[512,256]{1,0:T(8,128)(2,1)S(1)} %get-tuple-element.32.lift, bf16[256,512]{1,0:T(8,128)(2,1)S(1)} %get-tuple-element.33.k_right, bf16[256,256]{1,0:T(8,128)(2,1)S(1)} %get-tuple-element.34.aterm, ...), custom_call_target="tpu_custom_call" | custom-call | tf_op jit(solution)/shard_map/predict/pallas_call | solution.py:549
  28.8 10.0 %all_to_all.15.parts = bf16[8,40,128]{2,1,0:T(8,128)(2,1)S(1)} all-to-all(bf16[8,40,128]{2,1,0:T(8,128)(2,1)S(1)} %predict.1), channel_id=1, replica_groups=mesh['facet'=16,'team'=8,'sub'=2] {'team'}, dimensions={0} | all-to-all | bytes 163840 | tf_op jit(solution)/shard_map/all_to_all | solution.py:556
  38.8 1.9 %grid.1 = bf16[32,16,128]{2,1,0:T(8,128)(2,1)S(1)} custom-call(bf16[8,40,128]{2,1,0:T(8,128)(2,1)S(1)} %all_to_all.15.parts, bf16[512,2048]{1,0:T(8,128)(2,1)S(1)} %get-tuple-element.35.col_t, f32[24,2048]{1,0:T(8,128)S(1)} %get-tuple-element.36.row_fac, bf16[256,256]{1,0:T(8,128)(2,1)S(1)} %get-tuple-element.34.aterm, ...), custom_call_target="tpu_custom_call" | custom-call | tf_op jit(solution)/shard_map/grid/pallas_call | solution.py:557
  40.7 14.0 %all_to_all.16.folded = bf16[32,16,128]{2,1,0:T(8,128)(2,1)S(1)} all-to-all(bf16[32,16,128]{2,1,0:T(8,128)(2,1)S(1)} %grid.1), channel_id=1, replica_groups=mesh['facet'=16,'team'=8,'sub'=2] {'facet','sub'}, dimensions={0} | all-to-all | bytes 262144 | tf_op jit(solution)/shard_map/all_to_all | solution.py:568
  54.7 1.2 %update.1 = f32[2,8,2048]{2,1,0:T(8,128)} custom-call(bf16[32,16,128]{2,1,0:T(8,128)(2,1)S(1)} %all_to_all.16.folded, bf16[256,128]{1,0:T(8,128)(2,1)S(1)} %get-tuple-element.39.w_rows, f32[32,128]{1,0:T(8,128)S(1)} %get-tuple-element.40.picks, f32[2,128,128]{2,1,0:T(8,128)S(1)} %get-tuple-element.41.turn, bf16[32,256]{1,0:T(8,128)(2,1)S(1)} %get-tuple-element.42.w_high), custom_call_target="tpu_custom_call" | custom-call | tf_op jit(solution)/shard_map/update/pallas_call | solution.py:569
  (1 shorter events, 0.0 us)
Async XLA Ops:
  0.0 7.7 %collective-permute-start.2 = (s32[1,2,1,2,256]{4,3,1,2,0:T(2,128)}, s32[1,2,1,2,256]{4,3,1,2,0:T(2,128)S(1)}, u32[]{:S(2)}, u32[]{:S(2)}) collective-permute-start(s32[1,2,1,2,256]{4,3,1,2,0:T(2,128)} %bitcast.14), channel_id=1, source_target_pairs={{0,6},{2,4},{4,2},{6,0},{8,14},{10,12},{12,10},{14,8},{1,7},{3,5},... | collective-permute-start | bytes 12296 | tf_op jit(solution)/shard_map/ppermute | solution.py:476
  5.2 3.6 %collective-permute-start.1 = (s32[1,2,1,2,256]{4,3,1,2,0:T(2,128)}, s32[1,2,1,2,256]{4,3,1,2,0:T(2,128)S(1)}, u32[]{:S(2)}, u32[]{:S(2)}) collective-permute-start(s32[1,2,1,2,256]{4,3,1,2,0:T(2,128)} %bitcast.15), channel_id=1, source_target_pairs={{0,4},{2,6},{4,0},{6,2},{8,12},{10,14},{12,8},{14,10},{1,5},{3,7},... | collective-permute-start | bytes 12296 | tf_op jit(solution)/shard_map/ppermute | solution.py:476
  5.2 3.6 %collective-permute-start = (s32[1,2,1,2,256]{4,3,1,2,0:T(2,128)}, s32[1,2,1,2,256]{4,3,1,2,0:T(2,128)S(1)}, u32[]{:S(2)}, u32[]{:S(2)}) collective-permute-start(s32[1,2,1,2,256]{4,3,1,2,0:T(2,128)} %bitcast.16), channel_id=1, source_target_pairs={{0,2},{2,0},{4,6},{6,4},{8,10},{10,8},{12,14},{14,12},{1,3},{3,1},... | collective-permute-start | bytes 12296 | tf_op jit(solution)/shard_map/ppermute | solution.py:476
  8.8 12.1 %collective-permute-start.3 = (s32[4,2,2,256]{3,2,1,0:T(2,128)S(1)}, s32[4,2,2,256]{3,2,1,0:T(2,128)S(1)}, u32[]{:S(2)}, u32[]{:S(2)}) collective-permute-start(s32[4,2,2,256]{3,2,1,0:T(2,128)S(1)} %pad_add_fusion.near_h), channel_id=1, source_target_pairs={{0,8},{2,10},{4,12},{6,14},{8,0},{10,2},{12,4},{14,6},{1,9},{3,11}... | collective-permute-start | bytes 49160 | tf_op jit(solution)/shard_map/ppermute | solution.py:476
  13.7 13.0 %all-to-all-start = ((bf16[16,16,128]{2,1,0:T(8,128)(2,1)}), bf16[16,16,128]{2,1,0:T(8,128)(2,1)S(1)}, u32[]{:S(2)}, u32[]{:S(2)}) async-start(bf16[16,16,128]{2,1,0:T(8,128)(2,1)} %get-tuple-element.25), calls=%async_computation | async-start | bytes 131072 | tf_op jit(solution)/shard_map/all_to_all | solution.py:515

commit v5 on v4

--- a/solution.py
+++ b/solution.py
@@ -122,8 +122,7 @@
         ],
         sems,
     )
-    for copy in copies:
-        copy.wait()
+    copies[0].wait()
     row = lax.broadcasted_iota(jnp.int32, (NF, 2 * M), 0)
     lane = lax.broadcasted_iota(jnp.int32, (NF, 2 * M), 1)
     tuning = jnp.zeros((NF, 2 * M), jnp.int32)
@@ -138,6 +137,8 @@
             steps = (L // NH) * (first + late * later) + (L // 4) * (part - (lane >> 7))
             blocks.append((cos_of(turn_angle(steps, L)) * (1.0 / 64.0)).astype(BF))
     w_high = jnp.concatenate(blocks, 0)
+    for copy in copies[1:]:
+        copy.wait()
     for part in range(2):
         whole = rows[part].astype(F32)
         for high in range(NH):
@@ -257,7 +258,7 @@
         tail[4 + at : 5 + at, :] = weight[:, half]
     for step in range(NT // 2):
         spots[team ^ step] = near[step]
-        spots[team ^ (step + NT // 2)] = far[step]
+        spots[team ^ (NT - 1) ^ step] = far[step]
     count = lax.broadcasted_iota(jnp.int32, (8, M), 0)
 
     def turns(place, tile):
@@ -511,7 +512,7 @@
     )
     *others, windows = lax.optimization_barrier((*others, windows))
     near = jnp.stack([part.reshape(NB, 2, VB) for part in [cells_v] + others])
-    far = partner(near, NT // 2)
+    far = partner(near, NT - 1)
     arrived = lax.all_to_all(windows, "facet", 0, 0, tiled=True)
     col_t, row_fac, lift, k_right, own_map, tail, phase, w_rows, picks, turn, w_high = call(
         setup_kernel,

time: 56.1 us -> 55.6 us (level)
  starting transfers between devices: 17.6 us -> 16.2 us
  blocking collectives: 24 us -> 24.9 us
    ppermute x4, starting transfers between devices: 10.4 us -> 9.04 us  [partner(): return lax.ppermute(value, 'team', pairs)]
    all_to_all x1, blocking collectives: 10 us -> 10.9 us  [local(): gathered = lax.all_to_all(parts, 'team', 0, 0, tiled=True)]
where the time goes in v5:
time: 55.6 us; the launch traced here: 55.4 us
  blocking collectives  24.9 us (45%)
  starting transfers between devices  16.2 us (29%)
  Pallas kernels  9.65 us (17%)
  waiting for transfers between devices  4.57 us (8%)
    all_to_all x1, blocking collectives, local(): returned = lax.all_to_all(folded, ('facet', 'sub'), 0, 0, tiled=True)  14 us
    all_to_all x1, blocking collectives, local(): gathered = lax.all_to_all(parts, 'team', 0, 0, tiled=True)  10.9 us
    ppermute x4, starting transfers between devices, partner(): return lax.ppermute(value, 'team', pairs)  9.04 us
    all_to_all x1, starting transfers between devices, local(): arrived = lax.all_to_all(windows, 'facet', 0, 0, tiled=True)  7.21 us
    all_to_all x1, waiting for transfers between devices, local(): arrived = lax.all_to_all(windows, 'facet', 0, 0, tiled=True)  3.53 us
    pallas_call x1, Pallas kernels, local(): call(setup_kernel, [VMEM] * 2 + [ANY] * 2 + [HBM] * 7, [shape(2 * SG, NV)...  2.28 us
    pallas_call x1, Pallas kernels, local(): call(forward_kernel, [HBM] * 6, [shape(NF, 2 * RD, M), shape(2, NF * NB,...  2.23 us
    pallas_call x1, Pallas kernels, local(): call(predict_kernel, [VMEM] * 8, shape(NT, SENT, M), [buf(SENT, M, dtype=...  2.04 us
  transfers between devices with their start and end apart: 5, of which 2 were waited for; matrix products, arithmetic and copies ran while one was open for 0% of the time, Pallas kernels for 8%

profile of v5, /device:TPU:1, one launch (start us, length us, event | category | flops | bytes accessed | tf_op | source)
XLA Modules:
  0.0 55.4 jit_solution(8160315017314388456)
XLA Ops:
  0.0 5.2 %collective-permute-start.2 = (s32[1,2,1,2,256]{4,3,1,2,0:T(2,128)}, s32[1,2,1,2,256]{4,3,1,2,0:T(2,128)S(1)}, u32[]{:S(2)}, u32[]{:S(2)}) collective-permute-start(s32[1,2,1,2,256]{4,3,1,2,0:T(2,128)} %bitcast.14), channel_id=1, source_target_pairs={{0,6},{2,4},{4,2},{6,0},{8,14},{10,12},{12,10},{14,8},{1,7},{3,5},... | collective-permute-start | bytes 12296 | tf_op jit(solution)/shard_map/ppermute | solution.py:477
  5.2 0.0 collective-permute-start.1
  5.2 0.3 collective-permute-start
  5.5 2.2 %windows.1 = (bf16[16,16,128]{2,1,0:T(8,128)(2,1)}, s32[2,32]{1,0:T(2,128)S(1)}, s32[2,16]{1,0:T(2,128)S(1)}, s32[2,2,256]{2,1,0:T(2,128)S(1)}) custom-call(s32[2,32]{1,0:T(2,128)} %bitcast.17, s32[2,16]{1,0:T(2,128)} %bitcast.18, s32[1,2,1,2,256]{4,3,2,1,0:T(2,128)} %cells_h.1, bf16[1,2,8,4096]{3,2,1,0:T(8,128)(2,1)} %rows_h.1, ...), custom_call_target="tpu_custom_call" | custom-call | tf_op jit(solution)/shard_map/windows/pallas_call | solution.py:490
  7.7 0.0 collective-permute-done.2
  7.7 1.0 %collective-permute-done.1 = s32[1,2,1,2,256]{4,3,1,2,0:T(2,128)S(1)} collective-permute-done((s32[1,2,1,2,256]{4,3,1,2,0:T(2,128)}, s32[1,2,1,2,256]{4,3,1,2,0:T(2,128)S(1)}, u32[]{:S(2)}, u32[]{:S(2)}) %collective-permute-start.1) | collective-permute-done | bytes 4128 | tf_op jit(solution)/shard_map/ppermute | solution.py:477
  8.7 0.0 collective-permute-done
  8.8 3.6 %collective-permute-start.3 = (s32[4,2,2,256]{3,2,1,0:T(2,128)S(1)}, s32[4,2,2,256]{3,2,1,0:T(2,128)S(1)}, u32[]{:S(2)}, u32[]{:S(2)}) collective-permute-start(s32[4,2,2,256]{3,2,1,0:T(2,128)S(1)} %pad_add_fusion.near_h), channel_id=1, source_target_pairs={{0,14},{2,12},{4,10},{6,8},{8,6},{10,4},{12,2},{14,0},{1,15},{3,13... | collective-permute-start | bytes 49160 | tf_op jit(solution)/shard_map/ppermute | solution.py:477
  12.3 7.2 %all-to-all-start = ((bf16[16,16,128]{2,1,0:T(8,128)(2,1)}), bf16[16,16,128]{2,1,0:T(8,128)(2,1)S(1)}, u32[]{:S(2)}, u32[]{:S(2)}) async-start(bf16[16,16,128]{2,1,0:T(8,128)(2,1)} %get-tuple-element.25), calls=%async_computation | async-start | bytes 131072 | tf_op jit(solution)/shard_map/all_to_all | solution.py:516
  19.5 0.0 collective-permute-done.3.far_h
  19.5 2.3 %setup.1 = (bf16[512,2048]{1,0:T(8,128)(2,1)S(1)}, f32[24,2048]{1,0:T(8,128)S(1)}, bf16[512,256]{1,0:T(8,128)(2,1)S(1)}, bf16[256,512]{1,0:T(8,128)(2,1)S(1)}, b...) custom-call(s32[2,32]{1,0:T(2,128)S(1)} %get-tuple-element.26.offs_v, ...), custom_call_target="tpu_custom_call" | custom-call | flops 20000000000 | bytes 4194304 | tf_op jit(solution)/shard_map/setup/pallas_call | solution.py:517
  21.8 3.5 %all-to-all-done.spec = bf16[16,16,128]{2,1,0:T(8,128)(2,1)S(1)} async-done(((bf16[16,16,128]{2,1,0:T(8,128)(2,1)}), bf16[16,16,128]{2,1,0:T(8,128)(2,1)S(1)}, u32[]{:S(2)}, u32[]{:S(2)}) %all-to-all-start) | async-done | bytes 65568 | tf_op jit(solution)/shard_map/all_to_all | solution.py:516
  25.4 2.0 %predict.1 = bf16[8,40,128]{2,1,0:T(8,128)(2,1)S(1)} custom-call(bf16[16,16,128]{2,1,0:T(8,128)(2,1)S(1)} %all-to-all-done.spec, bf16[512,256]{1,0:T(8,128)(2,1)S(1)} %get-tuple-element.32.lift, bf16[256,512]{1,0:T(8,128)(2,1)S(1)} %get-tuple-element.33.k_right, bf16[256,256]{1,0:T(8,128)(2,1)S(1)} %get-tuple-element.34.aterm, ...), custom_call_target="tpu_custom_call" | custom-call | tf_op jit(solution)/shard_map/predict/pallas_call | solution.py:550
  27.4 10.9 %all_to_all.15.parts = bf16[8,40,128]{2,1,0:T(8,128)(2,1)S(1)} all-to-all(bf16[8,40,128]{2,1,0:T(8,128)(2,1)S(1)} %predict.1), channel_id=1, replica_groups=mesh['facet'=16,'team'=8,'sub'=2] {'team'}, dimensions={0} | all-to-all | bytes 163840 | tf_op jit(solution)/shard_map/all_to_all | solution.py:557
  38.3 1.9 %grid.1 = bf16[32,16,128]{2,1,0:T(8,128)(2,1)S(1)} custom-call(bf16[8,40,128]{2,1,0:T(8,128)(2,1)S(1)} %all_to_all.15.parts, bf16[512,2048]{1,0:T(8,128)(2,1)S(1)} %get-tuple-element.35.col_t, f32[24,2048]{1,0:T(8,128)S(1)} %get-tuple-element.36.row_fac, bf16[256,256]{1,0:T(8,128)(2,1)S(1)} %get-tuple-element.34.aterm, ...), custom_call_target="tpu_custom_call" | custom-call | tf_op jit(solution)/shard_map/grid/pallas_call | solution.py:558
  40.2 14.0 %all_to_all.16.folded = bf16[32,16,128]{2,1,0:T(8,128)(2,1)S(1)} all-to-all(bf16[32,16,128]{2,1,0:T(8,128)(2,1)S(1)} %grid.1), channel_id=1, replica_groups=mesh['facet'=16,'team'=8,'sub'=2] {'facet','sub'}, dimensions={0} | all-to-all | bytes 262144 | tf_op jit(solution)/shard_map/all_to_all | solution.py:569
  54.2 1.2 %update.1 = f32[2,8,2048]{2,1,0:T(8,128)} custom-call(bf16[32,16,128]{2,1,0:T(8,128)(2,1)S(1)} %all_to_all.16.folded, bf16[256,128]{1,0:T(8,128)(2,1)S(1)} %get-tuple-element.39.w_rows, f32[32,128]{1,0:T(8,128)S(1)} %get-tuple-element.40.picks, f32[2,128,128]{2,1,0:T(8,128)S(1)} %get-tuple-element.41.turn, bf16[32,256]{1,0:T(8,128)(2,1)S(1)} %get-tuple-element.42.w_high), custom_call_target="tpu_custom_call" | custom-call | tf_op jit(solution)/shard_map/update/pallas_call | solution.py:570
  (1 shorter events, 0.0 us)
Async XLA Ops:
  0.0 7.7 %collective-permute-start.2 = (s32[1,2,1,2,256]{4,3,1,2,0:T(2,128)}, s32[1,2,1,2,256]{4,3,1,2,0:T(2,128)S(1)}, u32[]{:S(2)}, u32[]{:S(2)}) collective-permute-start(s32[1,2,1,2,256]{4,3,1,2,0:T(2,128)} %bitcast.14), channel_id=1, source_target_pairs={{0,6},{2,4},{4,2},{6,0},{8,14},{10,12},{12,10},{14,8},{1,7},{3,5},... | collective-permute-start | bytes 12296 | tf_op jit(solution)/shard_map/ppermute | solution.py:477
  5.2 3.6 %collective-permute-start.1 = (s32[1,2,1,2,256]{4,3,1,2,0:T(2,128)}, s32[1,2,1,2,256]{4,3,1,2,0:T(2,128)S(1)}, u32[]{:S(2)}, u32[]{:S(2)}) collective-permute-start(s32[1,2,1,2,256]{4,3,1,2,0:T(2,128)} %bitcast.15), channel_id=1, source_target_pairs={{0,4},{2,6},{4,0},{6,2},{8,12},{10,14},{12,8},{14,10},{1,5},{3,7},... | collective-permute-start | bytes 12296 | tf_op jit(solution)/shard_map/ppermute | solution.py:477
  5.2 3.6 %collective-permute-start = (s32[1,2,1,2,256]{4,3,1,2,0:T(2,128)}, s32[1,2,1,2,256]{4,3,1,2,0:T(2,128)S(1)}, u32[]{:S(2)}, u32[]{:S(2)}) collective-permute-start(s32[1,2,1,2,256]{4,3,1,2,0:T(2,128)} %bitcast.16), channel_id=1, source_target_pairs={{0,2},{2,0},{4,6},{6,4},{8,10},{10,8},{12,14},{14,12},{1,3},{3,1},... | collective-permute-start | bytes 12296 | tf_op jit(solution)/shard_map/ppermute | solution.py:477
  8.8 10.8 %collective-permute-start.3 = (s32[4,2,2,256]{3,2,1,0:T(2,128)S(1)}, s32[4,2,2,256]{3,2,1,0:T(2,128)S(1)}, u32[]{:S(2)}, u32[]{:S(2)}) collective-permute-start(s32[4,2,2,256]{3,2,1,0:T(2,128)S(1)} %pad_add_fusion.near_h), channel_id=1, source_target_pairs={{0,14},{2,12},{4,10},{6,8},{8,6},{10,4},{12,2},{14,0},{1,15},{3,13... | collective-permute-start | bytes 49160 | tf_op jit(solution)/shard_map/ppermute | solution.py:477
  12.3 13.0 %all-to-all-start = ((bf16[16,16,128]{2,1,0:T(8,128)(2,1)}), bf16[16,16,128]{2,1,0:T(8,128)(2,1)S(1)}, u32[]{:S(2)}, u32[]{:S(2)}) async-start(bf16[16,16,128]{2,1,0:T(8,128)(2,1)} %get-tuple-element.25), calls=%async_computation | async-start | bytes 131072 | tf_op jit(solution)/shard_map/all_to_all | solution.py:516

commit v6 on v5

--- a/solution.py
+++ b/solution.py
@@ -20,6 +20,8 @@
 NH = L // M
 NV = NT * VB
 TWO_PI = 2.0 * math.pi
+NEAR = (0, 1, 2, 3)
+FAR = 6
 BF = jnp.bfloat16
 F32 = jnp.float32
 
@@ -256,9 +258,9 @@
         tail[at : at + 1, :] = both[0:1, half]
         tail[2 + at : 3 + at, :] = both[1:2, half]
         tail[4 + at : 5 + at, :] = weight[:, half]
-    for step in range(NT // 2):
-        spots[team ^ step] = near[step]
-        spots[team ^ (NT - 1) ^ step] = far[step]
+    for at, mask in enumerate(NEAR):
+        spots[team ^ mask] = near[at]
+        spots[team ^ FAR ^ mask] = far[at]
     count = lax.broadcasted_iota(jnp.int32, (8, M), 0)
 
     def turns(place, tile):
@@ -486,7 +488,7 @@
     offs = keep(offs)
     foffs = keep(foffs)
     ids = [smem(2, NF * NB), smem(2, NF)]
-    others = [partner(cells, mask) for mask in (1, 2, 3)]
+    others = [partner(cells, mask) for mask in NEAR[1:]]
     windows, offs_v, foffs_v, cells_v = call(
         forward_kernel,
         [HBM] * 6,
@@ -512,7 +514,7 @@
     )
     *others, windows = lax.optimization_barrier((*others, windows))
     near = jnp.stack([part.reshape(NB, 2, VB) for part in [cells_v] + others])
-    far = partner(near, NT - 1)
+    far = partner(near, FAR)
     arrived = lax.all_to_all(windows, "facet", 0, 0, tiled=True)
     col_t, row_fac, lift, k_right, own_map, tail, phase, w_rows, picks, turn, w_high = call(
         setup_kernel,

time: 55.6 us -> 55.6 us (level)
  starting transfers between devices: 16.2 us -> 17.1 us
  blocking collectives: 24.9 us -> 24 us
    all_to_all x1, blocking collectives: 10.9 us -> 9.99 us  [local(): gathered = lax.all_to_all(parts, 'team', 0, 0, tiled=True)]
    all_to_all x1, starting transfers between devices: 7.21 us -> 7.78 us  [local(): arrived = lax.all_to_all(windows, 'facet', 0, 0, tiled=True)]
where the time goes in v6:
time: 55.6 us; the launch traced here: 55.4 us
  blocking collectives  24 us (43%)
  starting transfers between devices  17.1 us (31%)
  Pallas kernels  9.66 us (17%)
  waiting for transfers between devices  4.57 us (8%)
    all_to_all x1, blocking collectives, local(): returned = lax.all_to_all(folded, ('facet', 'sub'), 0, 0, tiled=True)  14 us
    all_to_all x1, blocking collectives, local(): gathered = lax.all_to_all(parts, 'team', 0, 0, tiled=True)  9.99 us
    ppermute x4, starting transfers between devices, partner(): return lax.ppermute(value, 'team', pairs)  9.35 us
    all_to_all x1, starting transfers between devices, local(): arrived = lax.all_to_all(windows, 'facet', 0, 0, tiled=True)  7.78 us
    all_to_all x1, waiting for transfers between devices, local(): arrived = lax.all_to_all(windows, 'facet', 0, 0, tiled=True)  3.53 us
    pallas_call x1, Pallas kernels, local(): call(setup_kernel, [VMEM] * 2 + [ANY] * 2 + [HBM] * 7, [shape(2 * SG, NV)...  2.28 us
    pallas_call x1, Pallas kernels, local(): call(forward_kernel, [HBM] * 6, [shape(NF, 2 * RD, M), shape(2, NF * NB,...  2.23 us
    pallas_call x1, Pallas kernels, local(): call(predict_kernel, [VMEM] * 8, shape(NT, SENT, M), [buf(SENT, M, dtype=...  2.05 us
  transfers between devices with their start and end apart: 5, of which 2 were waited for; matrix products, arithmetic and copies ran while one was open for 0% of the time, Pallas kernels for 8%

profile of v6, /device:TPU:1, one launch (start us, length us, event | category | flops | bytes accessed | tf_op | source)
XLA Modules:
  0.0 55.4 jit_solution(5899506122387204136)
XLA Ops:
  0.0 5.2 %collective-permute-start.2 = (s32[1,2,1,2,256]{4,3,1,2,0:T(2,128)}, s32[1,2,1,2,256]{4,3,1,2,0:T(2,128)S(1)}, u32[]{:S(2)}, u32[]{:S(2)}) collective-permute-start(s32[1,2,1,2,256]{4,3,1,2,0:T(2,128)} %bitcast.14), channel_id=1, source_target_pairs={{0,6},{2,4},{4,2},{6,0},{8,14},{10,12},{12,10},{14,8},{1,7},{3,5},... | collective-permute-start | bytes 12296 | tf_op jit(solution)/shard_map/ppermute | solution.py:479
  5.2 0.0 collective-permute-start.1
  5.2 0.3 collective-permute-start
  5.5 2.2 %windows.1 = (bf16[16,16,128]{2,1,0:T(8,128)(2,1)}, s32[2,32]{1,0:T(2,128)S(1)}, s32[2,16]{1,0:T(2,128)S(1)}, s32[2,2,256]{2,1,0:T(2,128)S(1)}) custom-call(s32[2,32]{1,0:T(2,128)} %bitcast.17, s32[2,16]{1,0:T(2,128)} %bitcast.18, s32[1,2,1,2,256]{4,3,2,1,0:T(2,128)} %cells_h.1, bf16[1,2,8,4096]{3,2,1,0:T(8,128)(2,1)} %rows_h.1, ...), custom_call_target="tpu_custom_call" | custom-call | tf_op jit(solution)/shard_map/windows/pallas_call | solution.py:492
  7.7 0.0 collective-permute-done.2
  7.7 1.0 %collective-permute-done.1 = s32[1,2,1,2,256]{4,3,1,2,0:T(2,128)S(1)} collective-permute-done((s32[1,2,1,2,256]{4,3,1,2,0:T(2,128)}, s32[1,2,1,2,256]{4,3,1,2,0:T(2,128)S(1)}, u32[]{:S(2)}, u32[]{:S(2)}) %collective-permute-start.1) | collective-permute-done | bytes 4128 | tf_op jit(solution)/shard_map/ppermute | solution.py:479
  8.7 0.0 collective-permute-done
  8.8 3.9 %collective-permute-start.3 = (s32[4,2,2,256]{3,2,1,0:T(2,128)S(1)}, s32[4,2,2,256]{3,2,1,0:T(2,128)S(1)}, u32[]{:S(2)}, u32[]{:S(2)}) collective-permute-start(s32[4,2,2,256]{3,2,1,0:T(2,128)S(1)} %pad_add_fusion.near_h), channel_id=1, source_target_pairs={{0,12},{2,14},{4,8},{6,10},{8,4},{10,6},{12,0},{14,2},{1,13},{3,15... | collective-permute-start | bytes 49160 | tf_op jit(solution)/shard_map/ppermute | solution.py:479
  12.6 7.8 %all-to-all-start = ((bf16[16,16,128]{2,1,0:T(8,128)(2,1)}), bf16[16,16,128]{2,1,0:T(8,128)(2,1)S(1)}, u32[]{:S(2)}, u32[]{:S(2)}) async-start(bf16[16,16,128]{2,1,0:T(8,128)(2,1)} %get-tuple-element.25), calls=%async_computation | async-start | bytes 131072 | tf_op jit(solution)/shard_map/all_to_all | solution.py:518
  20.4 0.0 collective-permute-done.3.far_h
  20.4 2.3 %setup.1 = (bf16[512,2048]{1,0:T(8,128)(2,1)S(1)}, f32[24,2048]{1,0:T(8,128)S(1)}, bf16[512,256]{1,0:T(8,128)(2,1)S(1)}, bf16[256,512]{1,0:T(8,128)(2,1)S(1)}, b...) custom-call(s32[2,32]{1,0:T(2,128)S(1)} %get-tuple-element.26.offs_v, ...), custom_call_target="tpu_custom_call" | custom-call | flops 20000000000 | bytes 4194304 | tf_op jit(solution)/shard_map/setup/pallas_call | solution.py:519
  22.7 3.5 %all-to-all-done.spec = bf16[16,16,128]{2,1,0:T(8,128)(2,1)S(1)} async-done(((bf16[16,16,128]{2,1,0:T(8,128)(2,1)}), bf16[16,16,128]{2,1,0:T(8,128)(2,1)S(1)}, u32[]{:S(2)}, u32[]{:S(2)}) %all-to-all-start) | async-done | bytes 65568 | tf_op jit(solution)/shard_map/all_to_all | solution.py:518
  26.2 2.0 %predict.1 = bf16[8,40,128]{2,1,0:T(8,128)(2,1)S(1)} custom-call(bf16[16,16,128]{2,1,0:T(8,128)(2,1)S(1)} %all-to-all-done.spec, bf16[512,256]{1,0:T(8,128)(2,1)S(1)} %get-tuple-element.32.lift, bf16[256,512]{1,0:T(8,128)(2,1)S(1)} %get-tuple-element.33.k_right, bf16[256,256]{1,0:T(8,128)(2,1)S(1)} %get-tuple-element.34.aterm, ...), custom_call_target="tpu_custom_call" | custom-call | tf_op jit(solution)/shard_map/predict/pallas_call | solution.py:552
  28.3 10.0 %all_to_all.15.parts = bf16[8,40,128]{2,1,0:T(8,128)(2,1)S(1)} all-to-all(bf16[8,40,128]{2,1,0:T(8,128)(2,1)S(1)} %predict.1), channel_id=1, replica_groups=mesh['facet'=16,'team'=8,'sub'=2] {'team'}, dimensions={0} | all-to-all | bytes 163840 | tf_op jit(solution)/shard_map/all_to_all | solution.py:559
  38.3 1.9 %grid.1 = bf16[32,16,128]{2,1,0:T(8,128)(2,1)S(1)} custom-call(bf16[8,40,128]{2,1,0:T(8,128)(2,1)S(1)} %all_to_all.15.parts, bf16[512,2048]{1,0:T(8,128)(2,1)S(1)} %get-tuple-element.35.col_t, f32[24,2048]{1,0:T(8,128)S(1)} %get-tuple-element.36.row_fac, bf16[256,256]{1,0:T(8,128)(2,1)S(1)} %get-tuple-element.34.aterm, ...), custom_call_target="tpu_custom_call" | custom-call | tf_op jit(solution)/shard_map/grid/pallas_call | solution.py:560
  40.2 14.0 %all_to_all.16.folded = bf16[32,16,128]{2,1,0:T(8,128)(2,1)S(1)} all-to-all(bf16[32,16,128]{2,1,0:T(8,128)(2,1)S(1)} %grid.1), channel_id=1, replica_groups=mesh['facet'=16,'team'=8,'sub'=2] {'facet','sub'}, dimensions={0} | all-to-all | bytes 262144 | tf_op jit(solution)/shard_map/all_to_all | solution.py:571
  54.2 1.2 %update.1 = f32[2,8,2048]{2,1,0:T(8,128)} custom-call(bf16[32,16,128]{2,1,0:T(8,128)(2,1)S(1)} %all_to_all.16.folded, bf16[256,128]{1,0:T(8,128)(2,1)S(1)} %get-tuple-element.39.w_rows, f32[32,128]{1,0:T(8,128)S(1)} %get-tuple-element.40.picks, f32[2,128,128]{2,1,0:T(8,128)S(1)} %get-tuple-element.41.turn, bf16[32,256]{1,0:T(8,128)(2,1)S(1)} %get-tuple-element.42.w_high), custom_call_target="tpu_custom_call" | custom-call | tf_op jit(solution)/shard_map/update/pallas_call | solution.py:572
  (1 shorter events, 0.0 us)
Async XLA Ops:
  0.0 7.7 %collective-permute-start.2 = (s32[1,2,1,2,256]{4,3,1,2,0:T(2,128)}, s32[1,2,1,2,256]{4,3,1,2,0:T(2,128)S(1)}, u32[]{:S(2)}, u32[]{:S(2)}) collective-permute-start(s32[1,2,1,2,256]{4,3,1,2,0:T(2,128)} %bitcast.14), channel_id=1, source_target_pairs={{0,6},{2,4},{4,2},{6,0},{8,14},{10,12},{12,10},{14,8},{1,7},{3,5},... | collective-permute-start | bytes 12296 | tf_op jit(solution)/shard_map/ppermute | solution.py:479
  5.2 3.6 %collective-permute-start.1 = (s32[1,2,1,2,256]{4,3,1,2,0:T(2,128)}, s32[1,2,1,2,256]{4,3,1,2,0:T(2,128)S(1)}, u32[]{:S(2)}, u32[]{:S(2)}) collective-permute-start(s32[1,2,1,2,256]{4,3,1,2,0:T(2,128)} %bitcast.15), channel_id=1, source_target_pairs={{0,4},{2,6},{4,0},{6,2},{8,12},{10,14},{12,8},{14,10},{1,5},{3,7},... | collective-permute-start | bytes 12296 | tf_op jit(solution)/shard_map/ppermute | solution.py:479
  5.2 3.6 %collective-permute-start = (s32[1,2,1,2,256]{4,3,1,2,0:T(2,128)}, s32[1,2,1,2,256]{4,3,1,2,0:T(2,128)S(1)}, u32[]{:S(2)}, u32[]{:S(2)}) collective-permute-start(s32[1,2,1,2,256]{4,3,1,2,0:T(2,128)} %bitcast.16), channel_id=1, source_target_pairs={{0,2},{2,0},{4,6},{6,4},{8,10},{10,8},{12,14},{14,12},{1,3},{3,1},... | collective-permute-start | bytes 12296 | tf_op jit(solution)/shard_map/ppermute | solution.py:479
  8.8 11.7 %collective-permute-start.3 = (s32[4,2,2,256]{3,2,1,0:T(2,128)S(1)}, s32[4,2,2,256]{3,2,1,0:T(2,128)S(1)}, u32[]{:S(2)}, u32[]{:S(2)}) collective-permute-start(s32[4,2,2,256]{3,2,1,0:T(2,128)S(1)} %pad_add_fusion.near_h), channel_id=1, source_target_pairs={{0,12},{2,14},{4,8},{6,10},{8,4},{10,6},{12,0},{14,2},{1,13},{3,15... | collective-permute-start | bytes 49160 | tf_op jit(solution)/shard_map/ppermute | solution.py:479
  12.6 13.6 %all-to-all-start = ((bf16[16,16,128]{2,1,0:T(8,128)(2,1)}), bf16[16,16,128]{2,1,0:T(8,128)(2,1)S(1)}, u32[]{:S(2)}, u32[]{:S(2)}) async-start(bf16[16,16,128]{2,1,0:T(8,128)(2,1)} %get-tuple-element.25), calls=%async_computation | async-start | bytes 131072 | tf_op jit(solution)/shard_map/all_to_all | solution.py:518

commit v7 on v4

--- a/solution.py
+++ b/solution.py
@@ -20,6 +20,7 @@
 NH = L // M
 NV = NT * VB
 TWO_PI = 2.0 * math.pi
+FAR = 6
 BF = jnp.bfloat16
 F32 = jnp.float32
 
@@ -105,30 +106,22 @@
     return copies
 
 
+def lead_kernel(out):
+    out[...] = jnp.zeros_like(out)
+
+
 def forward_kernel(
-    offs_h, foffs_h, cells_h, rows_h, w_rows_h, turn_h,
-    out, offs_v, foffs_v, cells_v, offs, rows, w_rows, turn, xs, xo, sems,
+    lead, offs_in, foffs_in, rows, w_rows, turn, out, offs_v, foffs_v, xs, xo
 ):
     side = lax.axis_index("sub")
-    copies = fetch(
-        [
-            (offs_h, offs),
-            (rows_h.at[0], rows),
-            (w_rows_h, w_rows),
-            (turn_h, turn),
-            (offs_h, offs_v),
-            (foffs_h, foffs_v),
-            (cells_h.at[0, :, 0], cells_v),
-        ],
-        sems,
-    )
-    for copy in copies:
-        copy.wait()
-    row = lax.broadcasted_iota(jnp.int32, (NF, 2 * M), 0)
+    offs_v[...] = offs_in[...]
+    foffs_v[...] = foffs_in[...]
+    place = lax.broadcasted_iota(jnp.int32, (NF, NF * NB), 1)
+    owner = lax.broadcasted_iota(jnp.int32, (NF, NF * NB), 0)
+    columns = jnp.broadcast_to(offs_in[1:2, :].astype(F32), (NF, NF * NB))
+    tuning = jnp.sum(jnp.where(place == owner * NB + side, columns, 0.0), 1, keepdims=True)
+    tuning = jnp.broadcast_to(tuning, (NF, 2 * M)).astype(jnp.int32)
     lane = lax.broadcasted_iota(jnp.int32, (NF, 2 * M), 1)
-    tuning = jnp.zeros((NF, 2 * M), jnp.int32)
-    for a in range(NF):
-        tuning = jnp.where(row == a, offs[1, a * NB + side], tuning)
     pick = lane[:, :M] >= (tuning[:, :M] & (M - 1))
     first = (tuning >> 7) * (lane & (M - 1))
     later = lane & (M - 1)
@@ -139,7 +132,7 @@
             blocks.append((cos_of(turn_angle(steps, L)) * (1.0 / 64.0)).astype(BF))
     w_high = jnp.concatenate(blocks, 0)
     for part in range(2):
-        whole = rows[part].astype(F32)
+        whole = rows[0, part].astype(F32)
         for high in range(NH):
             xs[pl.ds((part * NH + high) * RD, RD), :] = whole[:, high * M : (high + 1) * M]
     stacked = jnp.concatenate(
@@ -257,7 +250,7 @@
         tail[4 + at : 5 + at, :] = weight[:, half]
     for step in range(NT // 2):
         spots[team ^ step] = near[step]
-        spots[team ^ (step + NT // 2)] = far[step]
+        spots[team ^ FAR ^ step] = far[step]
     count = lax.broadcasted_iota(jnp.int32, (8, M), 0)
 
     def turns(place, tile):
@@ -482,36 +475,36 @@
     foffs = facet_offsets.T
     live = counts.transpose(1, 2, 0)
     keep = lambda array: pltpu.with_memory_space_constraint(array, pltpu.HBM)
-    offs = keep(offs)
-    foffs = keep(foffs)
     ids = [smem(2, NF * NB), smem(2, NF)]
+    lead = call(
+        lead_kernel,
+        [],
+        shape(8, M, dtype=F32),
+        [],
+        "lead",
+        cost=pl.CostEstimate(flops=20 * 10**9, transcendentals=0, bytes_accessed=2**12),
+    )()
+    cells, lead = lax.optimization_barrier((cells, lead))
     others = [partner(cells, mask) for mask in (1, 2, 3)]
-    windows, offs_v, foffs_v, cells_v = call(
+    windows, offs_v, foffs_v = call(
         forward_kernel,
-        [HBM] * 6,
+        [ANY] + [VMEM] * 5,
         [
             shape(NF, 2 * RD, M),
             shape(2, NF * NB, dtype=jnp.int32),
             shape(2, NF, dtype=jnp.int32),
-            shape(NB, 2, VB, dtype=jnp.int32),
         ],
         [
-            smem(2, NF * NB),
-            buf(2, RD, L),
-            buf(2 * M, 2 * NH),
-            buf(2, M, M, dtype=F32),
             buf(2 * NH * RD, M, dtype=F32),
             buf(NF * 2 * RD, M, dtype=F32),
-            sems(7),
         ],
         "windows",
     )(
-        offs, foffs, keep(cells), keep(facet_rows),
-        keep(t["fwd_rows"]), keep(t["fwd_turn"]),
+        lead, offs, foffs, facet_rows, t["fwd_rows"], t["fwd_turn"],
     )
     *others, windows = lax.optimization_barrier((*others, windows))
-    near = jnp.stack([part.reshape(NB, 2, VB) for part in [cells_v] + others])
-    far = partner(near, NT // 2)
+    near = jnp.stack([part.reshape(NB, 2, VB) for part in [cells] + others])
+    far = partner(near, FAR)
     arrived = lax.all_to_all(windows, "facet", 0, 0, tiled=True)
     col_t, row_fac, lift, k_right, own_map, tail, phase, w_rows, picks, turn, w_high = call(
         setup_kernel,

time: 56.1 us -> 56.1 us (level)
  Pallas kernels: 9.68 us -> 8.62 us
  waiting for transfers between devices: 4.54 us -> 5.38 us
  local copies, waits for them, and re-layouts: 0 us -> 0.7 us
    pallas_call x1 -> x2, Pallas kernels: 2.26 us -> 1.2 us  [the longest x1 1.2 us: local(): call(forward_kernel, [ANY] + [VMEM] * 5, [shape(NF, 2 * RD, M), shape(2,...]
    ppermute x4, starting transfers between devices: 10.4 us -> 9.35 us  [partner(): return lax.ppermute(value, 'team', pairs)]
    ppermute x4, waiting for transfers between devices: 1.01 us -> 1.85 us  [partner(): return lax.ppermute(value, 'team', pairs)]
    unnamed x0 -> x12, local copies, waits for them, and re-layouts: none -> 0.7 us
    all_to_all x1, starting transfers between devices: 7.21 us -> 7.78 us  [local(): arrived = lax.all_to_all(windows, 'facet', 0, 0, tiled=True)]
  transfers between devices with their start and end apart: 5 -> 5, of which waited for: 2 -> 2; matrix products, arithmetic and copies ran while one was open for 0% -> 0% of each run, Pallas kernels for 8% -> 6%
where the time goes in v7:
time: 56.1 us; the launch traced here: 55.9 us
  blocking collectives  24 us (43%)
  starting transfers between devices  17.1 us (30%)
  Pallas kernels  8.62 us (15%)
  waiting for transfers between devices  5.38 us (10%)
  local copies, waits for them, and re-layouts  0.7 us (1%)
    all_to_all x1, blocking collectives, local(): returned = lax.all_to_all(folded, ('facet', 'sub'), 0, 0, tiled=True)  14 us
    all_to_all x1, blocking collectives, local(): gathered = lax.all_to_all(parts, 'team', 0, 0, tiled=True)  9.99 us
    ppermute x4, starting transfers between devices, partner(): return lax.ppermute(value, 'team', pairs)  9.35 us
    all_to_all x1, starting transfers between devices, local(): arrived = lax.all_to_all(windows, 'facet', 0, 0, tiled=True)  7.78 us
    all_to_all x1, waiting for transfers between devices, local(): arrived = lax.all_to_all(windows, 'facet', 0, 0, tiled=True)  3.53 us
    pallas_call x1, Pallas kernels, local(): call(setup_kernel, [VMEM] * 2 + [ANY] * 2 + [HBM] * 7, [shape(2 * SG, NV)...  2.28 us
    pallas_call x1, Pallas kernels, local(): call(predict_kernel, [VMEM] * 8, shape(NT, SENT, M), [buf(SENT, M, dtype=...  2.04 us
    pallas_call x1, Pallas kernels, local(): call(grid_kernel, [VMEM] * 7, shape(NF * NB, 2 * RD, M), [buf(2 * SG, NV)...  1.92 us
  transfers between devices with their start and end apart: 5, of which 2 were waited for; matrix products, arithmetic and copies ran while one was open for 0% of the time, Pallas kernels for 6%

profile of v7, /device:TPU:1, one launch (start us, length us, event | category | flops | bytes accessed | tf_op | source)
XLA Modules:
  0.0 55.9 jit_solution(16265685761222778981)
XLA Ops:
  0.0 0.0 copy-start.1
  0.0 0.0 copy-start.2
  0.0 0.0 copy-start.5
  0.0 0.0 copy-start.4
  0.0 0.0 copy-start.3
  0.0 0.0 copy-start
  0.0 0.7 %copy-done.5 = s32[1,2,1,2,256]{4,3,2,1,0:T(2,128)S(1)} copy-done((s32[1,2,1,2,256]{4,3,2,1,0:T(2,128)S(1)}, s32[1,2,1,2,256]{4,3,2,1,0:T(2,128)}, u32[]{:S(2)}) %copy-start.5) | copy-done | bytes 4120
  0.7 5.2 %collective-permute-start.2 = (s32[1,2,1,2,256]{4,3,1,2,0:T(2,128)S(1)}, s32[1,2,1,2,256]{4,3,1,2,0:T(2,128)S(1)}, u32[]{:S(2)}, u32[]{:S(2)}) collective-permute-start(s32[1,2,1,2,256]{4,3,1,2,0:T(2,128)S(1)} %bitcast.12), channel_id=1, source_target_pairs={{0,6},{2,4},{4,2},{6,0},{8,14},{10,12},{12,10},{14,8},{1,7},{3,5},... | collective-permute-start | bytes 12296 | tf_op jit(solution)/shard_map/ppermute | solution.py:469
  5.9 0.0 collective-permute-start.1
  5.9 0.3 collective-permute-start
  6.2 0.0 copy-done.1
  6.2 0.0 copy-done.2
  6.2 0.0 copy-done.4
  6.2 0.0 copy-done.3
  6.2 0.0 copy-done
  6.2 1.2 %windows.1 = (bf16[16,16,128]{2,1,0:T(8,128)(2,1)}, s32[2,32]{1,0:T(2,128)S(1)}, s32[2,16]{1,0:T(2,128)S(1)}) custom-call(f32[8,128]{1,0:T(8,128)S(1)} %lead.1, s32[2,32]{1,0:T(2,128)S(1)} %bitcast.10, s32[2,16]{1,0:T(2,128)S(1)} %bitcast.11, bf16[1,2,8,4096]{3,2,1,0:T(8,128)(2,1)S(1)} %copy-done, bf16[256,64]{1,0:T(8,128)(2,1)S(1)} %copy-done.2, ...), custom_call_target="tpu_custom_call" | custom-call | tf_op jit(solution)/shard_map/windows/pallas_call | solution.py:489
  7.4 0.0 collective-permute-done.2
  7.4 1.8 %collective-permute-done.1 = s32[1,2,1,2,256]{4,3,1,2,0:T(2,128)S(1)} collective-permute-done((s32[1,2,1,2,256]{4,3,1,2,0:T(2,128)S(1)}, s32[1,2,1,2,256]{4,3,1,2,0:T(2,128)S(1)}, u32[]{:S(2)}, u32[]{:S(2)}) %collective-permute-start.1) | collective-permute-done | bytes 4128 | tf_op jit(solution)/shard_map/ppermute | solution.py:469
  9.3 0.0 collective-permute-done
  9.3 3.9 %collective-permute-start.3 = (s32[4,2,2,256]{3,2,1,0:T(2,128)S(1)}, s32[4,2,2,256]{3,2,1,0:T(2,128)S(1)}, u32[]{:S(2)}, u32[]{:S(2)}) collective-permute-start(s32[4,2,2,256]{3,2,1,0:T(2,128)S(1)} %pad_add_fusion.near_h), channel_id=1, source_target_pairs={{0,12},{2,14},{4,8},{6,10},{8,4},{10,6},{12,0},{14,2},{1,13},{3,15... | collective-permute-start | bytes 49160 | tf_op jit(solution)/shard_map/ppermute | solution.py:469
  13.2 7.8 %all-to-all-start = ((bf16[16,16,128]{2,1,0:T(8,128)(2,1)}), bf16[16,16,128]{2,1,0:T(8,128)(2,1)S(1)}, u32[]{:S(2)}, u32[]{:S(2)}) async-start(bf16[16,16,128]{2,1,0:T(8,128)(2,1)} %get-tuple-element.28), calls=%async_computation | async-start | bytes 131072 | tf_op jit(solution)/shard_map/all_to_all | solution.py:508
  20.9 0.0 collective-permute-done.3.far_h
  20.9 2.3 %setup.1 = (bf16[512,2048]{1,0:T(8,128)(2,1)S(1)}, f32[24,2048]{1,0:T(8,128)S(1)}, bf16[512,256]{1,0:T(8,128)(2,1)S(1)}, bf16[256,512]{1,0:T(8,128)(2,1)S(1)}, b...) custom-call(s32[2,32]{1,0:T(2,128)S(1)} %get-tuple-element.29.offs_v, ...), custom_call_target="tpu_custom_call" | custom-call | flops 20000000000 | bytes 4194304 | tf_op jit(solution)/shard_map/setup/pallas_call | solution.py:509
  23.2 3.5 %all-to-all-done.spec = bf16[16,16,128]{2,1,0:T(8,128)(2,1)S(1)} async-done(((bf16[16,16,128]{2,1,0:T(8,128)(2,1)}), bf16[16,16,128]{2,1,0:T(8,128)(2,1)S(1)}, u32[]{:S(2)}, u32[]{:S(2)}) %all-to-all-start) | async-done | bytes 65568 | tf_op jit(solution)/shard_map/all_to_all | solution.py:508
  26.8 2.0 %predict.1 = bf16[8,40,128]{2,1,0:T(8,128)(2,1)S(1)} custom-call(bf16[16,16,128]{2,1,0:T(8,128)(2,1)S(1)} %all-to-all-done.spec, bf16[512,256]{1,0:T(8,128)(2,1)S(1)} %get-tuple-element.34.lift, bf16[256,512]{1,0:T(8,128)(2,1)S(1)} %get-tuple-element.35.k_right, bf16[256,256]{1,0:T(8,128)(2,1)S(1)} %get-tuple-element.36.aterm, ...), custom_call_target="tpu_custom_call" | custom-call | tf_op jit(solution)/shard_map/predict/pallas_call | solution.py:542
  28.8 10.0 %all_to_all.15.parts = bf16[8,40,128]{2,1,0:T(8,128)(2,1)S(1)} all-to-all(bf16[8,40,128]{2,1,0:T(8,128)(2,1)S(1)} %predict.1), channel_id=1, replica_groups=mesh['facet'=16,'team'=8,'sub'=2] {'team'}, dimensions={0} | all-to-all | bytes 163840 | tf_op jit(solution)/shard_map/all_to_all | solution.py:549
  38.8 1.9 %grid.1 = bf16[32,16,128]{2,1,0:T(8,128)(2,1)S(1)} custom-call(bf16[8,40,128]{2,1,0:T(8,128)(2,1)S(1)} %all_to_all.15.parts, bf16[512,2048]{1,0:T(8,128)(2,1)S(1)} %get-tuple-element.37.col_t, f32[24,2048]{1,0:T(8,128)S(1)} %get-tuple-element.38.row_fac, bf16[256,256]{1,0:T(8,128)(2,1)S(1)} %get-tuple-element.36.aterm, ...), custom_call_target="tpu_custom_call" | custom-call | tf_op jit(solution)/shard_map/grid/pallas_call | solution.py:550
  40.7 14.0 %all_to_all.16.folded = bf16[32,16,128]{2,1,0:T(8,128)(2,1)S(1)} all-to-all(bf16[32,16,128]{2,1,0:T(8,128)(2,1)S(1)} %grid.1), channel_id=1, replica_groups=mesh['facet'=16,'team'=8,'sub'=2] {'facet','sub'}, dimensions={0} | all-to-all | bytes 262144 | tf_op jit(solution)/shard_map/all_to_all | solution.py:561
  54.7 1.2 %update.1 = f32[2,8,2048]{2,1,0:T(8,128)} custom-call(bf16[32,16,128]{2,1,0:T(8,128)(2,1)S(1)} %all_to_all.16.folded, bf16[256,128]{1,0:T(8,128)(2,1)S(1)} %get-tuple-element.41.w_rows, f32[32,128]{1,0:T(8,128)S(1)} %get-tuple-element.42.picks, f32[2,128,128]{2,1,0:T(8,128)S(1)} %get-tuple-element.43.turn, bf16[32,256]{1,0:T(8,128)(2,1)S(1)} %get-tuple-element.44.w_high), custom_call_target="tpu_custom_call" | custom-call | tf_op jit(solution)/shard_map/update/pallas_call | solution.py:562
  (2 shorter events, 0.0 us)
Async XLA Ops:
  0.0 6.2 %copy-start.1 = (f32[2,128,128]{2,1,0:T(8,128)S(1)}, f32[2,128,128]{2,1,0:T(8,128)}, u32[]{:S(2)}) copy-start(f32[2,128,128]{2,1,0:T(8,128)} %constant.11.clone.turn) | copy-start | bytes 393220
  0.0 6.2 %copy-start.2 = (bf16[256,64]{1,0:T(8,128)(2,1)S(1)}, bf16[256,64]{1,0:T(8,128)(2,1)}, u32[]{:S(2)}) copy-start(bf16[256,64]{1,0:T(8,128)(2,1)} %constant.10.clone.w_rows) | copy-start | bytes 98308
  0.0 0.7 %copy-start.5 = (s32[1,2,1,2,256]{4,3,2,1,0:T(2,128)S(1)}, s32[1,2,1,2,256]{4,3,2,1,0:T(2,128)}, u32[]{:S(2)}) copy-start(s32[1,2,1,2,256]{4,3,2,1,0:T(2,128)} %param.17) | copy-start | bytes 12292
  0.0 6.2 %copy-start.4 = (s32[16,2]{0,1:T(2,128)S(1)}, s32[16,2]{0,1:T(2,128)}, u32[]{:S(2)}) copy-start(s32[16,2]{0,1:T(2,128)} %param.15) | copy-start | bytes 388
  0.0 6.2 %copy-start.3 = (s32[32,2]{0,1:T(2,128)S(1)}, s32[32,2]{0,1:T(2,128)}, u32[]{:S(2)}) copy-start(s32[32,2]{0,1:T(2,128)} %param.14) | copy-start | bytes 772
  0.0 6.2 %copy-start = (bf16[1,2,8,4096]{3,2,1,0:T(8,128)(2,1)S(1)}, bf16[1,2,8,4096]{3,2,1,0:T(8,128)(2,1)}, u32[]{:S(2)}) copy-start(bf16[1,2,8,4096]{3,2,1,0:T(8,128)(2,1)} %rows.1) | copy-start | bytes 393220
  0.7 6.7 %collective-permute-start.2 = (s32[1,2,1,2,256]{4,3,1,2,0:T(2,128)S(1)}, s32[1,2,1,2,256]{4,3,1,2,0:T(2,128)S(1)}, u32[]{:S(2)}, u32[]{:S(2)}) collective-permute-start(s32[1,2,1,2,256]{4,3,1,2,0:T(2,128)S(1)} %bitcast.12), channel_id=1, source_target_pairs={{0,6},{2,4},{4,2},{6,0},{8,14},{10,12},{12,10},{14,8},{1,7},{3,5},... | collective-permute-start | bytes 12296 | tf_op jit(solution)/shard_map/ppermute | solution.py:469
  5.9 3.4 %collective-permute-start.1 = (s32[1,2,1,2,256]{4,3,1,2,0:T(2,128)S(1)}, s32[1,2,1,2,256]{4,3,1,2,0:T(2,128)S(1)}, u32[]{:S(2)}, u32[]{:S(2)}) collective-permute-start(s32[1,2,1,2,256]{4,3,1,2,0:T(2,128)S(1)} %bitcast.13), channel_id=1, source_target_pairs={{0,4},{2,6},{4,0},{6,2},{8,12},{10,14},{12,8},{14,10},{1,5},{3,7},... | collective-permute-start | bytes 12296 | tf_op jit(solution)/shard_map/ppermute | solution.py:469
  5.9 3.4 %collective-permute-start = (s32[1,2,1,2,256]{4,3,1,2,0:T(2,128)S(1)}, s32[1,2,1,2,256]{4,3,1,2,0:T(2,128)S(1)}, u32[]{:S(2)}, u32[]{:S(2)}) collective-permute-start(s32[1,2,1,2,256]{4,3,1,2,0:T(2,128)S(1)} %bitcast.14), channel_id=1, source_target_pairs={{0,2},{2,0},{4,6},{6,4},{8,10},{10,8},{12,14},{14,12},{1,3},{3,1},... | collective-permute-start | bytes 12296 | tf_op jit(solution)/shard_map/ppermute | solution.py:469
  9.3 11.7 %collective-permute-start.3 = (s32[4,2,2,256]{3,2,1,0:T(2,128)S(1)}, s32[4,2,2,256]{3,2,1,0:T(2,128)S(1)}, u32[]{:S(2)}, u32[]{:S(2)}) collective-permute-start(s32[4,2,2,256]{3,2,1,0:T(2,128)S(1)} %pad_add_fusion.near_h), channel_id=1, source_target_pairs={{0,12},{2,14},{4,8},{6,10},{8,4},{10,6},{12,0},{14,2},{1,13},{3,15... | collective-permute-start | bytes 49160 | tf_op jit(solution)/shard_map/ppermute | solution.py:469
  13.2 13.6 %all-to-all-start = ((bf16[16,16,128]{2,1,0:T(8,128)(2,1)}), bf16[16,16,128]{2,1,0:T(8,128)(2,1)S(1)}, u32[]{:S(2)}, u32[]{:S(2)}) async-start(bf16[16,16,128]{2,1,0:T(8,128)(2,1)} %get-tuple-element.28), calls=%async_computation | async-start | bytes 131072 | tf_op jit(solution)/shard_map/all_to_all | solution.py:508
